TPU v7x, 32 devices: a whole 2x2x4 slice. The times are simulated.
32 devices in a mesh: seq: 4 (over x, core), dp: 8 (over z, y).
Axes of the slice: x: 2, y: 2, z: 4, core: 2. Of those that a mesh axis runs over, the one named last changes fastest.
Arguments:
- x_in: bfloat16 [8, 1536, 1024], P('dp', 'seq'), may hold values from -6 to 6
- cu_seqlens: int32 [8, 4], P('dp'), may hold values from 0 to 1536, as said below
- positions: int32 [8, 1536], P('dp', 'seq'), may hold values from 0 to 1535, as said below
- cotangent: bfloat16 [8, 1536, 1024], P('dp', 'seq'), may hold values from -6 to 6
- w_in: bfloat16 [1024, 3072], P('dp'), may hold values from -0.1875 to 0.1875
- conv_w: bfloat16 [3, 1024], P(None, 'dp'), may hold values from -3 to 3
- w_out: bfloat16 [1024, 1024], P('dp'), may hold values from -0.1875 to 0.1875
- w_gate1: bfloat16 [1024, 4608], P('dp'), may hold values from -0.1875 to 0.1875
- w_up1: bfloat16 [1024, 4608], P('dp'), may hold values from -0.1875 to 0.1875
- w_down1: bfloat16 [1024, 4608], P('dp'), may hold values from -0.09375 to 0.09375
- g_mix1: bfloat16 [1024], P('dp'), may hold values from 0.25 to 1.75
- g_ffn1: bfloat16 [1024], P('dp'), may hold values from 0.25 to 1.75
- w_q: bfloat16 [1024, 1024], P('dp'), may hold values from -0.1875 to 0.1875
- key_projection_weight: bfloat16 [1024, 512], P('dp'), may hold values from -0.1875 to 0.1875
- value_projection_weight: bfloat16 [1024, 512], P('dp'), may hold values from -0.1875 to 0.1875
- w_o: bfloat16 [1024, 1024], P('dp'), may hold values from -0.75 to 0.75
- g_q: bfloat16 [64], P('dp'), may hold values from 0.25 to 1.75
- g_k: bfloat16 [64], P('dp'), may hold values from 0.25 to 1.75
- w_gate2: bfloat16 [1024, 4608], P('dp'), may hold values from -0.1875 to 0.1875
- w_up2: bfloat16 [1024, 4608], P('dp'), may hold values from -0.1875 to 0.1875
- w_down2: bfloat16 [1024, 4608], P('dp'), may hold values from -0.09375 to 0.09375
- g_attn2: bfloat16 [1024], P('dp'), may hold values from 0.25 to 1.75
- g_ffn2: bfloat16 [1024], P('dp'), may hold values from 0.25 to 1.75
Outputs:
- out: bfloat16 [8, 1536, 1024], P('dp', 'seq')
- d_x: float32 [8, 1536, 1024], P('dp', 'seq')
- d_w_in: float32 [1024, 3072], P('dp')
- d_conv_w: float32 [3, 1024], P(None, 'dp')
- d_w_out: float32 [1024, 1024], P('dp')
- d_w_gate1: float32 [1024, 4608], P('dp')
- d_w_up1: float32 [1024, 4608], P('dp')
- d_w_down1: float32 [1024, 4608], P('dp')
- d_g_mix1: float32 [1024], P('dp')
- d_g_ffn1: float32 [1024], P('dp')
- d_w_q: float32 [1024, 1024], P('dp')
- d_w_k: float32 [1024, 512], P('dp')
- d_w_v: float32 [1024, 512], P('dp')
- d_w_o: float32 [1024, 1024], P('dp')
- d_g_q: float32 [64], P('dp')
- d_g_k: float32 [64], P('dp')
- d_w_gate2: float32 [1024, 4608], P('dp')
- d_w_up2: float32 [1024, 4608], P('dp')
- d_w_down2: float32 [1024, 4608], P('dp')
- d_g_attn2: float32 [1024], P('dp')
- d_g_ffn2: float32 [1024], P('dp')
Inputs may be any that keep to these rules, and one draw needn't show every extreme that they name: Row r holds n documents, 1 <= n <= 3; document j is tokens cu_seqlens[r, j] to cu_seqlens[r, j + 1] - 1 for j < n; cu_seqlens[r, 0] is 0, cu_seqlens[r, n] is 1536, later entries are 0; each document has 512 tokens or more. Some row holds 3 documents and some row one. positions[r, t] is t minus the first token of t's document.
All inputs are finite; a program needn't handle non-finite values.
Results may differ from a plain program's by a relative error of at most 0.03.
Values may be sent and summed in bfloat16 or wider, within the bound.
No kernel may reach another device: no remote copies, remote signals or barrier semaphores. Data moves between devices by JAX's collectives and lax.ppermute only.
A program may use at most 640 MiB of HBM per device.

v0:
```python
import jax
import jax.numpy as jnp
from jax import lax
from jax.sharding import PartitionSpec as P

QBLK = 512


EPS = 1e-05
THETA = 1000000.0
NEG = -1e30


def passed_along(array, axis, by):
    length = lax.axis_size(axis)
    pairs = [(i, i + by) for i in range(length) if 0 <= i + by < length]
    return lax.ppermute(array, axis, pairs)


def left_dot(left, right):
    return lax.dot_general(
        left, right, (((0,), (0,)), ((), ())), preferred_element_type=jnp.float32
    )


def right_dot(left, right):
    return lax.dot_general(
        left, right, (((1,), (1,)), ((), ())), preferred_element_type=jnp.float32
    )


def plain_dot(left, right):
    return jnp.dot(left, right, preferred_element_type=jnp.float32)


def unit_scale(value):
    scale = lax.rsqrt(jnp.mean(value * value, -1, keepdims=True) + EPS)
    return (value * scale, scale)


def norm_back(grad_out, gain, unit, scale):
    weighted = grad_out * gain
    grad_in = scale * (weighted - unit * jnp.mean(weighted * unit, -1, keepdims=True))
    gain_grad = jnp.sum((grad_out * unit).reshape(-1, unit.shape[-1]), 0)
    return (grad_in, gain_grad)


def doc_index(bounds, places):
    later = bounds[:, None, 1:]
    passed = (later <= places[:, :, None]) & (later > 0)
    return jnp.sum(passed.astype(jnp.int32), -1)


def rope_tables(places, head):
    half = head // 2
    freqs = THETA ** (-(2.0 * jnp.arange(half, dtype=jnp.float32)) / head)
    angles = places.astype(jnp.float32)[..., None] * freqs
    angles = jnp.concatenate([angles, angles], -1)
    return (jnp.cos(angles), jnp.sin(angles))


def rotate_half(value):
    half = value.shape[-1] // 2
    return jnp.concatenate([-value[..., half:], value[..., :half]], -1)


def rotate_back(grad):
    half = grad.shape[-1] // 2
    return jnp.concatenate([grad[..., half:], -grad[..., :half]], -1)


def ffn_forward(hidden, gain, w_gate, w_up, w_down):
    unit, scale = unit_scale(hidden)
    normed = (unit * gain).astype(jnp.bfloat16)
    gate = plain_dot(normed, w_gate)
    upper = plain_dot(normed, w_up)
    act = (gate * jax.nn.sigmoid(gate) * upper).astype(jnp.bfloat16)
    return (right_dot(act, w_down), (unit, scale, normed, gate, upper))


def ffn_back(grad, kept, gain, w_gate, w_up, w_down):
    unit, scale, normed, gate, upper = kept
    grad_low = grad.astype(jnp.bfloat16)
    sigma = jax.nn.sigmoid(gate)
    act = (gate * sigma * upper).astype(jnp.bfloat16)
    d_down = left_dot(grad_low, act)
    d_act = plain_dot(grad_low, w_down)
    d_gate = (d_act * upper * sigma * (1.0 + gate * (1.0 - sigma))).astype(jnp.bfloat16)
    d_up = (d_act * gate * sigma).astype(jnp.bfloat16)
    d_wgate = left_dot(normed, d_gate)
    d_wup = left_dot(normed, d_up)
    d_normed = right_dot(d_gate, w_gate) + right_dot(d_up, w_up)
    d_hidden, d_gain = norm_back(d_normed, gain, unit, scale)
    return (d_hidden, d_gain, d_wgate, d_wup, d_down)


def block_scores(query_block, keys, doc_rows, doc_cols, start):
    size, end = (query_block.shape[1], keys.shape[1])
    scores = jnp.einsum("rqkgd,rtkd->rkgqt", query_block, keys, preferred_element_type=jnp.float32)
    scores = scores * query_block.shape[-1] ** (-0.5)
    later = start + lax.broadcasted_iota(jnp.int32, (size, end), 0)
    earlier = lax.broadcasted_iota(jnp.int32, (size, end), 1)
    allowed = (doc_rows[:, :, None] == doc_cols[:, None, :]) & (earlier <= later)[None]
    return jnp.where(allowed[:, None, None], scores, NEG)


def attention_forward(queries, keys, values, docs):
    full = queries.shape[1]
    outputs = []
    totals = []
    for start in range(0, full, QBLK):
        end = start + QBLK
        scores = block_scores(
            queries[:, start:end], keys[:, :end], docs[:, start:end], docs[:, :end], start
        )
        top = jnp.max(scores, -1, keepdims=True)
        log_total = top + jnp.log(jnp.sum(jnp.exp(scores - top), -1, keepdims=True))
        weights = jnp.exp(scores - log_total).astype(jnp.bfloat16)
        outputs.append(
            jnp.einsum(
                "rkgqt,rtkd->rqkgd", weights, values[:, :end], preferred_element_type=jnp.float32
            )
        )
        totals.append(log_total)
    return (jnp.concatenate(outputs, 1), totals)


def attention_backward(queries, keys, values, docs, totals, grads):
    full = queries.shape[1]
    scale = queries.shape[-1] ** (-0.5)
    grad_keys = jnp.zeros(keys.shape, jnp.float32)
    grad_values = jnp.zeros(values.shape, jnp.float32)
    grad_queries = []
    for number, start in enumerate(range(0, full, QBLK)):
        end = start + QBLK
        query_block = queries[:, start:end]
        grad_block = grads[:, start:end]
        scores = block_scores(query_block, keys[:, :end], docs[:, start:end], docs[:, :end], start)
        probs = jnp.exp(scores - totals[number])
        padding = ((0, 0), (0, full - end), (0, 0), (0, 0))
        grad_values = grad_values + jnp.pad(
            jnp.einsum(
                "rkgqt,rqkgd->rtkd",
                probs.astype(jnp.bfloat16),
                grad_block,
                preferred_element_type=jnp.float32,
            ),
            padding,
        )
        grad_probs = jnp.einsum(
            "rqkgd,rtkd->rkgqt", grad_block, values[:, :end], preferred_element_type=jnp.float32
        )
        inner = jnp.sum(probs * grad_probs, -1, keepdims=True)
        grad_scores = (probs * (grad_probs - inner)).astype(jnp.bfloat16)
        grad_queries.append(
            jnp.einsum(
                "rkgqt,rtkd->rqkgd", grad_scores, keys[:, :end], preferred_element_type=jnp.float32
            )
            * scale
        )
        grad_keys = grad_keys + jnp.pad(
            jnp.einsum(
                "rkgqt,rqkgd->rtkd", grad_scores, query_block, preferred_element_type=jnp.float32
            )
            * scale,
            padding,
        )
    return (jnp.concatenate(grad_queries, 1), grad_keys, grad_values)


def pack_grads(row_items, col_items, dp_count, seq_count):
    pieces = [item.reshape(dp_count, -1) for item in row_items]
    for item in col_items:
        pieces.append(
            jnp.swapaxes(item.reshape(item.shape[0], dp_count, -1), 0, 1).reshape(dp_count, -1)
        )
    packed = jnp.concatenate(pieces, 1)
    extra = -packed.shape[1] % seq_count
    return jnp.pad(packed, ((0, 0), (0, extra)))


def unpack_grads(owned, row_items, col_items, dp_count):
    results = []
    offset = 0
    for item in row_items:
        size = item.size // dp_count
        results.append(
            owned[offset : offset + size].reshape(item.shape[0] // dp_count, item.shape[1])
        )
        offset = offset + size
    for item in col_items:
        size = item.size // dp_count
        results.append(
            owned[offset : offset + size].reshape(item.shape[0], item.shape[1] // dp_count)
        )
        offset = offset + size
    return results


def reduce_grads(packed):
    owned = lax.psum_scatter(packed.astype(jnp.bfloat16), "dp", scatter_dimension=0, tiled=True)
    return lax.psum(owned, "seq").astype(jnp.float32).reshape(-1)


def sum_block(row_items, col_items):
    dp_count = lax.axis_size("dp")
    seq_count = lax.axis_size("seq")
    packed = pack_grads(row_items, col_items, dp_count, seq_count)
    owned = reduce_grads(packed)
    return unpack_grads(owned, row_items, col_items, dp_count)


def local(
    x_in,
    cu_seqlens,
    positions,
    cotangent,
    w_in,
    conv_w,
    w_out,
    w_gate1,
    w_up1,
    w_down1,
    g_mix1,
    g_ffn1,
    w_q,
    key_projection_weight,
    value_projection_weight,
    w_o,
    g_q,
    g_k,
    w_gate2,
    w_up2,
    w_down2,
    g_attn2,
    g_ffn2,
):
    rows, length, width = x_in.shape
    seq_count = lax.axis_size("seq")
    seq_place = lax.axis_index("seq")
    tokens = rows * length
    full = length * seq_count
    mix_full = (
        lax.all_gather(w_in, "dp", axis=0, tiled=True),
        lax.all_gather(conv_w, "dp", axis=1, tiled=True),
        lax.all_gather(w_out, "dp", axis=0, tiled=True),
        lax.all_gather(w_gate1, "dp", axis=0, tiled=True),
        lax.all_gather(w_up1, "dp", axis=0, tiled=True),
        lax.all_gather(w_down1, "dp", axis=0, tiled=True),
        lax.all_gather(g_mix1, "dp", axis=0, tiled=True),
        lax.all_gather(g_ffn1, "dp", axis=0, tiled=True),
    )
    in_full, kernel_low, out_full, gate_one, up_one, down_one, gain_mix_low, gain_ffn_one_low = (
        mix_full
    )
    kernel = kernel_low.astype(jnp.float32)
    gain_mix = gain_mix_low.astype(jnp.float32)
    gain_ffn_one = gain_ffn_one_low.astype(jnp.float32)
    reach = kernel.shape[0] - 1
    places = seq_place * length + jnp.arange(length, dtype=jnp.int32)[None, :]
    docs_here = doc_index(cu_seqlens, places)
    masks = []
    for tap in range(1, reach + 1):
        before = doc_index(cu_seqlens, places - tap)
        masks.append((before == docs_here).astype(jnp.float32)[..., None])
    x_flat = x_in.reshape(tokens, width).astype(jnp.float32)
    unit_one, scale_one = unit_scale(x_flat)
    normed_one = (unit_one * gain_mix).astype(jnp.bfloat16)
    projected = plain_dot(normed_one, in_full).reshape(rows, length, 3 * width)
    part_b = projected[..., :width]
    part_c = projected[..., width : 2 * width]
    part_x = projected[..., 2 * width :]
    product_low = (part_b * part_x).astype(jnp.bfloat16)
    rim = passed_along(product_low[:, length - reach :], "seq", 1)
    extended = jnp.concatenate([rim, product_low], 1).astype(jnp.float32)
    conv_out = kernel[0] * extended[:, reach:]
    for tap in range(1, reach + 1):
        conv_out = (
            conv_out
            + kernel[tap] * extended[:, reach - tap : reach - tap + length] * masks[tap - 1]
        )
    gated = (part_c * conv_out).astype(jnp.bfloat16).reshape(tokens, width)
    hidden_one = x_flat + plain_dot(gated, out_full)
    ffn_out, keep_one = ffn_forward(hidden_one, gain_ffn_one, gate_one, up_one, down_one)
    hidden_two = hidden_one + ffn_out
    attn_full = (
        lax.all_gather(w_q, "dp", axis=0, tiled=True),
        lax.all_gather(key_projection_weight, "dp", axis=0, tiled=True),
        lax.all_gather(value_projection_weight, "dp", axis=0, tiled=True),
        lax.all_gather(w_o, "dp", axis=0, tiled=True),
        lax.all_gather(g_q, "dp", axis=0, tiled=True),
        lax.all_gather(g_k, "dp", axis=0, tiled=True),
        lax.all_gather(w_gate2, "dp", axis=0, tiled=True),
        lax.all_gather(w_up2, "dp", axis=0, tiled=True),
        lax.all_gather(w_down2, "dp", axis=0, tiled=True),
        lax.all_gather(g_attn2, "dp", axis=0, tiled=True),
        lax.all_gather(g_ffn2, "dp", axis=0, tiled=True),
    )
    (
        q_full,
        k_full,
        v_full,
        output_wide_rows,
        gain_q_low,
        gain_k_low,
        gate_two,
        up_two,
        down_two,
        gain_attn_low,
        gain_ffn_two_low,
    ) = attn_full
    gain_q = gain_q_low.astype(jnp.float32)
    gain_k = gain_k_low.astype(jnp.float32)
    gain_attn = gain_attn_low.astype(jnp.float32)
    gain_ffn_two = gain_ffn_two_low.astype(jnp.float32)
    head = gain_q.shape[0]
    unit_three, scale_three = unit_scale(hidden_two)
    normed_three = (unit_three * gain_attn).astype(jnp.bfloat16)
    query_raw = plain_dot(normed_three, q_full).reshape(rows, length, -1, head)
    key_raw = plain_dot(normed_three, k_full).reshape(rows, length, -1, head)
    value_low = plain_dot(normed_three, v_full).astype(jnp.bfloat16).reshape(rows, length, -1)
    cosine, sine = rope_tables(positions, head)
    cosine = cosine[:, :, None, :]
    sine = sine[:, :, None, :]
    unit_q, query_scale_factor = unit_scale(query_raw)
    unit_k, scale_k = unit_scale(key_raw)
    rotated_q = unit_q * gain_q
    rotated_k = unit_k * gain_k
    query_low = (
        (rotated_q * cosine + rotate_half(rotated_q) * sine)
        .astype(jnp.bfloat16)
        .reshape(rows, length, -1)
    )
    key_low = (
        (rotated_k * cosine + rotate_half(rotated_k) * sine)
        .astype(jnp.bfloat16)
        .reshape(rows, length, -1)
    )
    heads_q, heads_k, heads_v = (
        lax.all_to_all(query_low, "seq", split_axis=2, concat_axis=1, tiled=True),
        lax.all_to_all(key_low, "seq", split_axis=2, concat_axis=1, tiled=True),
        lax.all_to_all(value_low, "seq", split_axis=2, concat_axis=1, tiled=True),
    )
    kv_local = heads_k.shape[2] // head
    group = heads_q.shape[2] // (kv_local * head)
    queries = heads_q.reshape(rows, full, kv_local, group, head)
    keys = heads_k.reshape(rows, full, kv_local, head)
    values = heads_v.reshape(rows, full, kv_local, head)
    full_places = jnp.arange(full, dtype=jnp.int32)[None, :]
    docs_full = doc_index(cu_seqlens, full_places)
    attended, totals = attention_forward(queries, keys, values, docs_full)
    attended_low = attended.astype(jnp.bfloat16).reshape(rows, full, -1)
    attended_tokens = lax.all_to_all(
        attended_low, "seq", split_axis=1, concat_axis=2, tiled=True
    ).reshape(tokens, -1)
    hidden_three = hidden_two + plain_dot(attended_tokens, output_wide_rows)
    ffn_out_two, keep_two = ffn_forward(hidden_three, gain_ffn_two, gate_two, up_two, down_two)
    hidden_four = hidden_three + ffn_out_two
    out = hidden_four.astype(jnp.bfloat16).reshape(rows, length, width)
    grad_four = cotangent.reshape(tokens, width).astype(jnp.float32)
    d_hidden, d_gain_ffn_two, d_wgate_two, d_wup_two, d_down_two = ffn_back(
        grad_four, keep_two, gain_ffn_two, gate_two, up_two, down_two
    )
    grad_three = grad_four + d_hidden
    grad_attn = grad_three.astype(jnp.bfloat16)
    d_w_o = left_dot(attended_tokens, grad_attn)
    d_attended = (
        right_dot(grad_attn, output_wide_rows).astype(jnp.bfloat16).reshape(rows, length, -1)
    )
    grad_heads = lax.all_to_all(d_attended, "seq", split_axis=2, concat_axis=1, tiled=True)
    grad_heads = grad_heads.reshape(rows, full, kv_local, group, head)
    d_queries, d_keys, d_values = attention_backward(
        queries, keys, values, docs_full, totals, grad_heads
    )
    d_queries_low = d_queries.astype(jnp.bfloat16).reshape(rows, full, -1)
    key_rows_gradient_narrow = d_keys.astype(jnp.bfloat16).reshape(rows, full, -1)
    d_values_low = d_values.astype(jnp.bfloat16).reshape(rows, full, -1)
    back_q, back_k, back_v = (
        lax.all_to_all(d_queries_low, "seq", split_axis=1, concat_axis=2, tiled=True),
        lax.all_to_all(key_rows_gradient_narrow, "seq", split_axis=1, concat_axis=2, tiled=True),
        lax.all_to_all(d_values_low, "seq", split_axis=1, concat_axis=2, tiled=True),
    )
    turned_q = back_q.astype(jnp.float32).reshape(rows, length, -1, head)
    turned_k = back_k.astype(jnp.float32).reshape(rows, length, -1, head)
    d_rot_q = turned_q * cosine + rotate_back(turned_q * sine)
    d_rot_k = turned_k * cosine + rotate_back(turned_k * sine)
    d_query_raw, d_gain_q = norm_back(d_rot_q, gain_q, unit_q, query_scale_factor)
    d_key_raw, d_gain_k = norm_back(d_rot_k, gain_k, unit_k, scale_k)
    d_query_low = d_query_raw.astype(jnp.bfloat16).reshape(tokens, -1)
    d_key_low = d_key_raw.astype(jnp.bfloat16).reshape(tokens, -1)
    d_value_low = back_v.reshape(tokens, -1)
    d_w_q = left_dot(normed_three, d_query_low)
    d_w_k = left_dot(normed_three, d_key_low)
    d_w_v = left_dot(normed_three, d_value_low)
    d_attn_in = (
        right_dot(d_query_low, q_full)
        + right_dot(d_key_low, k_full)
        + right_dot(d_value_low, v_full)
    )
    d_attn_h, d_gain_attn = norm_back(d_attn_in, gain_attn, unit_three, scale_three)
    grad_two = grad_three + d_attn_h
    attn_total = sum_block(
        [d_w_q, d_w_k, d_w_v, d_w_o, d_wgate_two, d_wup_two, d_down_two],
        [jnp.stack([d_gain_attn, d_gain_ffn_two]), jnp.stack([d_gain_q, d_gain_k])],
    )
    d_hidden_one, d_gain_ffn_one, d_wgate_one, d_wup_one, d_down_one = ffn_back(
        grad_two, keep_one, gain_ffn_one, gate_one, up_one, down_one
    )
    grad_one = grad_two + d_hidden_one
    grad_mix = grad_one.astype(jnp.bfloat16)
    d_w_out = left_dot(gated, grad_mix)
    d_gated = right_dot(grad_mix, out_full).reshape(rows, length, width)
    d_part_c = d_gated * conv_out
    d_conv = d_gated * part_c
    grad_ext = jnp.pad(kernel[0] * d_conv, ((0, 0), (reach, 0), (0, 0)))
    kernel_grads = [jnp.sum((d_conv * extended[:, reach:]).reshape(-1, width), 0)]
    for tap in range(1, reach + 1):
        piece = extended[:, reach - tap : reach - tap + length]
        grad_ext = grad_ext + jnp.pad(
            kernel[tap] * masks[tap - 1] * d_conv, ((0, 0), (reach - tap, tap), (0, 0))
        )
        kernel_grads.append(jnp.sum((d_conv * piece * masks[tap - 1]).reshape(-1, width), 0))
    rim_grad = passed_along(grad_ext[:, :reach], "seq", -1)
    d_product_sum = grad_ext[:, reach:] + jnp.pad(rim_grad, ((0, 0), (length - reach, 0), (0, 0)))
    d_product = lax.optimization_barrier(d_product_sum.astype(jnp.bfloat16)).astype(jnp.float32)
    d_projected = jnp.concatenate([d_product * part_x, d_part_c, d_product * part_b], -1)
    d_projected = d_projected.astype(jnp.bfloat16).reshape(tokens, 3 * width)
    d_w_in = left_dot(normed_one, d_projected)
    d_normed = right_dot(d_projected, in_full)
    d_x_part, d_gain_mix = norm_back(d_normed, gain_mix, unit_one, scale_one)
    d_x = (grad_one + d_x_part).reshape(rows, length, width)
    small_mix = jnp.concatenate(
        [jnp.stack(kernel_grads), d_gain_mix[None], d_gain_ffn_one[None]], 0
    )
    mix_total = sum_block([d_w_in, d_w_out, d_wgate_one, d_wup_one, d_down_one], [small_mix])
    return (
        out,
        d_x,
        mix_total[0],
        mix_total[5][: reach + 1],
        mix_total[1],
        mix_total[2],
        mix_total[3],
        mix_total[4],
        mix_total[5][reach + 1],
        mix_total[5][reach + 2],
        attn_total[0],
        attn_total[1],
        attn_total[2],
        attn_total[3],
        attn_total[8][0],
        attn_total[8][1],
        attn_total[4],
        attn_total[5],
        attn_total[6],
        attn_total[7][0],
        attn_total[7][1],
    )


def solution(mesh):
    in_specs = (
        P("dp", "seq", None),
        P("dp", None),
        P("dp", "seq"),
        P("dp", "seq", None),
        P("dp", None),
        P(None, "dp"),
        P("dp", None),
        P("dp", None),
        P("dp", None),
        P("dp", None),
        P("dp"),
        P("dp"),
        P("dp", None),
        P("dp", None),
        P("dp", None),
        P("dp", None),
        P("dp"),
        P("dp"),
        P("dp", None),
        P("dp", None),
        P("dp", None),
        P("dp"),
        P("dp"),
    )
    out_specs = (
        P("dp", "seq", None),
        P("dp", "seq", None),
        P("dp", None),
        P(None, "dp"),
        P("dp", None),
        P("dp", None),
        P("dp", None),
        P("dp", None),
        P("dp"),
        P("dp"),
        P("dp", None),
        P("dp", None),
        P("dp", None),
        P("dp", None),
        P("dp"),
        P("dp"),
        P("dp", None),
        P("dp", None),
        P("dp", None),
        P("dp"),
        P("dp"),
    )
    return jax.shard_map(local, mesh=mesh, in_specs=in_specs, out_specs=out_specs, check_vma=False)
```

profile of v0, /device:TPU:0, one launch (start us, length us, event | category | flops | bytes accessed | tf_op | source)
XLA Modules:
  0.0 4211.3 jit_solution(11266925573531421584)
XLA Ops:
  16.6 22.5 all-gather
  39.1 16.4 all_gather.59
  57.2 54.8 %all-gather.17.cloned.1.call-done = bf16[1024,3072]{1,0:T(8,128)(2,1)} async-done(((bf16[128,3072]{1,0:T(8,128)(2,1)}), bf16[1024,3072]{1,0:T(8,128)(2,1)}) %all-gather.17.cloned.1.call-update) | async-done | bytes 6291472 | tf_op jit(solution)/shard_map/all_gather | solution.py:244
  123.4 19.4 all-reduce.12
  144.0 16.4 all-gather.1
  160.4 18.5 all-gather.2
  194.1 106.7 %all-gather.21.cloned.1.call-done = bf16[1024,4608]{1,0:T(8,128)(2,1)} async-done(((bf16[128,4608]{1,0:T(8,128)(2,1)}), bf16[1024,4608]{1,0:T(8,128)(2,1)}) %all-gather.21.cloned.1.call-update) | async-done | bytes 9437200 | tf_op jit(solution)/shard_map/all_gather | solution.py:247
  310.4 128.7 %all-gather.23.cloned.1.call-done = bf16[1024,4608]{1,0:T(8,128)(2,1)} async-done(((bf16[128,4608]{1,0:T(8,128)(2,1)}), bf16[1024,4608]{1,0:T(8,128)(2,1)}) %all-gather.23.cloned.1.call-update) | async-done | bytes 9437200 | tf_op jit(solution)/shard_map/all_gather | solution.py:248
  450.4 127.0 %all-gather.25.cloned.1.call-done = bf16[1024,4608]{1,0:T(8,128)(2,1)} async-done(((bf16[128,4608]{1,0:T(8,128)(2,1)}), bf16[1024,4608]{1,0:T(8,128)(2,1)}) %all-gather.25.cloned.1.call-update) | async-done | bytes 9437200 | tf_op jit(solution)/shard_map/all_gather | solution.py:249
  585.7 32.1 all-gather.27.cloned.1.call-done
  625.1 14.4 all-to-all-start
  639.5 19.4 all-gather.29.cloned.1.call-done
  675.9 33.2 all-gather.31.cloned.1.call-done
  816.1 18.4 all-gather.3
  856.0 41.8 all-gather.37.cloned.1.call-done
  907.3 129.0 %all-gather.35.cloned.1.call-done = bf16[1024,4608]{1,0:T(8,128)(2,1)} async-done(((bf16[128,4608]{1,0:T(8,128)(2,1)}), bf16[1024,4608]{1,0:T(8,128)(2,1)}) %all-gather.35.cloned.1.call-update) | async-done | bytes 9437200 | tf_op jit(solution)/shard_map/all_gather | solution.py:293
  1045.8 128.8 %all-gather.39.cloned.1.call-done = bf16[1024,4608]{1,0:T(8,128)(2,1)} async-done(((bf16[128,4608]{1,0:T(8,128)(2,1)}), bf16[1024,4608]{1,0:T(8,128)(2,1)}) %all-gather.39.cloned.1.call-update) | async-done | bytes 9437200 | tf_op jit(solution)/shard_map/all_gather | solution.py:295
  1655.3 2086.5 %all-reduce.18.cloned.1.call-done = (bf16[8,2294400]{1,0:T(8,128)(2,1)}, bf16[8,2162960]{1,0:T(8,128)(2,1)}) async-done(((bf16[8,2294400]{1,0:T(8,128)(2,1)}, bf16[8,2162960]{1,0:T(8,128)(2,1)}), (bf16[8,2294400]{1,0:T(8,128)(2,1)}, bf16[8,2162960]{1,0:T(8,128)(2,1)})) %all-reduce.18.cloned.1.call-update) | async-done | bytes 71317776
  3741.8 16.7 constant_dynamic-slice_fusion.1
  3758.4 15.7 constant_dynamic-slice_fusion
  3786.0 294.0 %all-reduce.20.cloned.1.call-done = (bf16[1,2294400]{1,0:T(2,128)(2,1)}, bf16[1,2162960]{1,0:T(2,128)(2,1)}) async-done(((bf16[1,2294400]{1,0:T(2,128)(2,1)}, bf16[1,2162960]{1,0:T(2,128)(2,1)}), (bf16[1,2294400]{1,0:T(2,128)(2,1)}, bf16[1,2162960]{1,0:T(2,128)(2,1)})) %all-reduce.20.cloned.1.call-update) | async-done | bytes 8914736 | tf_op jit(solution)/shard_map/psum | solution.py:202
  4093.6 17.4 slice_reduce_fusion.6
  4111.0 28.1 slice_reduce_fusion.3
  4154.4 28.5 slice_reduce_fusion
  (736 shorter events, 779.4 us)
Async XLA Ops:
  7.2 104.9 %all-gather.17.cloned.1.call-start = ((), (), s32[]{:S(2)}) async-start(), calls=%async_computation.8 | async-start | bytes 7077888 | tf_op jit(solution)/shard_map/all_gather | solution.py:244
  7.9 182.9 %all-gather.19.cloned.1.call-start = ((), (), s32[]{:S(2)}) async-start(), calls=%async_computation.9 | async-start | bytes 2359296 | tf_op jit(solution)/shard_map/all_gather | solution.py:246
  8.7 292.1 %all-gather.21.cloned.1.call-start = ((), (), s32[]{:S(2)}) async-start(), calls=%async_computation.10 | async-start | bytes 10616832 | tf_op jit(solution)/shard_map/all_gather | solution.py:247
  9.4 429.7 %all-gather.23.cloned.1.call-start = ((), (), s32[]{:S(2)}) async-start(), calls=%async_computation.11 | async-start | bytes 10616832 | tf_op jit(solution)/shard_map/all_gather | solution.py:248
  10.0 567.4 %all-gather.25.cloned.1.call-start = ((), (), s32[]{:S(2)}) async-start(), calls=%async_computation.12 | async-start | bytes 10616832 | tf_op jit(solution)/shard_map/all_gather | solution.py:249
  10.6 607.2 %all-gather.27.cloned.1.call-start = ((), (), s32[]{:S(2)}) async-start(), calls=%async_computation.13 | async-start | bytes 1179648 | tf_op jit(solution)/shard_map/all_gather | solution.py:289
  11.2 647.7 %all-gather.29.cloned.1.call-start = ((), (), s32[]{:S(2)}) async-start(), calls=%async_computation.14 | async-start | bytes 1179648 | tf_op jit(solution)/shard_map/all_gather | solution.py:288
  11.9 697.2 %all-gather.31.cloned.1.call-start = ((), (), s32[]{:S(2)}) async-start(), calls=%async_computation.15 | async-start | bytes 2359296 | tf_op jit(solution)/shard_map/all_gather | solution.py:287
  12.7 840.1 %all-gather.33.cloned.1.call-start = ((), (), s32[]{:S(2)}) async-start(), calls=%async_computation.16 | async-start | bytes 2359296 | tf_op jit(solution)/shard_map/all_gather | solution.py:290
  13.4 884.4 %all-gather.37.cloned.1.call-start = ((), (), s32[]{:S(2)}) async-start(), calls=%async_computation.18 | async-start | bytes 10616832 | tf_op jit(solution)/shard_map/all_gather | solution.py:294
  14.0 1022.2 %all-gather.35.cloned.1.call-start = ((), (), s32[]{:S(2)}) async-start(), calls=%async_computation.17 | async-start | bytes 10616832 | tf_op jit(solution)/shard_map/all_gather | solution.py:293
  14.8 1159.8 %all-gather.39.cloned.1.call-start = ((), (), s32[]{:S(2)}) async-start(), calls=%async_computation.19 | async-start | bytes 10616832 | tf_op jit(solution)/shard_map/all_gather | solution.py:295
  120.3 64.7 %collective-permute-start = (bf16[1,2,1024]{2,1,0:T(2,128)(2,1)S(1)}, bf16[1,2,1024]{2,1,0:T(2,128)(2,1)S(1)}, u32[]{:S(2)}, u32[]{:S(2)}) collective-permute-start(bf16[1,2,1024]{2,1,0:T(2,128)(2,1)S(1)} %slice.282), channel_id=1, source_target_pairs={{0,8},{8,16},{16,24},{1,9},{9,17},{17,25},{2,10},{10,18},{18,26},{... | collective-permute-start | bytes 12296 | tf_op jit(solution)/shard_map/ppermute | solution.py:17
  625.1 99.2 %all-to-all-start = ((bf16[4,2,24576]{2,1,0:T(2,128)(2,1)}), bf16[4,2,24576]{2,1,0:T(2,128)(2,1)}, u32[]{:S(2)}, u32[]{:S(2)}) async-start(bf16[4,2,24576]{2,1,0:T(2,128)(2,1)} %reshape.2150), calls=%async_computation | async-start | bytes 786432 | tf_op jit(solution)/shard_map/all_to_all | solution.py:342
  724.3 21.2 all-to-all-start.1
  745.5 16.3 all-to-all-start.2
  811.9 35.1 all-to-all-start.3
  1226.3 73.0 %all-to-all-start.4 = ((bf16[4,2,49152]{2,1,0:T(2,128)(2,1)}), bf16[4,2,49152]{2,1,0:T(2,128)(2,1)S(1)}, u32[]{:S(2)}, u32[]{:S(2)}) async-start(bf16[4,2,49152]{2,1,0:T(2,128)(2,1)} %reshape.2154), calls=%async_computation.4 | async-start | bytes 1572864 | tf_op jit(solution)/shard_map/all_to_all | solution.py:370
  1370.7 10.9 all-to-all-start.6
  1382.3 24.4 all-to-all-start.7
  1406.7 26.1 all-to-all-start.5
  1411.0 2330.8 %all-reduce.18.cloned.1.call-start = ((), (), s32[]{:S(2)}) async-start(), calls=%async_computation.20 | async-start | bytes 142639104
  1534.0 69.4 %collective-permute-start.1 = (f32[1,2,1024]{2,1,0:T(2,128)S(1)}, f32[1,2,1024]{2,1,0:T(2,128)S(1)}, u32[]{:S(2)}, u32[]{:S(2)}) collective-permute-start(f32[1,2,1024]{2,1,0:T(2,128)S(1)} %pad_add_fusion.1), channel_id=1, source_target_pairs={{8,0},{16,8},{24,16},{9,1},{17,9},{25,17},{10,2},{18,10},{26,18},{... | collective-permute-start | bytes 24584 | tf_op jit(solution)/shard_map/ppermute | solution.py:17
  1655.2 2424.7 %all-reduce.20.cloned.1.call-start = ((), (), s32[]{:S(2)}) async-start(), calls=%async_computation.21 | async-start | bytes 35659776 | tf_op jit(solution)/shard_map/psum | solution.py:202
  (184 other events, 5788.6 us)
Sparse Core Ops, SparseCore 0:
  10.2 101.8 all-gather.16
  114.2 47.7 all-gather.18
  164.2 136.5 all-gather.20
  302.8 136.2 all-gather.22
  441.1 136.2 all-gather.24
  579.4 38.3 all-gather.26
  620.0 38.8 all-gather.28
  661.0 48.0 all-gather.30
  711.2 47.7 all-gather.32
  761.1 136.6 all-gather.36
  900.0 136.2 all-gather.34
  1038.3 136.2 all-gather.38
  1655.3 2086.4 all-reduce.17
  3774.3 305.6 all-reduce.19
where the time goes:
time: 4220 us; the launch traced here: 4210 us
  waiting for transfers between devices  3200 us (76%)
  local copies, waits for them, and re-layouts  420 us (10%)
  matrix products  259 us (6%)
  other arithmetic  164 us (4%)
  blocking collectives  112 us (3%)
  starting transfers between devices  44.7 us (1%)
    unnamed x15, waiting for transfers between devices  2090 us
    psum x1, waiting for transfers between devices, reduce_grads(): return lax.psum(owned, 'seq').astype(jnp.float32).reshape(-1)  294 us
    unnamed x415, local copies, waits for them, and re-layouts  131 us
    all_gather x1, waiting for transfers between devices, local(): lax.all_gather(w_gate2, 'dp', axis=0, tiled=True)  129 us
    all_gather x1, waiting for transfers between devices, local(): lax.all_gather(w_down2, 'dp', axis=0, tiled=True)  129 us
    all_gather x1, waiting for transfers between devices, local(): lax.all_gather(w_up1, 'dp', axis=0, tiled=True)  129 us
    all_gather x1, waiting for transfers between devices, local(): lax.all_gather(w_down1, 'dp', axis=0, tiled=True)  127 us
    all_gather x1, waiting for transfers between devices, local(): lax.all_gather(w_gate1, 'dp', axis=0, tiled=True)  107 us
  transfers between devices with their start and end apart: 24, of which 14 were waited for; matrix products, arithmetic and copies ran while one was open for 9% of the time, Pallas kernels for 0%

commit v1 on v0

v1 whole, which is shorter than its diff:
```python
import jax
import jax.numpy as jnp
from jax import lax
from jax.experimental import pallas as pl
from jax.experimental.pallas import tpu as pltpu
from jax.sharding import PartitionSpec as P

EPS = 1e-05
THETA = 1000000.0
NEG = -1e30
F32 = jnp.float32
BF16 = jnp.bfloat16
TILE = 256
LANES = 128
VMEM_LIMIT = 56 << 20


def left_dot(left, right):
    return lax.dot_general(left, right, (((0,), (0,)), ((), ())), preferred_element_type=F32)


def right_dot(left, right):
    return lax.dot_general(left, right, (((1,), (1,)), ((), ())), preferred_element_type=F32)


def plain_dot(left, right):
    return jnp.dot(left, right, preferred_element_type=F32)


def unit_scale(value):
    scale = lax.rsqrt(jnp.mean(value * value, -1, keepdims=True) + EPS)
    return (value * scale, scale)


def norm_back(grad_out, gain, unit, scale):
    weighted = grad_out * gain
    grad_in = scale * (weighted - unit * jnp.mean(weighted * unit, -1, keepdims=True))
    gain_grad = jnp.sum((grad_out * unit).reshape(-1, unit.shape[-1]), 0)
    return (grad_in, gain_grad)


def doc_index(bounds, places):
    later = bounds[1:]
    passed = (later <= places[..., None]) & (later > 0)
    return jnp.sum(passed.astype(jnp.int32), -1)


def doc_starts(bounds, places):
    return jnp.max(jnp.where(bounds <= places[..., None], bounds, 0), -1)


def rope_tables(places, head):
    half = head // 2
    freqs = THETA ** (-(2.0 * jnp.arange(half, dtype=F32)) / head)
    angles = places.astype(F32)[:, None] * freqs
    cosine = jnp.cos(angles)
    sine = jnp.sin(angles)
    return (
        jnp.concatenate([cosine] * 4, 1),
        jnp.concatenate([-sine, sine, -sine, sine], 1),
    )


def seq_bits():
    size = lax.axis_size("seq")
    bits = []
    bit = 1
    while bit < size:
        bits.append(bit)
        bit = bit * 2
    return bits


def swap_seq(array, bit):
    size = lax.axis_size("seq")
    return lax.ppermute(array, "seq", [(i, i ^ bit) for i in range(size)])


def seq_gather(block):
    have = {0: block}
    for bit in reversed(seq_bits()):
        for place in sorted(have):
            have[place | bit] = swap_seq(have[place], bit)
    return jnp.concatenate([have[place] for place in sorted(have)], 0)


def seq_scatter(partial):
    size = lax.axis_size("seq")
    length = partial.shape[0] // size
    have = {place: partial[place * length : (place + 1) * length] for place in range(size)}
    for bit in seq_bits():
        for place in sorted(have, reverse=True):
            if place & bit:
                got = swap_seq(have.pop(place).astype(BF16), bit).astype(F32)
                have[place ^ bit] = have[place ^ bit] + got
    return have[0]


def flip_blocks(array):
    place = lax.axis_index("seq")
    for bit in seq_bits():
        shape = array.shape
        split = array.reshape((shape[0] // (2 * bit), 2, bit) + shape[1:])
        turned = jnp.concatenate([split[:, 1:], split[:, :1]], 1)
        array = jnp.where((place & bit) > 0, turned, split).reshape(shape)
    return array


def half_lanes(shape):
    return lax.broadcasted_iota(jnp.int32, shape, 1) < LANES // 2


def head_mean(value):
    row = lax.broadcasted_iota(jnp.int32, (LANES, LANES), 0) < LANES // 2
    column = half_lanes((LANES, LANES))
    ones = jnp.where(row == column, 2.0 / LANES, 0.0).astype(BF16)
    high = value.astype(BF16)
    low = (value - high.astype(F32)).astype(BF16)
    return plain_dot(high, ones) + plain_dot(low, ones)


def swap_quarters(value):
    quarter = LANES // 4
    lane = lax.broadcasted_iota(jnp.int32, value.shape, 1)
    first = (lane // quarter) % 2 == 0
    return jnp.where(
        first, pltpu.roll(value, LANES - quarter, 1), pltpu.roll(value, quarter, 1)
    )


def head_unit(value):
    scale = lax.rsqrt(head_mean(value * value) + EPS)
    return (value * scale, scale)


def pad_pair(value, second):
    lower = half_lanes(value.shape)
    if second:
        high = jnp.where(lower, 0.0, value)
        return (pltpu.roll(high, LANES // 2, 1), high)
    low = jnp.where(lower, value, 0.0)
    return (low, pltpu.roll(low, LANES // 2, 1))


def load_heads(raw_ref, cos_ref, sin_ref, gains_ref, source, target, length, pairs):
    rows = pl.ds(source, length)
    cosine = cos_ref[pl.ds(target, length), :]
    sine = sin_ref[pl.ds(target, length), :]
    groups = raw_ref.shape[1] // LANES

    def turned(group, gain):
        value = head_unit(raw_ref[rows, group * LANES : (group + 1) * LANES])[0] * gain
        return value * cosine + swap_quarters(value) * sine

    scale = (LANES // 2) ** (-0.5)
    queries = [(turned(g, gains_ref[0:1, :]) * scale).astype(BF16) for g in range(pairs)]
    keys = []
    values = []
    cached = {}
    for g in range(pairs):
        place = pairs * LANES + g * (LANES // 2)
        group, second = divmod(place, LANES)
        if group not in cached:
            cached[group] = turned(group, gains_ref[1:2, :]).astype(BF16).astype(F32)
        keys.append([k.astype(BF16) for k in pad_pair(cached[group], second > 0)])
        place = place + pairs * (LANES // 2)
        group, second = divmod(place, LANES)
        value = raw_ref[rows, group * LANES : (group + 1) * LANES]
        values.append([v.astype(BF16) for v in pad_pair(value, second > 0)])
    return (queries, keys, values)


def allowed_tile(start_ref, first_key, first_query):
    query = first_query + lax.broadcasted_iota(jnp.int32, (1, TILE), 1)
    start = start_ref[0:1, pl.ds(first_query, TILE)]
    key = first_key + lax.broadcasted_iota(jnp.int32, (TILE, TILE), 0)
    return (key >= start) & (key <= query)


def attention_forward_kernel(
    place_ref, raw_ref, cos_ref, sin_ref, start_ref, gains_ref,
    out_ref, wide_ref, total_ref, query_ref, key_ref, value_ref,
    *, length, pairs,
):
    full = raw_ref.shape[0]
    count = full // length
    place = place_ref[0]

    def prepare(block, _):
        target = pl.multiple_of(block * length, 8)
        source = pl.multiple_of((block ^ place) * length, 8)
        queries, keys, values = load_heads(
            raw_ref, cos_ref, sin_ref, gains_ref, source, target, length, pairs
        )
        for g in range(pairs):
            query_ref[g, pl.ds(target, length), :] = queries[g]
            for h in range(2):
                key_ref[2 * g + h, pl.ds(target, length), :] = keys[g][h]
                value_ref[2 * g + h, pl.ds(target, length), :] = values[g][h]
        return 0

    lax.fori_loop(0, count, prepare, 0)
    half = LANES // 2

    def query_tile(i, _):
        first_query = pl.multiple_of(i * TILE, TILE)

        def key_tile(j, carry):
            first_key = pl.multiple_of(j * TILE, TILE)
            allowed = allowed_tile(start_ref, first_key, first_query)
            sums, outs = carry
            new_sums = []
            new_outs = []
            for g in range(pairs):
                query = query_ref[g, pl.ds(first_query, TILE), :]
                total = outs[g]
                for h in range(2):
                    key = key_ref[2 * g + h, pl.ds(first_key, TILE), :]
                    value = value_ref[2 * g + h, pl.ds(first_key, TILE), :]
                    weight = jnp.where(allowed, jnp.exp(right_dot(key, query)), 0.0)
                    new_sums.append(sums[2 * g + h] + jnp.sum(weight, 0, keepdims=True))
                    total = total + lax.dot_general(
                        value, weight.astype(BF16), (((0,), (0,)), ((), ())),
                        preferred_element_type=F32,
                    )
                new_outs.append(total)
            return (new_sums, new_outs)

        carry = (
            [jnp.zeros((1, TILE), F32) for _ in range(2 * pairs)],
            [jnp.zeros((LANES, TILE), F32) for _ in range(pairs)],
        )
        sums, outs = lax.fori_loop(0, i + 1, key_tile, carry)
        columns = pl.ds(first_query, TILE)
        for g in range(pairs):
            scaled = jnp.concatenate(
                [outs[g][h * half : (h + 1) * half] / sums[2 * g + h] for h in range(2)], 0
            )
            for h in range(2):
                total_ref[2 * g + h : 2 * g + h + 1, columns] = sums[2 * g + h]
            wide_ref[g * LANES : (g + 1) * LANES, columns] = scaled
            query_ref[g, columns, :] = scaled.T.astype(BF16)
        return 0

    lax.fori_loop(0, full // TILE, query_tile, 0)

    def finish(block, _):
        source = pl.multiple_of(block * length, 8)
        target = pl.multiple_of((block ^ place) * length, 8)
        for g in range(pairs):
            out_ref[pl.ds(target, length), g * LANES : (g + 1) * LANES] = query_ref[
                g, pl.ds(source, length), :
            ]
        return 0

    lax.fori_loop(0, count, finish, 0)


def attention_backward_kernel(
    place_ref, raw_ref, cos_ref, sin_ref, start_ref, gains_ref, wide_ref, total_ref, grad_ref,
    out_ref, gain_grad_ref,
    query_ref, key_ref, value_ref, hold_ref, dq_ref, dk_ref, dv_ref,
    *, length, pairs,
):
    full = raw_ref.shape[0]
    count = full // length
    place = place_ref[0]
    half = LANES // 2

    def prepare(block, _):
        target = pl.multiple_of(block * length, 8)
        source = pl.multiple_of((block ^ place) * length, 8)
        queries, keys, values = load_heads(
            raw_ref, cos_ref, sin_ref, gains_ref, source, target, length, pairs
        )
        rows = pl.ds(target, length)
        for g in range(pairs):
            query_ref[g, rows, :] = queries[g]
            hold_ref[g, rows, :] = grad_ref[
                pl.ds(source, length), g * LANES : (g + 1) * LANES
            ]
            dk_ref[g, rows, :] = jnp.zeros((length, LANES), F32)
            dv_ref[g, rows, :] = jnp.zeros((length, LANES), F32)
            for h in range(2):
                key_ref[2 * g + h, rows, :] = keys[g][h]
                value_ref[2 * g + h, rows, :] = values[g][h]
        return 0

    lax.fori_loop(0, count, prepare, 0)
    lower = half_lanes((TILE, LANES))

    def query_tile(i, _):
        first_query = pl.multiple_of(i * TILE, TILE)
        columns = pl.ds(first_query, TILE)
        inverse = [1.0 / total_ref[n : n + 1, columns] for n in range(2 * pairs)]
        inner = []
        for g in range(pairs):
            grad = hold_ref[g, columns, :].astype(F32).T
            both = grad * wide_ref[g * LANES : (g + 1) * LANES, columns]
            for h in range(2):
                inner.append(jnp.sum(both[h * half : (h + 1) * half], 0, keepdims=True))

        def key_tile(j, outs):
            first_key = pl.multiple_of(j * TILE, TILE)
            rows = pl.ds(first_key, TILE)
            allowed = allowed_tile(start_ref, first_key, first_query)
            new_outs = []
            for g in range(pairs):
                query = query_ref[g, columns, :]
                grad = hold_ref[g, columns, :]
                zero = jnp.zeros_like(query)
                total = outs[g]
                d_key = dk_ref[g, rows, :]
                d_value = dv_ref[g, rows, :]
                for h in range(2):
                    keep = lower if h == 0 else jnp.logical_not(lower)
                    key = key_ref[2 * g + h, rows, :]
                    value = value_ref[2 * g + h, rows, :]
                    weight = jnp.exp(right_dot(key, query)) * inverse[2 * g + h]
                    weight = jnp.where(allowed, weight, 0.0)
                    d_weight = right_dot(value, grad)
                    d_score = (weight * (d_weight - inner[2 * g + h])).astype(BF16)
                    d_value = d_value + plain_dot(
                        weight.astype(BF16), jnp.where(keep, grad, zero)
                    )
                    d_key = d_key + plain_dot(d_score, jnp.where(keep, query, zero))
                    total = total + lax.dot_general(
                        key, d_score, (((0,), (0,)), ((), ())), preferred_element_type=F32
                    )
                dk_ref[g, rows, :] = d_key
                dv_ref[g, rows, :] = d_value
                new_outs.append(total)
            return new_outs

        outs = lax.fori_loop(
            0, i + 1, key_tile, [jnp.zeros((LANES, TILE), F32) for _ in range(pairs)]
        )
        for g in range(pairs):
            dq_ref[g, columns, :] = outs[g].T
        return 0

    lax.fori_loop(0, full // TILE, query_tile, 0)
    scale = half ** (-0.5)

    def finish(block, carry):
        source = pl.multiple_of(block * length, 8)
        target = pl.multiple_of((block ^ place) * length, 8)
        rows = pl.ds(source, length)
        cosine = cos_ref[rows, :]
        sine = sin_ref[rows, :]
        low = half_lanes((length, LANES))

        def back(grad, group, gain):
            grad = grad.astype(BF16).astype(F32)
            unit, inverse = head_unit(
                raw_ref[pl.ds(target, length), group * LANES : (group + 1) * LANES]
            )
            d_rot = grad * cosine + swap_quarters(grad * sine)
            weighted = d_rot * gain
            d_raw = inverse * (weighted - unit * head_mean(weighted * unit))
            return (d_raw, d_rot * unit)

        query_gain, key_gain = carry
        for g in range(pairs):
            d_raw, terms = back(dq_ref[g, rows, :] * scale, g, gains_ref[0:1, :])
            query_gain = query_gain + jnp.sum(terms, 0, keepdims=True)
            out_ref[pl.ds(target, length), g * LANES : (g + 1) * LANES] = d_raw.astype(BF16)
        groups = {}
        for kind, held in ((0, dk_ref), (1, dv_ref)):
            for g in range(pairs):
                place_of = pairs * LANES + kind * pairs * half + g * half
                group, second = divmod(place_of, LANES)
                value = held[g, rows, :]
                value = value + pltpu.roll(value, half, 1)
                groups.setdefault(group, {})[second // half] = (kind, value)
        for group, parts in groups.items():
            merged = jnp.where(low, parts[0][1], parts[1][1])
            is_key = [parts[n][0] == 0 for n in range(2)]
            result = merged
            if any(is_key):
                d_raw, terms = back(merged, group, gains_ref[1:2, :])
                if not is_key[1]:
                    d_raw = jnp.where(low, d_raw, merged)
                    terms = jnp.where(low, terms, 0.0)
                result = d_raw
                key_gain = key_gain + jnp.sum(terms, 0, keepdims=True)
            out_ref[pl.ds(target, length), group * LANES : (group + 1) * LANES] = result.astype(
                BF16
            )
        return (query_gain, key_gain)

    zero = jnp.zeros((1, LANES), F32)
    query_gain, key_gain = lax.fori_loop(0, count, finish, (zero, zero))
    gain_grad_ref[0:1, :] = query_gain
    gain_grad_ref[1:2, :] = key_gain


def whole(count):
    return [pl.BlockSpec(memory_space=pltpu.VMEM)] * count


def attention_forward(place, raw, cosine, sine, start, gains, length):
    full, columns = raw.shape
    pairs = columns // (2 * LANES)
    return pl.pallas_call(
        lambda *refs: attention_forward_kernel(*refs, length=length, pairs=pairs),
        in_specs=[pl.BlockSpec(memory_space=pltpu.SMEM)] + whole(5),
        out_specs=tuple(whole(3)),
        out_shape=(
            jax.ShapeDtypeStruct((full, pairs * LANES), BF16),
            jax.ShapeDtypeStruct((pairs * LANES, full), F32),
            jax.ShapeDtypeStruct((8, full), F32),
        ),
        scratch_shapes=[
            pltpu.VMEM((pairs, full, LANES), BF16),
            pltpu.VMEM((2 * pairs, full, LANES), BF16),
            pltpu.VMEM((2 * pairs, full, LANES), BF16),
        ],
        compiler_params=pltpu.CompilerParams(vmem_limit_bytes=VMEM_LIMIT),
        name="attention_forward",
    )(place, raw, cosine, sine, start, gains)


def attention_backward(place, raw, cosine, sine, start, gains, wide, totals, grads, length):
    full, columns = raw.shape
    pairs = columns // (2 * LANES)
    return pl.pallas_call(
        lambda *refs: attention_backward_kernel(*refs, length=length, pairs=pairs),
        in_specs=[pl.BlockSpec(memory_space=pltpu.SMEM)] + whole(8),
        out_specs=tuple(whole(2)),
        out_shape=(
            jax.ShapeDtypeStruct((full, columns), BF16),
            jax.ShapeDtypeStruct((2, LANES), F32),
        ),
        scratch_shapes=[
            pltpu.VMEM((pairs, full, LANES), BF16),
            pltpu.VMEM((2 * pairs, full, LANES), BF16),
            pltpu.VMEM((2 * pairs, full, LANES), BF16),
            pltpu.VMEM((pairs, full, LANES), BF16),
            pltpu.VMEM((pairs, full, LANES), F32),
            pltpu.VMEM((pairs, full, LANES), F32),
            pltpu.VMEM((pairs, full, LANES), F32),
        ],
        compiler_params=pltpu.CompilerParams(vmem_limit_bytes=VMEM_LIMIT),
        name="attention_backward",
    )(place, raw, cosine, sine, start, gains, wide, totals, grads)

def column_block(weight, parts):
    size = lax.axis_size("seq")
    place = lax.axis_index("seq")
    rows, columns = weight.shape
    block = columns // parts // size
    split = weight.reshape(rows, parts, size * block)
    return lax.dynamic_slice_in_dim(split, place * block, block, 2).reshape(rows, parts * block)


def deal_pairs():
    size = lax.axis_size("seq")
    count = lax.axis_size("dp")
    pairs = []
    for place in range(size):
        for owner in range(count):
            source = (owner % size) * count + place * (count // size) + owner // size
            pairs.append((source, place * count + owner))
    return pairs


def deal_rows(weight):
    size = lax.axis_size("seq")
    place = lax.axis_index("seq")
    piece = weight.shape[0] // size
    part = lax.dynamic_slice_in_dim(weight, place * piece, piece, 0)
    return lax.ppermute(part, ("seq", "dp"), deal_pairs())


def undeal_rows(part):
    return lax.ppermute(part, ("seq", "dp"), [(b, a) for a, b in deal_pairs()])


def dp_gather(block):
    return lax.all_gather(block, "dp", axis=0, tiled=True)


def dp_scatter(grads):
    return lax.psum_scatter(grads, "dp", scatter_dimension=0, tiled=True)


def share(owned):
    size = lax.axis_size("seq")
    place = lax.axis_index("seq")
    everywhere = seq_gather(owned).reshape((size,) + owned.shape)
    return [lax.dynamic_index_in_dim(everywhere, place ^ i, 0, False) for i in range(size)]


def split_columns(blocks, parts):
    results = []
    offset = 0
    for split, columns in parts:
        pieces = []
        for number in range(split):
            start = offset + number * columns
            pieces = pieces + [block[:, start : start + columns] for block in blocks]
        results.append(jnp.concatenate(pieces, 1).astype(F32))
        offset = offset + split * columns
    return (results, [block[:, offset:] for block in blocks])


def ffn_gate(normed, weights):
    hidden = weights.shape[1] // 3
    both = plain_dot(normed, weights[:, : 2 * hidden])
    gate = both[:, :hidden]
    upper = both[:, hidden:]
    sigma = jax.nn.sigmoid(gate)
    act = (gate * sigma * upper).astype(BF16)
    return (gate, upper, act)


def ffn_back(grad_all, kept, normed_all, weights):
    gate, upper, act = kept
    hidden = weights.shape[1] // 3
    sigma = jax.nn.sigmoid(gate)
    d_down = left_dot(grad_all, act)
    d_act = plain_dot(grad_all, weights[:, 2 * hidden :])
    d_gate = (d_act * upper * sigma * (1.0 + gate * (1.0 - sigma))).astype(BF16)
    d_up = (d_act * gate * sigma).astype(BF16)
    d_both = jnp.concatenate([d_gate, d_up], 1)
    d_gate_up = left_dot(normed_all, d_both)
    partial = right_dot(d_both, weights[:, : 2 * hidden])
    grads = jnp.concatenate([d_gate_up.astype(BF16), d_down.astype(BF16)], 1)
    return (seq_scatter(partial), grads)


def local(
    x_in,
    cu_seqlens,
    positions,
    cotangent,
    w_in,
    conv_w,
    w_out,
    w_gate1,
    w_up1,
    w_down1,
    g_mix1,
    g_ffn1,
    w_q,
    key_projection_weight,
    value_projection_weight,
    w_o,
    g_q,
    g_k,
    w_gate2,
    w_up2,
    w_down2,
    g_attn2,
    g_ffn2,
):
    rows, length, width = x_in.shape
    assert rows == 1
    seq_count = lax.axis_size("seq")
    dp_count = lax.axis_size("dp")
    seq_place = lax.axis_index("seq")
    full = length * seq_count
    channels = width // seq_count
    slots = width // dp_count
    head = g_q.shape[0] * dp_count
    taps = conv_w.shape[0]
    reach = taps - 1

    x_all = seq_gather(x_in.reshape(length, width)).astype(F32)
    head_gains = jnp.pad(jnp.stack([g_q, g_k], 1), ((0, slots - head // dp_count), (0, 0)))
    small = jnp.concatenate(
        [conv_w.T, jnp.stack([g_mix1, g_ffn1, g_attn2, g_ffn2], 1), head_gains], 1
    )
    small = jnp.pad(small, ((0, 0), (0, 128 - small.shape[1])))
    dealt = deal_rows(jnp.stack([w_out, w_o], 1))
    out_piece = dealt[:, 0].reshape(slots, -1)
    o_piece = dealt[:, 1].reshape(slots, -1)
    mix_all = dp_gather(jnp.concatenate([column_block(w_in, 3), small, out_piece], 1))
    ffn_one = dp_gather(
        jnp.concatenate([column_block(w, 1) for w in (w_gate1, w_up1, w_down1)], 1)
    )
    attn_all = dp_gather(
        jnp.concatenate(
            [
                column_block(w_q, 1),
                column_block(key_projection_weight, 1),
                column_block(value_projection_weight, 1),
                o_piece,
            ],
            1,
        )
    )
    ffn_two = dp_gather(
        jnp.concatenate([column_block(w, 1) for w in (w_gate2, w_up2, w_down2)], 1)
    )
    in_block = mix_all[:, : 3 * channels]
    out_block = mix_all[:, 3 * channels + 128 :].reshape(channels, width)
    qkv_width = attn_all.shape[1] - channels
    qkv_block = attn_all[:, :qkv_width]
    o_block = attn_all[:, qkv_width:].reshape(channels, width)
    small_all = mix_all[:, 3 * channels : 3 * channels + 128].astype(F32).T
    kernel = lax.dynamic_slice_in_dim(small_all[:taps], seq_place * channels, channels, 1)
    gain_mix, gain_ffn_one, gain_attn, gain_ffn_two = (small_all[taps + i] for i in range(4))
    head_gains = small_all[taps + 4 : taps + 6].reshape(2, dp_count, slots)
    head_gains = jnp.tile(head_gains[:, :, : head // dp_count].reshape(2, head), (1, 2))

    bounds = cu_seqlens[0]
    turn = seq_place ^ jnp.arange(seq_count, dtype=jnp.int32)
    places = turn[:, None] * length + jnp.arange(length, dtype=jnp.int32)[None, :]
    docs_here = doc_index(bounds, places)
    masks = [
        (doc_index(bounds, places - tap) == docs_here).astype(F32)[..., None]
        for tap in range(1, reach + 1)
    ]

    order = jnp.arange(full, dtype=jnp.int32)
    starts = doc_starts(bounds, order)
    cosine, sine = rope_tables(order - starts, head)
    starts = starts[None, :]
    place = seq_place.reshape(1).astype(jnp.int32)

    x_flat = x_in.reshape(length, width).astype(F32)
    unit_one, scale_one = unit_scale(x_flat)
    normed_one = (unit_scale(x_all)[0] * gain_mix).astype(BF16)
    projected = plain_dot(normed_one, in_block).reshape(seq_count, length, 3 * channels)
    part_b = projected[..., :channels]
    part_c = projected[..., channels : 2 * channels]
    part_x = projected[..., 2 * channels :]
    product = (part_b * part_x).astype(BF16)
    tails = flip_blocks(product[:, length - reach :])
    before = flip_blocks(jnp.concatenate([jnp.zeros_like(tails[:1]), tails[:-1]], 0))
    extended = jnp.concatenate([before, product], 1).astype(F32)
    conv_out = kernel[0] * extended[:, reach:]
    for tap in range(1, reach + 1):
        conv_out = (
            conv_out
            + kernel[tap] * extended[:, reach - tap : reach - tap + length] * masks[tap - 1]
        )
    gated = (part_c * conv_out).astype(BF16).reshape(full, channels)
    hidden_one = x_flat + seq_scatter(plain_dot(gated, out_block))

    unit_two, scale_two = unit_scale(hidden_one)
    normed_two = seq_gather((unit_two * gain_ffn_one).astype(BF16))
    keep_one = ffn_gate(normed_two, ffn_one)
    hidden = ffn_one.shape[1] // 3
    hidden_two = hidden_one + seq_scatter(right_dot(keep_one[2], ffn_one[:, 2 * hidden :]))

    unit_three, scale_three = unit_scale(hidden_two)
    normed_three = seq_gather((unit_three * gain_attn).astype(BF16))
    raw = plain_dot(normed_three, qkv_block)
    kv_width = (qkv_width - channels) // 2
    attended_low, wide, totals = attention_forward(
        place, raw, cosine, sine, starts, head_gains, length
    )
    hidden_three = hidden_two + seq_scatter(plain_dot(attended_low, o_block))

    unit_four, scale_four = unit_scale(hidden_three)
    normed_four = seq_gather((unit_four * gain_ffn_two).astype(BF16))
    keep_two = ffn_gate(normed_four, ffn_two)
    hidden_four = hidden_three + seq_scatter(right_dot(keep_two[2], ffn_two[:, 2 * hidden :]))
    out = hidden_four.astype(BF16).reshape(rows, length, width)

    cotangent_all = seq_gather(cotangent.reshape(length, width))
    grad_four = cotangent.reshape(length, width).astype(F32)
    d_ffn_in, grads_two = ffn_back(cotangent_all, keep_two, normed_four, ffn_two)
    owned_two = dp_scatter(grads_two)
    d_hidden, d_gain_ffn_two = norm_back(d_ffn_in, gain_ffn_two, unit_four, scale_four)
    grad_three = grad_four + d_hidden

    grad_attn = seq_gather(grad_three.astype(BF16))
    d_w_o = left_dot(attended_low, grad_attn)
    d_attended = right_dot(grad_attn, o_block).astype(BF16)
    d_raw, d_head_gains = attention_backward(
        place, raw, cosine, sine, starts, head_gains, wide, totals, d_attended, length
    )
    d_head_gains = d_head_gains[:, :head] + d_head_gains[:, head:]
    d_qkv = left_dot(normed_three, d_raw)
    d_attn_in = seq_scatter(right_dot(d_raw, qkv_block))
    grads_attn = jnp.concatenate(
        [d_qkv.astype(BF16), d_w_o.astype(BF16).reshape(width, channels)], 1
    )
    owned_attn = dp_scatter(grads_attn)
    d_attn_h, d_gain_attn = norm_back(d_attn_in, gain_attn, unit_three, scale_three)
    grad_two = grad_three + d_attn_h

    grad_two_all = seq_gather(grad_two.astype(BF16))
    grad_two_all, owned_two = lax.optimization_barrier((grad_two_all, owned_two))
    d_ffn_in_one, grads_one = ffn_back(grad_two_all, keep_one, normed_two, ffn_one)
    d_hidden_one, d_gain_ffn_one = norm_back(d_ffn_in_one, gain_ffn_one, unit_two, scale_two)
    grad_one = grad_two + d_hidden_one

    grad_mix = seq_gather(grad_one.astype(BF16))
    grad_mix, owned_attn, grads_one = lax.optimization_barrier((grad_mix, owned_attn, grads_one))
    owned_one = dp_scatter(grads_one)
    d_w_out = left_dot(gated, grad_mix)
    d_gated = right_dot(grad_mix, out_block).reshape(seq_count, length, channels)
    d_part_c = d_gated * conv_out
    d_conv = d_gated * part_c
    sent = [d_conv * masks[tap - 1] for tap in range(1, reach + 1)]
    kernel_grads = [jnp.sum((d_conv * extended[:, reach:]).reshape(-1, channels), 0)]
    for tap in range(1, reach + 1):
        piece = extended[:, reach - tap : reach - tap + length]
        kernel_grads.append(jnp.sum((sent[tap - 1] * piece).reshape(-1, channels), 0))
    d_product_sum = kernel[0] * d_conv
    for tap in range(1, reach + 1):
        heads = flip_blocks(sent[tap - 1][:, :tap])
        after = flip_blocks(jnp.concatenate([heads[1:], jnp.zeros_like(heads[:1])], 0))
        moved = jnp.concatenate([sent[tap - 1][:, tap:], after], 1)
        d_product_sum = d_product_sum + kernel[tap] * moved
    d_product = lax.optimization_barrier(d_product_sum.astype(BF16)).astype(F32)
    d_projected = jnp.concatenate([d_product * part_x, d_part_c, d_product * part_b], -1)
    d_projected = d_projected.astype(BF16).reshape(full, 3 * channels)
    d_w_in = left_dot(normed_one, d_projected)
    d_normed = seq_scatter(right_dot(d_projected, in_block))
    d_x_part, d_gain_mix = norm_back(d_normed, gain_mix, unit_one, scale_one)
    d_x = (grad_one + d_x_part).reshape(rows, length, width)

    kernel_wide = lax.dynamic_update_slice_in_dim(
        jnp.zeros((taps, width), F32), jnp.stack(kernel_grads), seq_place * channels, 1
    )
    head_wide = jnp.pad(
        d_head_gains.reshape(2, dp_count, -1),
        ((0, 0), (0, 0), (0, slots - head // dp_count)),
    ).reshape(2, width)
    vectors = jnp.concatenate(
        [
            jnp.stack([d_gain_mix, d_gain_ffn_one, d_gain_attn, d_gain_ffn_two]),
            kernel_wide,
            head_wide,
        ],
        0,
    )
    vector_columns = jnp.pad(vectors.T, ((0, 0), (0, 128 - vectors.shape[0])))
    grads_mix = jnp.concatenate(
        [
            d_w_in.astype(BF16),
            vector_columns.astype(BF16),
            d_w_out.astype(BF16).reshape(width, channels),
        ],
        1,
    )
    grads_mix, owned_one = lax.optimization_barrier((grads_mix, owned_one))
    owned_mix = dp_scatter(grads_mix)

    def redeal(owned):
        block = owned[:, owned.shape[1] - channels :].reshape(-1, width)
        back = undeal_rows(block).reshape(slots, channels)
        return jnp.concatenate([owned[:, : owned.shape[1] - channels], back], 1)

    (d_wgate_two, d_wup_two, d_down_two), _ = split_columns(share(owned_two), [(1, hidden)] * 3)
    shared_one = share(jnp.concatenate([owned_one, redeal(owned_attn)], 1))
    one, rest_attn = split_columns(
        shared_one, [(1, hidden)] * 3 + [(1, channels), (1, kv_width), (1, kv_width)]
    )
    d_wgate_one, d_wup_one, d_down_one, d_w_q, d_w_k, d_w_v = one
    (d_w_in_full,), rest_mix = split_columns(share(redeal(owned_mix)), [(3, channels)])
    d_w_o_full = jnp.concatenate([b.reshape(-1, width) for b in rest_attn], 0).astype(F32)
    d_w_out_full = jnp.concatenate([b[:, 128:].reshape(-1, width) for b in rest_mix], 0)
    d_w_out_full = d_w_out_full.astype(F32)
    sums = sum(b[:, :128].astype(F32) for b in rest_mix).T
    small_head = head // dp_count
    return (
        out,
        d_x,
        d_w_in_full,
        sums[4 : 4 + taps],
        d_w_out_full,
        d_wgate_one,
        d_wup_one,
        d_down_one,
        sums[0],
        sums[1],
        d_w_q,
        d_w_k,
        d_w_v,
        d_w_o_full,
        sums[4 + taps, :small_head],
        sums[5 + taps, :small_head],
        d_wgate_two,
        d_wup_two,
        d_down_two,
        sums[2],
        sums[3],
    )


def solution(mesh):
    matrix = P("dp", None)
    vector = P("dp")
    tokens = P("dp", "seq", None)
    kernel = P(None, "dp")
    in_specs = (
        (tokens, matrix, P("dp", "seq"), tokens, matrix, kernel)
        + (matrix,) * 4
        + (vector,) * 2
        + (matrix,) * 4
        + (vector,) * 2
        + (matrix,) * 3
        + (vector,) * 2
    )
    out_specs = (
        (tokens, tokens, matrix, kernel)
        + (matrix,) * 4
        + (vector,) * 2
        + (matrix,) * 4
        + (vector,) * 2
        + (matrix,) * 3
        + (vector,) * 2
    )
    return jax.shard_map(local, mesh=mesh, in_specs=in_specs, out_specs=out_specs, check_vma=False)
```

time: 4220 us -> 967 us (0.23)
  waiting for transfers between devices: 3200 us -> 511 us
  local copies, waits for them, and re-layouts: 420 us -> 41.2 us
  blocking collectives: 112 us -> 0 us
  matrix products: 259 us -> 171 us
  other arithmetic: 164 us -> 101 us
  Pallas kernels: 0 us -> 62.2 us
    unnamed x15 -> x10, waiting for transfers between devices: 2090 us -> 85.7 us
    all_gather x12 -> x4, waiting for transfers between devices: 802 us -> 74.3 us  [dp_gather(): return lax.all_gather(block, 'dp', axis=0, tiled=True)]
    ppermute x2 -> x60, waiting for transfers between devices: 0.01 us -> 303 us  [the longest x57 303 us: swap_seq(): return lax.ppermute(array, 'seq', [(i, i ^ bit) for i in range(size)])]
    psum x1 -> x0, waiting for transfers between devices: 294 us -> none  [reduce_grads(): return lax.psum(owned, 'seq').astype(jnp.float32).reshape(-1)]
    unnamed x415 -> x207, local copies, waits for them, and re-layouts: 131 us -> 9.42 us
    reshape x35 -> x27, local copies, waits for them, and re-layouts: 124 us -> 12.5 us  [the longest x6 5.04 us: column_block(): lax.dynamic_slice_in_dim(split, place * block, block, 2)]
    all_gather x5 -> x0, blocking collectives: 92.2 us -> none  [the longest x1 22.5 us: local(): lax.all_gather(g_mix1, 'dp', axis=0, tiled=True)]
    unnamed x21 -> x0, other arithmetic: 70.9 us -> none
  transfers between devices with their start and end apart: 24 -> 68, of which waited for: 14 -> 30; matrix products, arithmetic and copies ran while one was open for 9% -> 26% of each run, Pallas kernels for 0% -> 6%
where the time goes in v1:
time: 967 us; the launch traced here: 959 us
  waiting for transfers between devices  511 us (53%)
  matrix products  171 us (18%)
  other arithmetic  101 us (10%)
  Pallas kernels  62.2 us (6%)
  starting transfers between devices  54.8 us (6%)
  local copies, waits for them, and re-layouts  41.2 us (4%)
  between operations  16.9 us (2%)
    ppermute x57, waiting for transfers between devices, swap_seq(): return lax.ppermute(array, 'seq', [(i, i ^ bit) for i in range(size)])  303 us
    unnamed x10, waiting for transfers between devices  85.7 us
    all_gather x4, waiting for transfers between devices, dp_gather(): return lax.all_gather(block, 'dp', axis=0, tiled=True)  74.3 us
    dot_general x8, matrix products, plain_dot(): return jnp.dot(left, right, preferred_element_type=F32)  67.9 us
    dot_general x8, matrix products, right_dot(): lax.dot_general(left, right, (((1,), (1,)), ((), ())), preferred_element_...  53 us
    ppermute x57, starting transfers between devices, swap_seq(): return lax.ppermute(array, 'seq', [(i, i ^ bit) for i in range(size)])  51.6 us
    dot_general x8, matrix products, left_dot(): lax.dot_general(left, right, (((0,), (0,)), ((), ())), preferred_element_...  50.1 us
    reduce_scatter x2, waiting for transfers between devices, dp_scatter(): return lax.psum_scatter(grads, 'dp', scatter_dimension=0, tiled=True)  48 us
  transfers between devices with their start and end apart: 68, of which 30 were waited for; matrix products, arithmetic and copies ran while one was open for 26% of the time, Pallas kernels for 6%

profile of v1, /device:TPU:0, one launch (start us, length us, event | category | flops | bytes accessed | tf_op | source)
XLA Modules:
  0.0 958.6 jit_solution(5338820047552578976)
XLA Ops:
  27.2 18.2 %collective-permute-done.1 = bf16[384,1024]{1,0:T(8,128)(2,1)S(1)} collective-permute-done((bf16[384,1024]{1,0:T(8,128)(2,1)S(1)}, bf16[384,1024]{1,0:T(8,128)(2,1)S(1)}, u32[]{:S(2)}, u32[]{:S(2)}) %collective-permute-start.1) | collective-permute-done | bytes 786464 | tf_op jit(solution)/shard_map/ppermute | solution.py:76
  48.5 30.6 %all-gather.5.cloned.1.call-done = bf16[1024,1152]{0,1:T(8,128)(2,1)} async-done(((bf16[128,1152]{0,1:T(8,128)(2,1)}), bf16[1024,1152]{0,1:T(8,128)(2,1)}) %all-gather.5.cloned.1.call-update) | async-done | bytes 2359312 | tf_op jit(solution)/shard_map/all_gather | solution.py:481
  104.5 15.5 %collective-permute-done.6 = bf16[384,1024]{1,0:T(8,128)(2,1)} collective-permute-done((bf16[384,1024]{1,0:T(8,128)(2,1)S(1)}, bf16[384,1024]{1,0:T(8,128)(2,1)}, u32[]{:S(2)}, u32[]{:S(2)}) %collective-permute-start.6) | collective-permute-done | bytes 786464 | tf_op jit(solution)/shard_map/ppermute | solution.py:76
  124.6 17.0 %collective-permute-done.8 = bf16[384,1024]{1,0:T(8,128)(2,1)S(1)} collective-permute-done((bf16[384,1024]{1,0:T(8,128)(2,1)S(1)}, bf16[384,1024]{1,0:T(8,128)(2,1)S(1)}, u32[]{:S(2)}, u32[]{:S(2)}) %collective-permute-start.8) | collective-permute-done | bytes 786464 | tf_op jit(solution)/shard_map/ppermute | solution.py:76
  145.2 43.7 %all-gather.7.cloned.1.call-done = bf16[1024,3456]{1,0:T(8,128)(2,1)} async-done(((bf16[128,3456]{1,0:T(8,128)(2,1)}), bf16[1024,3456]{1,0:T(8,128)(2,1)}) %all-gather.7.cloned.1.call-update) | async-done | bytes 7077904 | tf_op jit(solution)/shard_map/all_gather | solution.py:481
  214.0 18.1 %collective-permute-done.12 = bf16[384,1024]{1,0:T(8,128)(2,1)S(1)} collective-permute-done((bf16[384,1024]{1,0:T(8,128)(2,1)S(1)}, bf16[384,1024]{1,0:T(8,128)(2,1)S(1)}, u32[]{:S(2)}, u32[]{:S(2)}) %collective-permute-start.12) | collective-permute-done | bytes 786464 | tf_op jit(solution)/shard_map/ppermute | solution.py:76
  236.0 16.9 %collective-permute-done.14 = bf16[384,1024]{1,0:T(8,128)(2,1)} collective-permute-done((bf16[384,1024]{1,0:T(8,128)(2,1)}, bf16[384,1024]{1,0:T(8,128)(2,1)}, u32[]{:S(2)}, u32[]{:S(2)}) %collective-permute-start.14) | collective-permute-done | bytes 786464 | tf_op jit(solution)/shard_map/ppermute | solution.py:76
  266.9 25.7 %attention_forward.1 = (bf16[1536,256]{1,0:T(8,128)(2,1)}, f32[256,1536]{1,0:T(8,128)}, f32[8,1536]{1,0:T(8,128)}) custom-call(s32[1]{0:T(128)} %bitcast.33.refs_0_, f32[1536,512]{1,0:T(8,128)} %fusion.64.refs_1_, f32[1536,128]{1,0:T(8,128)} %get-tuple-element.368.refs_2_, f32[1536,128]{1,0:T(8,128)} %get-tuple-element.369.refs_3_, ...), custom_call_target="tpu_custom_call" | custom-call | tf_op jit(solution)/shard_map/attention_forward/pallas_call | solution.py:405
  299.2 18.3 %collective-permute-done.18 = bf16[384,1024]{1,0:T(8,128)(2,1)S(1)} collective-permute-done((bf16[384,1024]{1,0:T(8,128)(2,1)S(1)}, bf16[384,1024]{1,0:T(8,128)(2,1)S(1)}, u32[]{:S(2)}, u32[]{:S(2)}) %collective-permute-start.18) | collective-permute-done | bytes 786464 | tf_op jit(solution)/shard_map/ppermute | solution.py:76
  321.2 18.7 %collective-permute-done.20 = bf16[384,1024]{1,0:T(8,128)(2,1)} collective-permute-done((bf16[384,1024]{1,0:T(8,128)(2,1)}, bf16[384,1024]{1,0:T(8,128)(2,1)}, u32[]{:S(2)}, u32[]{:S(2)}) %collective-permute-start.20) | collective-permute-done | bytes 786464 | tf_op jit(solution)/shard_map/ppermute | solution.py:76
  340.4 15.0 %collective-permute-done.26 = bf16[384,1024]{1,0:T(8,128)(2,1)} collective-permute-done((bf16[384,1024]{1,0:T(8,128)(2,1)}, bf16[384,1024]{1,0:T(8,128)(2,1)}, u32[]{:S(2)}, u32[]{:S(2)}) %collective-permute-start.26) | collective-permute-done | bytes 786464 | tf_op jit(solution)/shard_map/ppermute | solution.py:76
  355.4 14.0 %fusion.8 = f32[1536,2304]{1,0:T(8,128)} fusion(bf16[1024,3456]{1,0:T(8,128)(2,1)} %all-gather.11.cloned.1.call-done, bf16[384,1024]{1,0:T(8,128)(2,1)} %collective-permute-done.21, bf16[384,1024]{1,0:T(8,128)(2,1)} %collective-permute-done.20, bf16[384,1024]{1,0:T(8,128)(2,1)} %collective-permute-done.19, bf16[384,1024]{1,0:T(8,128)(2,1)} %multiply_convert_fusion.7), kind=kOutput, calls=%fused_computation.27 | convolution fusion | flops 7260340224 | bytes 22020096 | tf_op jit(solution)/shard_map/dot_general | solution.py:27
  426.2 18.3 %collective-permute-done.30 = bf16[384,1024]{1,0:T(8,128)(2,1)S(1)} collective-permute-done((bf16[384,1024]{1,0:T(8,128)(2,1)S(1)}, bf16[384,1024]{1,0:T(8,128)(2,1)S(1)}, u32[]{:S(2)}, u32[]{:S(2)}) %collective-permute-start.30) | collective-permute-done | bytes 786464 | tf_op jit(solution)/shard_map/ppermute | solution.py:76
  448.4 17.7 %collective-permute-done.32 = bf16[384,1024]{1,0:T(8,128)(2,1)S(1)} collective-permute-done((bf16[384,1024]{1,0:T(8,128)(2,1)S(1)}, bf16[384,1024]{1,0:T(8,128)(2,1)S(1)}, u32[]{:S(2)}, u32[]{:S(2)}) %collective-permute-start.32) | collective-permute-done | bytes 786464 | tf_op jit(solution)/shard_map/ppermute | solution.py:76
  472.9 36.5 %attention_backward.1 = (bf16[1536,512]{1,0:T(8,128)(2,1)}, f32[2,128]{1,0:T(2,128)}) custom-call(s32[1]{0:T(128)} %bitcast.33.refs_0_, f32[1536,512]{1,0:T(8,128)} %fusion.64.refs_1_, f32[1536,128]{1,0:T(8,128)} %get-tuple-element.368.refs_2_, f32[1536,128]{1,0:T(8,128)} %get-tuple-element.369.refs_3_, s32[1,1536]{1,0:T(1,128)} %broadcast_in_dim.9.refs_4_, ...), custom_call_target="tpu_custom_call" | custom-call | tf_op jit(solution)/shard_map/attention_backward/pallas_call | solution.py:427
  523.4 17.1 %collective-permute-done.36 = bf16[384,1024]{1,0:T(8,128)(2,1)S(1)} collective-permute-done((bf16[384,1024]{1,0:T(8,128)(2,1)S(1)}, bf16[384,1024]{1,0:T(8,128)(2,1)S(1)}, u32[]{:S(2)}, u32[]{:S(2)}) %collective-permute-start.36) | collective-permute-done | bytes 786464 | tf_op jit(solution)/shard_map/ppermute | solution.py:76
  541.2 15.6 %collective-permute-done.24 = bf16[384,1024]{1,0:T(8,128)(2,1)S(1)} collective-permute-done((bf16[384,1024]{1,0:T(8,128)(2,1)S(1)}, bf16[384,1024]{1,0:T(8,128)(2,1)S(1)}, u32[]{:S(2)}, u32[]{:S(2)}) %collective-permute-start.24) | collective-permute-done | bytes 786464 | tf_op jit(solution)/shard_map/ppermute | solution.py:76
  562.0 17.7 %collective-permute-done.38 = bf16[384,1024]{1,0:T(8,128)(2,1)S(1)} collective-permute-done((bf16[384,1024]{1,0:T(8,128)(2,1)}, bf16[384,1024]{1,0:T(8,128)(2,1)S(1)}, u32[]{:S(2)}, u32[]{:S(2)}) %collective-permute-start.38) | collective-permute-done | bytes 786464 | tf_op jit(solution)/shard_map/ppermute | solution.py:76
  601.5 14.5 %fusion.143 = (bf16[1536,1024]{1,0:T(8,128)(2,1)S(1)}, f32[1536,1024]{1,0:T(8,128)S(1)}) fusion(bf16[1024,3456]{1,0:T(8,128)(2,1)} %all-gather.7.cloned.1.call-done, bf16[1536,1152]{1,0:T(8,128)(2,1)} %get-tuple-element.208, bf16[1536,1152]{1,0:T(8,128)(2,1)S(1)} %get-tuple-element.207), kind=kOutput, calls=%fused_computation.362 | convolution fusion | flops 7263485952 | bytes 21233664 | tf_op jit(solution)/shard_map/dot_general | solution.py:23
  623.3 27.0 %reduce-scatter.13.cloned.1.call-done = bf16[128,768]{1,0:T(8,128)(2,1)} async-done(((bf16[1024,768]{1,0:T(8,128)(2,1)}), bf16[128,768]{1,0:T(8,128)(2,1)}) %reduce-scatter.13.cloned.1.call-update) | async-done | bytes 196624
  691.0 20.7 %collective-permute-done.58 = bf16[128,3456]{1,0:T(8,128)(2,1)} collective-permute-done((bf16[128,3456]{1,0:T(8,128)(2,1)}, bf16[128,3456]{1,0:T(8,128)(2,1)}, u32[]{:S(2)}, u32[]{:S(2)}) %collective-permute-start.58) | collective-permute-done | bytes 884768 | tf_op jit(solution)/shard_map/ppermute | solution.py:76
  773.1 48.0 %reduce-scatter.11.cloned.1.call-done = bf16[128,3456]{1,0:T(8,128)(2,1)} async-done(((bf16[1024,3456]{1,0:T(8,128)(2,1)}), bf16[128,3456]{1,0:T(8,128)(2,1)}) %reduce-scatter.11.cloned.1.call-update) | async-done | bytes 884752 | tf_op jit(solution)/shard_map/reduce_scatter | solution.py:485
  829.5 18.9 %collective-permute-done.55 = bf16[128,4224]{1,0:T(8,128)(2,1)} collective-permute-done((bf16[128,4224]{1,0:T(8,128)(2,1)}, bf16[128,4224]{1,0:T(8,128)(2,1)}, u32[]{:S(2)}, u32[]{:S(2)}) %collective-permute-start.55) | collective-permute-done | bytes 1081376 | tf_op jit(solution)/shard_map/ppermute | solution.py:76
  866.9 58.6 %reduce-scatter.15.cloned.1.call-done = bf16[128,1152]{1,0:T(8,128)(2,1)} async-done(((bf16[1024,1152]{1,0:T(8,128)(2,1)}), bf16[128,1152]{1,0:T(8,128)(2,1)}) %reduce-scatter.15.cloned.1.call-update) | async-done | bytes 294928
  (567 shorter events, 379.4 us)
Async XLA Ops:
  7.2 71.9 %all-gather.5.cloned.1.call-start = ((), (), s32[]{:S(2)}) async-start(), calls=%async_computation.4 | async-start | bytes 2654208 | tf_op jit(solution)/shard_map/all_gather | solution.py:481
  13.0 175.8 %all-gather.7.cloned.1.call-start = ((), (), s32[]{:S(2)}) async-start(), calls=%async_computation.5 | async-start | bytes 7962624 | tf_op jit(solution)/shard_map/all_gather | solution.py:481
  15.2 242.9 %all-gather.9.cloned.1.call-start = ((), (), s32[]{:S(2)}) async-start(), calls=%async_computation.6 | async-start | bytes 1769472 | tf_op jit(solution)/shard_map/all_gather | solution.py:481
  15.3 30.1 %collective-permute-start.1 = (bf16[384,1024]{1,0:T(8,128)(2,1)S(1)}, bf16[384,1024]{1,0:T(8,128)(2,1)S(1)}, u32[]{:S(2)}, u32[]{:S(2)}) collective-permute-start(bf16[384,1024]{1,0:T(8,128)(2,1)S(1)} %bitcast.193), channel_id=1, source_target_pairs={{0,16},{8,24},{16,0},{24,8},{1,17},{9,25},{17,1},{25,9},{2,18},{10... | collective-permute-start | bytes 2359304 | tf_op jit(solution)/shard_map/ppermute | solution.py:76
  104.4 251.0 %all-gather.11.cloned.1.call-start = ((), (), s32[]{:S(2)}) async-start(), calls=%async_computation.7 | async-start | bytes 7962624 | tf_op jit(solution)/shard_map/all_gather | solution.py:481
  124.6 20.6 %collective-permute-start.7 = (bf16[384,1024]{1,0:T(8,128)(2,1)S(1)}, bf16[384,1024]{1,0:T(8,128)(2,1)}, u32[]{:S(2)}, u32[]{:S(2)}) collective-permute-start(bf16[384,1024]{1,0:T(8,128)(2,1)S(1)} %multiply_convert_fusion.9), channel_id=1, source_target_pairs={{0,8},{8,0},{16,24},{24,16},{1,9},{9,1},{17,25},{25,17},{2,10},{10... | collective-permute-start | bytes 2359304 | tf_op jit(solution)/shard_map/ppermute | solution.py:76
  145.0 444.4 %reduce-scatter.9.cloned.1.call-start = ((), (), s32[]{:S(2)}) async-start(), calls=%async_computation.8 | async-start | bytes 7962624 | tf_op jit(solution)/shard_map/reduce_scatter | solution.py:485
  235.9 25.3 %collective-permute-start.13 = (bf16[384,1024]{1,0:T(8,128)(2,1)}, bf16[384,1024]{1,0:T(8,128)(2,1)}, u32[]{:S(2)}, u32[]{:S(2)}) collective-permute-start(bf16[384,1024]{1,0:T(8,128)(2,1)} %multiply_convert_fusion.8), channel_id=1, source_target_pairs={{0,8},{8,0},{16,24},{24,16},{1,9},{9,1},{17,25},{25,17},{2,10},{10... | collective-permute-start | bytes 2359304 | tf_op jit(solution)/shard_map/ppermute | solution.py:76
  319.1 20.8 %collective-permute-start.20 = (bf16[384,1024]{1,0:T(8,128)(2,1)}, bf16[384,1024]{1,0:T(8,128)(2,1)}, u32[]{:S(2)}, u32[]{:S(2)}) collective-permute-start(bf16[384,1024]{1,0:T(8,128)(2,1)} %multiply_convert_fusion.7), channel_id=1, source_target_pairs={{0,16},{8,24},{16,0},{24,8},{1,17},{9,25},{17,1},{25,9},{2,18},{10... | collective-permute-start | bytes 2359304 | tf_op jit(solution)/shard_map/ppermute | solution.py:76
  320.6 34.8 %collective-permute-start.26 = (bf16[384,1024]{1,0:T(8,128)(2,1)}, bf16[384,1024]{1,0:T(8,128)(2,1)}, u32[]{:S(2)}, u32[]{:S(2)}) collective-permute-start(bf16[384,1024]{1,0:T(8,128)(2,1)} %bitcast.38), channel_id=1, source_target_pairs={{0,16},{8,24},{16,0},{24,8},{1,17},{9,25},{17,1},{25,9},{2,18},{10... | collective-permute-start | bytes 2359304 | tf_op jit(solution)/shard_map/ppermute | solution.py:76
  321.2 34.3 %collective-permute-start.19 = (bf16[384,1024]{1,0:T(8,128)(2,1)}, bf16[384,1024]{1,0:T(8,128)(2,1)}, u32[]{:S(2)}, u32[]{:S(2)}) collective-permute-start(bf16[384,1024]{1,0:T(8,128)(2,1)} %multiply_convert_fusion.7), channel_id=1, source_target_pairs={{0,8},{8,0},{16,24},{24,16},{1,9},{9,1},{17,25},{25,17},{2,10},{10... | collective-permute-start | bytes 2359304 | tf_op jit(solution)/shard_map/ppermute | solution.py:76
  339.9 29.6 %collective-permute-start.25 = (bf16[384,1024]{1,0:T(8,128)(2,1)}, bf16[384,1024]{1,0:T(8,128)(2,1)}, u32[]{:S(2)}, u32[]{:S(2)}) collective-permute-start(bf16[384,1024]{1,0:T(8,128)(2,1)} %bitcast.38), channel_id=1, source_target_pairs={{0,8},{8,0},{16,24},{24,16},{1,9},{9,1},{17,25},{25,17},{2,10},{10... | collective-permute-start | bytes 2359304 | tf_op jit(solution)/shard_map/ppermute | solution.py:76
  410.3 239.9 %reduce-scatter.13.cloned.1.call-start = ((), (), s32[]{:S(2)}) async-start(), calls=%async_computation.10 | async-start | bytes 1769472
  522.0 34.8 %collective-permute-start.24 = (bf16[384,1024]{1,0:T(8,128)(2,1)S(1)}, bf16[384,1024]{1,0:T(8,128)(2,1)S(1)}, u32[]{:S(2)}, u32[]{:S(2)}) collective-permute-start(bf16[384,1024]{1,0:T(8,128)(2,1)S(1)} %fusion.43), channel_id=1, source_target_pairs={{0,16},{8,24},{16,0},{24,8},{1,17},{9,25},{17,1},{25,9},{2,18},{10... | collective-permute-start | bytes 2359304 | tf_op jit(solution)/shard_map/ppermute | solution.py:76
  562.0 25.0 %collective-permute-start.37 = (bf16[384,1024]{1,0:T(8,128)(2,1)}, bf16[384,1024]{1,0:T(8,128)(2,1)}, u32[]{:S(2)}, u32[]{:S(2)}) collective-permute-start(bf16[384,1024]{1,0:T(8,128)(2,1)} %get-tuple-element.196), channel_id=1, source_target_pairs={{0,8},{8,0},{16,24},{24,16},{1,9},{9,1},{17,25},{25,17},{2,10},{10... | collective-permute-start | bytes 2359304 | tf_op jit(solution)/shard_map/ppermute | solution.py:76
  587.0 234.0 %reduce-scatter.11.cloned.1.call-start = ((), (), s32[]{:S(2)}) async-start(), calls=%async_computation.9 | async-start | bytes 7962624 | tf_op jit(solution)/shard_map/reduce_scatter | solution.py:485
  617.5 33.8 %collective-permute-start.40 = (bf16[384,1024]{1,0:T(8,128)(2,1)}, bf16[384,1024]{1,0:T(8,128)(2,1)}, u32[]{:S(2)}, u32[]{:S(2)}) collective-permute-start(bf16[384,1024]{1,0:T(8,128)(2,1)} %get-tuple-element.224), channel_id=1, source_target_pairs={{0,8},{8,0},{16,24},{24,16},{1,9},{9,1},{17,25},{25,17},{2,10},{10... | collective-permute-start | bytes 2359304 | tf_op jit(solution)/shard_map/ppermute | solution.py:76
  621.7 29.7 %collective-permute-start.42 = (bf16[384,1024]{1,0:T(8,128)(2,1)}, bf16[384,1024]{1,0:T(8,128)(2,1)}, u32[]{:S(2)}, u32[]{:S(2)}) collective-permute-start(bf16[384,1024]{1,0:T(8,128)(2,1)} %fusion.37), channel_id=1, source_target_pairs={{0,16},{8,24},{16,0},{24,8},{1,17},{9,25},{17,1},{25,9},{2,18},{10... | collective-permute-start | bytes 2359304 | tf_op jit(solution)/shard_map/ppermute | solution.py:76
  689.2 236.3 %reduce-scatter.15.cloned.1.call-start = ((), (), s32[]{:S(2)}) async-start(), calls=%async_computation.11 | async-start | bytes 2654208
  689.3 22.4 %collective-permute-start.58 = (bf16[128,3456]{1,0:T(8,128)(2,1)}, bf16[128,3456]{1,0:T(8,128)(2,1)}, u32[]{:S(2)}, u32[]{:S(2)}) collective-permute-start(bf16[128,3456]{1,0:T(8,128)(2,1)} %reduce-scatter.9.cloned.1.call-done), channel_id=1, source_target_pairs={{0,16},{8,24},{16,0},{24,8},{1,17},{9,25},{17,1},{25,9},{2,18},{10... | collective-permute-start | bytes 2654216 | tf_op jit(solution)/shard_map/ppermute | solution.py:76
  690.8 24.5 %collective-permute-start.57 = (bf16[128,3456]{1,0:T(8,128)(2,1)}, bf16[128,3456]{1,0:T(8,128)(2,1)}, u32[]{:S(2)}, u32[]{:S(2)}) collective-permute-start(bf16[128,3456]{1,0:T(8,128)(2,1)} %reduce-scatter.9.cloned.1.call-done), channel_id=1, source_target_pairs={{0,8},{8,0},{16,24},{24,16},{1,9},{9,1},{17,25},{25,17},{2,10},{10... | collective-permute-start | bytes 2654216 | tf_op jit(solution)/shard_map/ppermute | solution.py:76
  746.1 22.0 %collective-permute-start.48 = (bf16[384,1024]{1,0:T(8,128)(2,1)}, bf16[384,1024]{1,0:T(8,128)(2,1)S(1)}, u32[]{:S(2)}, u32[]{:S(2)}) collective-permute-start(bf16[384,1024]{1,0:T(8,128)(2,1)} %fusion.35), channel_id=1, source_target_pairs={{0,16},{8,24},{16,0},{24,8},{1,17},{9,25},{17,1},{25,9},{2,18},{10... | collective-permute-start | bytes 2359304 | tf_op jit(solution)/shard_map/ppermute | solution.py:76
  823.4 25.0 %collective-permute-start.55 = (bf16[128,4224]{1,0:T(8,128)(2,1)}, bf16[128,4224]{1,0:T(8,128)(2,1)}, u32[]{:S(2)}, u32[]{:S(2)}) collective-permute-start(bf16[128,4224]{1,0:T(8,128)(2,1)} %pad_maximum_fusion.21), channel_id=1, source_target_pairs={{0,16},{8,24},{16,0},{24,8},{1,17},{9,25},{17,1},{25,9},{2,18},{10... | collective-permute-start | bytes 3244040 | tf_op jit(solution)/shard_map/ppermute | solution.py:76
  829.5 26.5 %collective-permute-start.54 = (bf16[128,4224]{1,0:T(8,128)(2,1)}, bf16[128,4224]{1,0:T(8,128)(2,1)}, u32[]{:S(2)}, u32[]{:S(2)}) collective-permute-start(bf16[128,4224]{1,0:T(8,128)(2,1)} %pad_maximum_fusion.21), channel_id=1, source_target_pairs={{0,8},{8,0},{16,24},{24,16},{1,9},{9,1},{17,25},{25,17},{2,10},{10... | collective-permute-start | bytes 3244040 | tf_op jit(solution)/shard_map/ppermute | solution.py:76
  (141 other events, 2187.4 us)
Sparse Core Ops, SparseCore 0:
  13.2 65.8 all-gather.4
  81.9 106.9 all-gather.6
  191.6 42.3 all-gather.8
  236.7 107.5 all-gather.10
  410.5 127.3 reduce-scatter.8
  587.2 63.0 reduce-scatter.12
  689.3 131.6 reduce-scatter.10
  856.2 69.2 reduce-scatter.14

commit v2 on v1

--- a/solution.py
+++ b/solution.py
@@ -12,7 +12,7 @@
 BF16 = jnp.bfloat16
 TILE = 256
 LANES = 128
-VMEM_LIMIT = 56 << 20
+VMEM_LIMIT = 48 << 20
 
 
 def left_dot(left, right):
@@ -76,24 +76,44 @@
     return lax.ppermute(array, "seq", [(i, i ^ bit) for i in range(size)])
 
 
-def seq_gather(block):
+def tie(*values):
+    return lax.optimization_barrier(values)
+
+
+def near_blocks(block):
     have = {0: block}
-    for bit in reversed(seq_bits()):
+    for bit in reversed(seq_bits()[:-1]):
         for place in sorted(have):
             have[place | bit] = swap_seq(have[place], bit)
-    return jnp.concatenate([have[place] for place in sorted(have)], 0)
-
-
-def seq_scatter(partial):
-    size = lax.axis_size("seq")
-    length = partial.shape[0] // size
-    have = {place: partial[place * length : (place + 1) * length] for place in range(size)}
-    for bit in seq_bits():
+    return [have[place] for place in sorted(have)]
+
+
+def near_half(block):
+    return jnp.concatenate(near_blocks(block), 0)
+
+
+def far_half(block):
+    return swap_seq(block, seq_bits()[-1])
+
+
+def near_sum(half):
+    size = lax.axis_size("seq") // 2
+    length = half.shape[0] // size
+    have = {place: half[place * length : (place + 1) * length] for place in range(size)}
+    for bit in seq_bits()[:-1]:
         for place in sorted(have, reverse=True):
             if place & bit:
                 got = swap_seq(have.pop(place).astype(BF16), bit).astype(F32)
-                have[place ^ bit] = have[place ^ bit] + got
-    return have[0]
+                have[place ^ bit] = have[place ^ bit].astype(F32) + got
+    return have[0].astype(F32)
+
+
+def seq_scatter(near, far, *work):
+    sent = far_half(near_sum(far).astype(BF16))
+    kept = near_sum(near)
+    sent, kept, *work = tie(sent, kept, *work)
+    total = kept + sent.astype(F32)
+    return (total, *work) if work else total
 
 
 def flip_blocks(array):
@@ -417,6 +437,7 @@
             pltpu.VMEM((2 * pairs, full, LANES), BF16),
         ],
         compiler_params=pltpu.CompilerParams(vmem_limit_bytes=VMEM_LIMIT),
+        cost_estimate=pl.CostEstimate(flops=20_000_000_000, transcendentals=6000000, bytes_accessed=20000000),
         name="attention_forward",
     )(place, raw, cosine, sine, start, gains)
 
@@ -442,6 +463,7 @@
             pltpu.VMEM((pairs, full, LANES), F32),
         ],
         compiler_params=pltpu.CompilerParams(vmem_limit_bytes=VMEM_LIMIT),
+        cost_estimate=pl.CostEstimate(flops=20_000_000_000, transcendentals=6000000, bytes_accessed=20000000),
         name="attention_backward",
     )(place, raw, cosine, sine, start, gains, wide, totals, grads)
 
@@ -485,10 +507,52 @@
     return lax.psum_scatter(grads, "dp", scatter_dimension=0, tiled=True)
 
 
+def swap_dp(array, bit):
+    size = lax.axis_size("dp")
+    return lax.ppermute(array, "dp", [(i, i ^ bit) for i in range(size)])
+
+
+def dp_gather_small(block, later):
+    size = lax.axis_size("dp")
+    if size != 8:
+        return (dp_gather(block), later)
+    place = lax.axis_index("dp")
+    rows = block.shape[0]
+    have = {0: block}
+    for far in (2, 4, 6):
+        have[far] = swap_dp(block, far)
+    have[2], later = tie(have[2], later)
+    for far in (0, 2, 4, 6):
+        have[far ^ 1] = swap_dp(have[far], 1)
+    result = jnp.zeros((size * rows, block.shape[1]), block.dtype)
+    for turn in range(size):
+        result = lax.dynamic_update_slice_in_dim(result, have[turn], (place ^ turn) * rows, 0)
+    return (result, later)
+
+
+def dp_scatter_small(grads):
+    size = lax.axis_size("dp")
+    if size != 8:
+        return dp_scatter(grads)
+    place = lax.axis_index("dp")
+    rows = grads.shape[0] // size
+
+    def part(turn):
+        return lax.dynamic_slice_in_dim(grads, (place ^ turn) * rows, rows, 0)
+
+    sums = {}
+    for far in (4, 6, 2, 0):
+        sums[far] = part(far).astype(F32) + swap_dp(part(far ^ 1), 1).astype(F32)
+    total = sums[0]
+    for far in (4, 6, 2):
+        total = total + swap_dp(sums[far].astype(BF16), far).astype(F32)
+    return total.astype(BF16)
+
+
 def share(owned):
     size = lax.axis_size("seq")
     place = lax.axis_index("seq")
-    everywhere = seq_gather(owned).reshape((size,) + owned.shape)
+    everywhere = jnp.stack(near_blocks(owned) + near_blocks(far_half(owned)), 0)
     return [lax.dynamic_index_in_dim(everywhere, place ^ i, 0, False) for i in range(size)]
 
 
@@ -505,29 +569,152 @@
     return (results, [block[:, offset:] for block in blocks])
 
 
-def ffn_gate(normed, weights):
-    hidden = weights.shape[1] // 3
-    both = plain_dot(normed, weights[:, : 2 * hidden])
-    gate = both[:, :hidden]
-    upper = both[:, hidden:]
+def gate_terms(normed, w_gate, w_up):
+    gate = plain_dot(normed, w_gate)
+    upper = plain_dot(normed, w_up)
     sigma = jax.nn.sigmoid(gate)
-    act = (gate * sigma * upper).astype(BF16)
-    return (gate, upper, act)
-
-
-def ffn_back(grad_all, kept, normed_all, weights):
-    gate, upper, act = kept
-    hidden = weights.shape[1] // 3
-    sigma = jax.nn.sigmoid(gate)
-    d_down = left_dot(grad_all, act)
-    d_act = plain_dot(grad_all, weights[:, 2 * hidden :])
-    d_gate = (d_act * upper * sigma * (1.0 + gate * (1.0 - sigma))).astype(BF16)
-    d_up = (d_act * gate * sigma).astype(BF16)
-    d_both = jnp.concatenate([d_gate, d_up], 1)
-    d_gate_up = left_dot(normed_all, d_both)
-    partial = right_dot(d_both, weights[:, : 2 * hidden])
-    grads = jnp.concatenate([d_gate_up.astype(BF16), d_down.astype(BF16)], 1)
-    return (seq_scatter(partial), grads)
+    swish = gate * sigma
+    return (upper * (sigma + swish * (1.0 - sigma)), swish, swish * upper)
+
+
+def ffn_forward_kernel(normed_ref, gate_ref, up_ref, down_ref, *rest):
+    kept_ref, partial_ref = rest[-2:]
+    hidden = gate_ref.shape[1]
+    slope, swish, act = gate_terms(normed_ref[...], gate_ref[...], up_ref[...])
+    act = act.astype(BF16)
+    kept_ref[:, :hidden] = slope.astype(BF16)
+    kept_ref[:, hidden : 2 * hidden] = swish.astype(BF16)
+    kept_ref[:, 2 * hidden :] = act
+    partial_ref[...] = right_dot(act, down_ref[...]).astype(BF16)
+
+
+def ffn_turn_kernel(normed_ref, grad_ref, gate_ref, up_ref, down_ref, *rest):
+    kept_ref, partial_ref = rest[-2:]
+    hidden = gate_ref.shape[1]
+    slope, swish, act = gate_terms(normed_ref[...], gate_ref[...], up_ref[...])
+    d_act = plain_dot(grad_ref[...], down_ref[...])
+    d_gate = (d_act * slope).astype(BF16)
+    d_up = (d_act * swish).astype(BF16)
+    kept_ref[:, :hidden] = d_gate
+    kept_ref[:, hidden : 2 * hidden] = d_up
+    kept_ref[:, 2 * hidden :] = act.astype(BF16)
+    partial = right_dot(d_gate, gate_ref[...]) + right_dot(d_up, up_ref[...])
+    partial_ref[...] = partial.astype(BF16)
+
+
+def ffn_backward_kernel(grad_ref, terms_ref, gate_ref, up_ref, down_ref, *rest):
+    kept_ref, partial_ref = rest[-2:]
+    hidden = gate_ref.shape[1]
+    d_act = plain_dot(grad_ref[...], down_ref[...])
+    d_gate = (d_act * terms_ref[:, :hidden].astype(F32)).astype(BF16)
+    d_up = (d_act * terms_ref[:, hidden:].astype(F32)).astype(BF16)
+    kept_ref[:, :hidden] = d_gate
+    kept_ref[:, hidden:] = d_up
+    partial = right_dot(d_gate, gate_ref[...]) + right_dot(d_up, up_ref[...])
+    partial_ref[...] = partial.astype(BF16)
+
+
+def ffn_call(kernel, name, tokens, terms, weights, hidden, length, first, full, kept_width, kept):
+    width = weights.shape[0]
+    count = tokens[0].shape[0] // length
+    in_specs = [pl.BlockSpec((length, width), lambda i: (i, 0)) for _ in tokens]
+    operands = list(tokens)
+    if terms is not None:
+        in_specs.append(pl.BlockSpec((length, 2 * hidden), lambda i: (i + first, 0)))
+        operands.append(terms)
+    for place in range(3):
+        in_specs.append(
+            pl.BlockSpec(
+                (width, hidden), lambda i, place=place: (0, place), pipeline_mode=pl.Buffered(1)
+            )
+        )
+        operands.append(weights)
+    aliases = {}
+    if kept is not None:
+        aliases = {len(operands): 0}
+        in_specs.append(pl.BlockSpec(memory_space=pl.ANY))
+        operands.append(kept)
+    return pl.pallas_call(
+        kernel,
+        grid=(count,),
+        in_specs=in_specs,
+        out_specs=(
+            pl.BlockSpec((length, kept_width), lambda i: (i + first, 0)),
+            pl.BlockSpec((length, width), lambda i: (i, 0)),
+        ),
+        out_shape=(
+            jax.ShapeDtypeStruct((full, kept_width), BF16),
+            jax.ShapeDtypeStruct((count * length, width), BF16),
+        ),
+        input_output_aliases=aliases,
+        compiler_params=pltpu.CompilerParams(vmem_limit_bytes=VMEM_LIMIT),
+        cost_estimate=pl.CostEstimate(flops=6_000_000_000, transcendentals=1000000, bytes_accessed=20000000),
+        name=name,
+    )(*operands)
+
+
+def split_weights(weights, hidden):
+    return [weights[:, n * hidden : (n + 1) * hidden] for n in range(3)]
+
+
+def halves_of(array):
+    half = array.shape[0] // 2
+    return (array[:half], array[half:])
+
+
+def first_block(number, full, length):
+    return number * (full // length // 2)
+
+
+def place_rows(kept, part, number):
+    if kept is None:
+        kept = jnp.zeros((2 * part.shape[0], part.shape[1]), part.dtype)
+    return lax.dynamic_update_slice_in_dim(kept, part, number * part.shape[0], 0)
+
+
+def ffn_forward(normed, weights, hidden, length, number, kept):
+    full = 2 * normed.shape[0]
+    if hidden % LANES:
+        w_gate, w_up, w_down = split_weights(weights, hidden)
+        terms = jnp.concatenate(gate_terms(normed, w_gate, w_up), 1).astype(BF16)
+        partial = right_dot(terms[:, 2 * hidden :], w_down).astype(BF16)
+        return (place_rows(kept, terms, number), partial)
+    return ffn_call(
+        ffn_forward_kernel, "ffn_forward", [normed], None, weights, hidden, length,
+        first_block(number, full, length), full, 3 * hidden, kept,
+    )
+
+
+def ffn_turn(normed, grads, weights, hidden, length, number, kept):
+    full = 2 * normed.shape[0]
+    if hidden % LANES:
+        w_gate, w_up, w_down = split_weights(weights, hidden)
+        slope, swish, act = gate_terms(normed, w_gate, w_up)
+        d_act = plain_dot(grads, w_down)
+        part = jnp.concatenate([d_act * slope, d_act * swish, act], 1).astype(BF16)
+        partial = right_dot(part[:, : 2 * hidden], weights[:, : 2 * hidden]).astype(BF16)
+        return (place_rows(kept, part, number), partial)
+    return ffn_call(
+        ffn_turn_kernel, "ffn_turn", [normed, grads], None, weights, hidden, length,
+        first_block(number, full, length), full, 3 * hidden, kept,
+    )
+
+
+def ffn_backward(grads, terms, weights, hidden, length, number, kept):
+    full = 2 * grads.shape[0]
+    if hidden % LANES:
+        w_gate, w_up, w_down = split_weights(weights, hidden)
+        rows = slice(number * grads.shape[0], (number + 1) * grads.shape[0])
+        d_act = plain_dot(grads, w_down)
+        slope = terms[rows, :hidden].astype(F32)
+        swish = terms[rows, hidden : 2 * hidden].astype(F32)
+        part = jnp.concatenate([d_act * slope, d_act * swish], 1).astype(BF16)
+        partial = right_dot(part, weights[:, : 2 * hidden]).astype(BF16)
+        return (place_rows(kept, part, number), partial)
+    return ffn_call(
+        ffn_backward_kernel, "ffn_backward", [grads], terms, weights, hidden, length,
+        first_block(number, full, length), full, 2 * hidden, kept,
+    )
 
 
 def local(
@@ -567,7 +754,10 @@
     taps = conv_w.shape[0]
     reach = taps - 1
 
-    x_all = seq_gather(x_in.reshape(length, width)).astype(F32)
+    x_far = far_half(x_in.reshape(length, width))
+    cotangent_low, x_far = tie(cotangent.reshape(length, width), x_far)
+    x_all = jnp.concatenate([near_half(x_in.reshape(length, width)), near_half(x_far)], 0)
+    cotangent_halves = [near_half(cotangent_low), near_half(far_half(cotangent_low))]
     head_gains = jnp.pad(jnp.stack([g_q, g_k], 1), ((0, slots - head // dp_count), (0, 0)))
     small = jnp.concatenate(
         [conv_w.T, jnp.stack([g_mix1, g_ffn1, g_attn2, g_ffn2], 1), head_gains], 1
@@ -576,21 +766,25 @@
     dealt = deal_rows(jnp.stack([w_out, w_o], 1))
     out_piece = dealt[:, 0].reshape(slots, -1)
     o_piece = dealt[:, 1].reshape(slots, -1)
-    mix_all = dp_gather(jnp.concatenate([column_block(w_in, 3), small, out_piece], 1))
-    ffn_one = dp_gather(
-        jnp.concatenate([column_block(w, 1) for w in (w_gate1, w_up1, w_down1)], 1)
-    )
-    attn_all = dp_gather(
-        jnp.concatenate(
-            [
-                column_block(w_q, 1),
-                column_block(key_projection_weight, 1),
-                column_block(value_projection_weight, 1),
-                o_piece,
-            ],
-            1,
-        )
-    )
+    ffn_columns = 3 * w_gate1.shape[1] // seq_count
+    both = jnp.concatenate(
+        [column_block(w, 1) for w in (w_gate1, w_up1, w_down1)]
+        + [
+            column_block(w_q, 1),
+            column_block(key_projection_weight, 1),
+            column_block(value_projection_weight, 1),
+            o_piece,
+        ],
+        1,
+    )
+    mix_all, both = dp_gather_small(
+        jnp.concatenate([column_block(w_in, 3), small, out_piece], 1), both
+    )
+    both = dp_gather(both)
+    mix_all, *cotangent_halves = tie(mix_all, *cotangent_halves)
+    ffn_one = both
+    hidden = ffn_columns // 3
+    attn_all = both[:, ffn_columns:]
     ffn_two = dp_gather(
         jnp.concatenate([column_block(w, 1) for w in (w_gate2, w_up2, w_down2)], 1)
     )
@@ -622,7 +816,7 @@
 
     x_flat = x_in.reshape(length, width).astype(F32)
     unit_one, scale_one = unit_scale(x_flat)
-    normed_one = (unit_scale(x_all)[0] * gain_mix).astype(BF16)
+    normed_one = (unit_scale(x_all.astype(F32))[0] * gain_mix).astype(BF16)
     projected = plain_dot(normed_one, in_block).reshape(seq_count, length, 3 * channels)
     part_b = projected[..., :channels]
     part_c = projected[..., channels : 2 * channels]
@@ -638,61 +832,93 @@
             + kernel[tap] * extended[:, reach - tap : reach - tap + length] * masks[tap - 1]
         )
     gated = (part_c * conv_out).astype(BF16).reshape(full, channels)
-    hidden_one = x_flat + seq_scatter(plain_dot(gated, out_block))
+    hidden_one = x_flat + seq_scatter(*halves_of(plain_dot(gated, out_block)))
 
     unit_two, scale_two = unit_scale(hidden_one)
-    normed_two = seq_gather((unit_two * gain_ffn_one).astype(BF16))
-    keep_one = ffn_gate(normed_two, ffn_one)
-    hidden = ffn_one.shape[1] // 3
-    hidden_two = hidden_one + seq_scatter(right_dot(keep_one[2], ffn_one[:, 2 * hidden :]))
+    near_two = (unit_two * gain_ffn_one).astype(BF16)
+    far_two = far_half(near_two)
+    near_two = near_half(near_two)
+    terms_one, near_out = ffn_forward(near_two, ffn_one, hidden, length, 0, None)
+    far_two, near_out = tie(far_two, near_out)
+    far_two = near_half(far_two)
+    terms_one, far_out = ffn_forward(far_two, ffn_one, hidden, length, 1, terms_one)
+    hidden_two = hidden_one + seq_scatter(near_out, far_out)
 
     unit_three, scale_three = unit_scale(hidden_two)
-    normed_three = seq_gather((unit_three * gain_attn).astype(BF16))
+    normed_three = (unit_three * gain_attn).astype(BF16)
+    normed_three = jnp.concatenate(
+        [near_half(normed_three), near_half(far_half(normed_three))], 0
+    )
     raw = plain_dot(normed_three, qkv_block)
     kv_width = (qkv_width - channels) // 2
     attended_low, wide, totals = attention_forward(
         place, raw, cosine, sine, starts, head_gains, length
     )
-    hidden_three = hidden_two + seq_scatter(plain_dot(attended_low, o_block))
+    hidden_three = hidden_two + seq_scatter(*halves_of(plain_dot(attended_low, o_block)))
 
     unit_four, scale_four = unit_scale(hidden_three)
-    normed_four = seq_gather((unit_four * gain_ffn_two).astype(BF16))
-    keep_two = ffn_gate(normed_four, ffn_two)
-    hidden_four = hidden_three + seq_scatter(right_dot(keep_two[2], ffn_two[:, 2 * hidden :]))
-    out = hidden_four.astype(BF16).reshape(rows, length, width)
-
-    cotangent_all = seq_gather(cotangent.reshape(length, width))
+    near_four = (unit_four * gain_ffn_two).astype(BF16)
+    far_four = far_half(near_four)
+    near_four = near_half(near_four)
+    kept_two, near_out = ffn_turn(near_four, cotangent_halves[0], ffn_two, hidden, length, 0, None)
+    far_four, near_out = tie(far_four, near_out)
+    far_four = near_half(far_four)
+    kept_two, far_out = ffn_turn(far_four, cotangent_halves[1], ffn_two, hidden, length, 1, kept_two)
+
     grad_four = cotangent.reshape(length, width).astype(F32)
-    d_ffn_in, grads_two = ffn_back(cotangent_all, keep_two, normed_four, ffn_two)
-    owned_two = dp_scatter(grads_two)
+    kept_two, far_out = tie(kept_two, far_out)
+    normed_four = jnp.concatenate([near_four, far_four], 0)
+    d_gate_up = left_dot(normed_four, kept_two[:, : 2 * hidden]).astype(BF16)
+    d_ffn_in, d_gate_up = seq_scatter(near_out, far_out, d_gate_up)
     d_hidden, d_gain_ffn_two = norm_back(d_ffn_in, gain_ffn_two, unit_four, scale_four)
     grad_three = grad_four + d_hidden
 
-    grad_attn = seq_gather(grad_three.astype(BF16))
+    grad_attn = grad_three.astype(BF16)
+    far_attn = far_half(grad_attn)
+    d_down = left_dot(jnp.concatenate(cotangent_halves, 0), kept_two[:, 2 * hidden :])
+    grads_two = jnp.concatenate([d_gate_up, d_down.astype(BF16)], 1)
+    far_attn, grads_two = tie(far_attn, grads_two)
+    owned_two = dp_scatter(grads_two)
+    grad_attn = jnp.concatenate([near_half(grad_attn), near_half(far_attn)], 0)
     d_w_o = left_dot(attended_low, grad_attn)
     d_attended = right_dot(grad_attn, o_block).astype(BF16)
     d_raw, d_head_gains = attention_backward(
         place, raw, cosine, sine, starts, head_gains, wide, totals, d_attended, length
     )
     d_head_gains = d_head_gains[:, :head] + d_head_gains[:, head:]
+    partial_attn = right_dot(d_raw, qkv_block)
+    d_raw, partial_attn = tie(d_raw, partial_attn)
     d_qkv = left_dot(normed_three, d_raw)
-    d_attn_in = seq_scatter(right_dot(d_raw, qkv_block))
     grads_attn = jnp.concatenate(
         [d_qkv.astype(BF16), d_w_o.astype(BF16).reshape(width, channels)], 1
     )
-    owned_attn = dp_scatter(grads_attn)
+    d_attn_in, grads_attn = seq_scatter(*halves_of(partial_attn), grads_attn)
     d_attn_h, d_gain_attn = norm_back(d_attn_in, gain_attn, unit_three, scale_three)
     grad_two = grad_three + d_attn_h
 
-    grad_two_all = seq_gather(grad_two.astype(BF16))
-    grad_two_all, owned_two = lax.optimization_barrier((grad_two_all, owned_two))
-    d_ffn_in_one, grads_one = ffn_back(grad_two_all, keep_one, normed_two, ffn_one)
+    owned_attn = dp_scatter_small(grads_attn)
+    near_grad = grad_two.astype(BF16)
+    far_grad = far_half(near_grad)
+    near_grad = near_half(near_grad)
+    kept_one, near_out = ffn_backward(near_grad, terms_one, ffn_one, hidden, length, 0, None)
+    far_grad, near_out = tie(far_grad, near_out)
+    far_grad = near_half(far_grad)
+    kept_one, far_out = ffn_backward(far_grad, terms_one, ffn_one, hidden, length, 1, kept_one)
+    kept_one, far_out = tie(kept_one, far_out)
+    d_gate_up = left_dot(jnp.concatenate([near_two, far_two], 0), kept_one).astype(BF16)
+    d_ffn_in_one, d_gate_up, owned_attn = seq_scatter(near_out, far_out, d_gate_up, owned_attn)
     d_hidden_one, d_gain_ffn_one = norm_back(d_ffn_in_one, gain_ffn_one, unit_two, scale_two)
     grad_one = grad_two + d_hidden_one
 
-    grad_mix = seq_gather(grad_one.astype(BF16))
-    grad_mix, owned_attn, grads_one = lax.optimization_barrier((grad_mix, owned_attn, grads_one))
+    grad_mix = grad_one.astype(BF16)
+    far_mix = far_half(grad_mix)
+    d_down = left_dot(
+        jnp.concatenate([near_grad, far_grad], 0), terms_one[:, 2 * hidden :]
+    ).astype(BF16)
+    far_mix, grads_one = tie(far_mix, jnp.concatenate([d_gate_up, d_down], 1))
     owned_one = dp_scatter(grads_one)
+    grad_mix = jnp.concatenate([near_half(grad_mix), near_half(far_mix)], 0)
+    grad_mix, owned_two = tie(grad_mix, owned_two)
     d_w_out = left_dot(gated, grad_mix)
     d_gated = right_dot(grad_mix, out_block).reshape(seq_count, length, channels)
     d_part_c = d_gated * conv_out
@@ -711,8 +937,12 @@
     d_product = lax.optimization_barrier(d_product_sum.astype(BF16)).astype(F32)
     d_projected = jnp.concatenate([d_product * part_x, d_part_c, d_product * part_b], -1)
     d_projected = d_projected.astype(BF16).reshape(full, 3 * channels)
+    kept_two, d_projected = tie(kept_two, d_projected)
+    ffn_out = right_dot(kept_two[:, 2 * hidden :], ffn_two[:, 2 * hidden :])
+    hidden_four = hidden_three + seq_scatter(*halves_of(ffn_out))
+    out = hidden_four.astype(BF16).reshape(rows, length, width)
     d_w_in = left_dot(normed_one, d_projected)
-    d_normed = seq_scatter(right_dot(d_projected, in_block))
+    d_normed = seq_scatter(*halves_of(right_dot(d_projected, in_block)))
     d_x_part, d_gain_mix = norm_back(d_normed, gain_mix, unit_one, scale_one)
     d_x = (grad_one + d_x_part).reshape(rows, length, width)
 
@@ -740,21 +970,27 @@
         ],
         1,
     )
-    grads_mix, owned_one = lax.optimization_barrier((grads_mix, owned_one))
-    owned_mix = dp_scatter(grads_mix)
+    owned_mix = dp_scatter_small(grads_mix)
 
     def redeal(owned):
         block = owned[:, owned.shape[1] - channels :].reshape(-1, width)
         back = undeal_rows(block).reshape(slots, channels)
         return jnp.concatenate([owned[:, : owned.shape[1] - channels], back], 1)
 
+    attn_cut = owned_attn.shape[1]
+    shared_small = share(jnp.concatenate([redeal(owned_attn), redeal(owned_mix)], 1))
+    (d_w_q, d_w_k, d_w_v), _ = split_columns(
+        shared_small, [(1, channels), (1, kv_width), (1, kv_width)]
+    )
+    (d_w_in_full,), rest_mix = split_columns(
+        [b[:, attn_cut:] for b in shared_small], [(3, channels)]
+    )
+    rest_attn = [b[:, attn_cut - channels : attn_cut] for b in shared_small]
     (d_wgate_two, d_wup_two, d_down_two), _ = split_columns(share(owned_two), [(1, hidden)] * 3)
-    shared_one = share(jnp.concatenate([owned_one, redeal(owned_attn)], 1))
-    one, rest_attn = split_columns(
-        shared_one, [(1, hidden)] * 3 + [(1, channels), (1, kv_width), (1, kv_width)]
-    )
-    d_wgate_one, d_wup_one, d_down_one, d_w_q, d_w_k, d_w_v = one
-    (d_w_in_full,), rest_mix = split_columns(share(redeal(owned_mix)), [(3, channels)])
+    owned_one, d_wgate_two, d_wup_two, d_down_two, out = tie(
+        owned_one, d_wgate_two, d_wup_two, d_down_two, out
+    )
+    (d_wgate_one, d_wup_one, d_down_one), _ = split_columns(share(owned_one), [(1, hidden)] * 3)
     d_w_o_full = jnp.concatenate([b.reshape(-1, width) for b in rest_attn], 0).astype(F32)
     d_w_out_full = jnp.concatenate([b[:, 128:].reshape(-1, width) for b in rest_mix], 0)
     d_w_out_full = d_w_out_full.astype(F32)

time: 967 us -> 817 us (0.84)
  waiting for transfers between devices: 511 us -> 307 us
  matrix products: 171 us -> 86.5 us
  Pallas kernels: 62.2 us -> 130 us
  starting transfers between devices: 54.8 us -> 97.1 us
  local copies, waits for them, and re-layouts: 41.2 us -> 69.6 us
    ppermute x57, waiting for transfers between devices: 303 us -> 188 us  [swap_seq(): return lax.ppermute(array, 'seq', [(i, i ^ bit) for i in range(size)])]
    ppermute x0 -> x21, waiting for transfers between devices: none -> 96.7 us  [swap_dp(): return lax.ppermute(array, 'dp', [(i, i ^ bit) for i in range(size)])]
    unnamed x10 -> x4, waiting for transfers between devices: 85.7 us -> 0.07 us
    pallas_call x0 -> x6, Pallas kernels: none -> 71.6 us  [ffn_call(): pl.pallas_call(kernel, grid=(count,), in_specs=in_specs, out_specs=(pl.Bl...]
    dot_general x8 -> x4, matrix products: 67.9 us -> 12 us  [plain_dot(): return jnp.dot(left, right, preferred_element_type=F32)]
    all_gather x4 -> x2, waiting for transfers between devices: 74.3 us -> 22.5 us  [dp_gather(): return lax.all_gather(block, 'dp', axis=0, tiled=True)]
    reduce_scatter x2, waiting for transfers between devices: 48 us -> 0.02 us  [dp_scatter(): return lax.psum_scatter(grads, 'dp', scatter_dimension=0, tiled=True)]
    ppermute x0 -> x21, starting transfers between devices: none -> 31.4 us  [swap_dp(): return lax.ppermute(array, 'dp', [(i, i ^ bit) for i in range(size)])]
  transfers between devices with their start and end apart: 68 -> 85, of which waited for: 30 -> 43; matrix products, arithmetic and copies ran while one was open for 26% -> 27% of each run, Pallas kernels for 6% -> 14%
where the time goes in v2:
time: 817 us; the launch traced here: 802 us
  waiting for transfers between devices  307 us (38%)
  Pallas kernels  130 us (16%)
  starting transfers between devices  97.1 us (12%)
  other arithmetic  96.2 us (12%)
  matrix products  86.5 us (11%)
  local copies, waits for them, and re-layouts  69.6 us (9%)
  between operations  16.2 us (2%)
    ppermute x57, waiting for transfers between devices, swap_seq(): return lax.ppermute(array, 'seq', [(i, i ^ bit) for i in range(size)])  188 us
    ppermute x21, waiting for transfers between devices, swap_dp(): return lax.ppermute(array, 'dp', [(i, i ^ bit) for i in range(size)])  96.7 us
    pallas_call x6, Pallas kernels, ffn_call(): pl.pallas_call(kernel, grid=(count,), in_specs=in_specs, out_specs=(pl.Bl...  71.6 us
    ppermute x57, starting transfers between devices, swap_seq(): return lax.ppermute(array, 'seq', [(i, i ^ bit) for i in range(size)])  61.6 us
    dot_general x8, matrix products, left_dot(): lax.dot_general(left, right, (((0,), (0,)), ((), ())), preferred_element_...  52.6 us
    pallas_call x1, Pallas kernels, attention_backward(): pl.pallas_call(lambda *refs: attention_backward_kernel(*refs, length=leng...  34.2 us
    ppermute x21, starting transfers between devices, swap_dp(): return lax.ppermute(array, 'dp', [(i, i ^ bit) for i in range(size)])  31.4 us
    unnamed x238, local copies, waits for them, and re-layouts  26 us
  transfers between devices with their start and end apart: 85, of which 43 were waited for; matrix products, arithmetic and copies ran while one was open for 27% of the time, Pallas kernels for 14%

profile of v2, /device:TPU:0, one launch (start us, length us, event | category | flops | bytes accessed | tf_op | source)
XLA Modules:
  0.0 802.4 jit_solution(17150909280773958498)
XLA Ops:
  50.5 27.6 %collective-permute-done.7 = bf16[128,1152]{0,1:T(8,128)(2,1)S(1)} collective-permute-done((bf16[128,1152]{0,1:T(8,128)(2,1)}, bf16[128,1152]{0,1:T(8,128)(2,1)S(1)}, u32[]{:S(2)}, u32[]{:S(2)}) %collective-permute-start.7) | collective-permute-done | bytes 294944 | tf_op jit(solution)/shard_map/ppermute | solution.py:512
  89.4 12.0 %collective-permute-done.12 = bf16[384,1024]{1,0:T(8,128)(2,1)S(1)} collective-permute-done((bf16[384,1024]{1,0:T(8,128)(2,1)S(1)}, bf16[384,1024]{1,0:T(8,128)(2,1)S(1)}, u32[]{:S(2)}, u32[]{:S(2)}) %collective-permute-start.12) | collective-permute-done | bytes 786464 | tf_op jit(solution)/shard_map/ppermute | solution.py:76
  134.3 19.3 %collective-permute-done.15 = bf16[384,1024]{1,0:T(8,128)(2,1)S(1)} collective-permute-done((bf16[384,1024]{1,0:T(8,128)(2,1)S(1)}, bf16[384,1024]{1,0:T(8,128)(2,1)S(1)}, u32[]{:S(2)}, u32[]{:S(2)}) %collective-permute-start.15) | collective-permute-done | bytes 786464 | tf_op jit(solution)/shard_map/ppermute | solution.py:76
  160.9 22.5 %all-gather.3.cloned.1.call-done.gate_ref.up_ref.down_ref = bf16[1024,4224]{1,0:T(8,128)(2,1)} async-done(((bf16[128,4224]{1,0:T(8,128)(2,1)}), bf16[1024,4224]{1,0:T(8,128)(2,1)}) %all-gather.3.cloned.1.call-update) | async-done | bytes 8650768 | tf_op jit(solution)/shard_map/all_gather | solution.py:503
  184.8 10.7 %ffn_forward.2 = (bf16[1536,3456]{1,0:T(8,128)(2,1)}, bf16[768,1024]{1,0:T(8,128)(2,1)S(1)}) custom-call(bf16[768,1024]{1,0:T(8,128)(2,1)S(1)} %copy-done.4, bf16[1024,4224]{1,0:T(8,128)(2,1)} %all-gather.3.cloned.1.call-done.gate_ref.up_ref.down_ref, bf16[1024,4224]{1,0:T(8,128)(2,1)} %all-gather.3.cloned.1.call-done.gate_ref.up_ref.down_ref, ...), custom_call_target="tpu_custom_call" | custom-call | flops 6000000000 | bytes 20000000 | tf_op jit(solution)/shard_map/ffn_forward/pallas_call | solution.py:637
  200.7 11.1 %ffn_forward.3 = (bf16[1536,3456]{1,0:T(8,128)(2,1)}, bf16[768,1024]{1,0:T(8,128)(2,1)S(1)}) custom-call(bf16[768,1024]{1,0:T(8,128)(2,1)S(1)} %pad_maximum_fusion.13.normed_ref, bf16[1024,4224]{1,0:T(8,128)(2,1)} %all-gather.3.cloned.1.call-done.gate_ref.up_ref.down_ref, ...), custom_call_target="tpu_custom_call", output_to_operand_aliasing={{0}: (4, {})} | custom-call | flops 6000000000 | bytes 20000000 | tf_op jit(solution)/shard_map/ffn_forward/pallas_call | solution.py:637
  216.2 17.9 %collective-permute-done.21 = bf16[384,1024]{1,0:T(8,128)(2,1)S(1)} collective-permute-done((bf16[384,1024]{1,0:T(8,128)(2,1)S(1)}, bf16[384,1024]{1,0:T(8,128)(2,1)S(1)}, u32[]{:S(2)}, u32[]{:S(2)}) %collective-permute-start.21) | collective-permute-done | bytes 786464 | tf_op jit(solution)/shard_map/ppermute | solution.py:76
  237.3 17.6 %collective-permute-done.24 = bf16[384,1024]{1,0:T(8,128)(2,1)} collective-permute-done((bf16[384,1024]{1,0:T(8,128)(2,1)}, bf16[384,1024]{1,0:T(8,128)(2,1)}, u32[]{:S(2)}, u32[]{:S(2)}) %collective-permute-start.24) | collective-permute-done | bytes 786464 | tf_op jit(solution)/shard_map/ppermute | solution.py:76
  267.8 23.8 %attention_forward.1 = (bf16[1536,256]{1,0:T(8,128)(2,1)S(1)}, f32[256,1536]{1,0:T(8,128)S(1)}, f32[8,1536]{1,0:T(8,128)S(1)}) custom-call(s32[1]{0:T(128)} %bitcast.34.refs_0_, f32[1536,512]{1,0:T(8,128)} %fusion.66.refs_1_, f32[1536,128]{1,0:T(8,128)S(1)} %get-tuple-element.458.refs_2_, f32[1536,128]{1,0:T(8,128)S(1)} %copy-done.7, ...), custom_call_target="tpu_custom_call" | custom-call | flops 20000000000 | bytes 20000000 | tf_op jit(solution)/shard_map/attention_forward/pallas_call | solution.py:425
  298.5 18.5 %collective-permute-done.27 = bf16[384,1024]{1,0:T(8,128)(2,1)S(1)} collective-permute-done((bf16[384,1024]{1,0:T(8,128)(2,1)S(1)}, bf16[384,1024]{1,0:T(8,128)(2,1)S(1)}, u32[]{:S(2)}, u32[]{:S(2)}) %collective-permute-start.27) | collective-permute-done | bytes 786464 | tf_op jit(solution)/shard_map/ppermute | solution.py:76
  328.3 14.1 %ffn_turn.2 = (bf16[1536,3456]{1,0:T(8,128)(2,1)}, bf16[768,1024]{1,0:T(8,128)(2,1)S(1)}) custom-call(bf16[768,1024]{1,0:T(8,128)(2,1)S(1)} %copy-done.3, bf16[768,1024]{1,0:T(8,128)(2,1)S(1)} %copy-done.2, bf16[1024,3456]{1,0:T(8,128)(2,1)} %all-gather.5.cloned.1.call-done.gate_ref.up_ref.down_ref, ...), custom_call_target="tpu_custom_call" | custom-call | flops 6000000000 | bytes 20000000 | tf_op jit(solution)/shard_map/ffn_turn/pallas_call | solution.py:637
  346.2 14.1 %ffn_turn.3 = (bf16[1536,3456]{1,0:T(8,128)(2,1)}, bf16[768,1024]{1,0:T(8,128)(2,1)S(1)}) custom-call(bf16[768,1024]{1,0:T(8,128)(2,1)S(1)} %pad_maximum_fusion.15.normed_ref, bf16[768,1024]{1,0:T(8,128)(2,1)S(1)} %pad_maximum_fusion.11.grad_ref, ...), custom_call_target="tpu_custom_call", output_to_operand_aliasing={{0}: (5, {})} | custom-call | flops 6000000000 | bytes 20000000 | tf_op jit(solution)/shard_map/ffn_turn/pallas_call | solution.py:637
  364.4 12.7 %fusion.5 = bf16[1024,2304]{1,0:T(8,128)(2,1)} fusion(bf16[1536,3456]{1,0:T(8,128)(2,1)} %get-tuple-element.138, bf16[384,1024]{1,0:T(8,128)(2,1)S(1)} %collective-permute-done.31, bf16[384,1024]{1,0:T(8,128)(2,1)} %collective-permute-done.29, bf16[384,1024]{1,0:T(8,128)(2,1)S(1)} %copy-done.66, bf16[384,1024]{1,0:T(8,128)(2,1)} %multiply_convert_fusion.1), kind=kOutput, calls=%fused_computation.12 | convolution fusion | flops 7262699520 | bytes 14942208 | tf_op jit(solution)/shard_map/dot_general | solution.py:19
  410.1 34.2 %attention_backward.1 = (bf16[1536,512]{1,0:T(8,128)(2,1)S(1)}, f32[2,128]{1,0:T(2,128)S(1)}) custom-call(s32[1]{0:T(128)} %bitcast.34.refs_0_, f32[1536,512]{1,0:T(8,128)} %fusion.66.refs_1_, f32[1536,128]{1,0:T(8,128)S(1)} %get-tuple-element.458.refs_2_, f32[1536,128]{1,0:T(8,128)S(1)} %copy-done.8, s32[1,1536]{1,0:T(1,128)S(1)} %broadcast_in_dim.12.refs_4_, ...), custom_call_target="tpu_custom_call" | custom-call | flops 20000000000 | bytes 20000000 | tf_op jit(solution)/shard_map/attention_backward/pallas_call | solution.py:448
  475.6 10.7 %ffn_backward.2 = (bf16[1536,2304]{1,0:T(8,128)(2,1)}, bf16[768,1024]{1,0:T(8,128)(2,1)S(1)}) custom-call(bf16[768,1024]{1,0:T(8,128)(2,1)S(1)} %pad_maximum_fusion.17.grad_ref, bf16[1536,3456]{1,0:T(8,128)(2,1)} %get-tuple-element.122.terms_ref, bf16[1024,4224]{1,0:T(8,128)(2,1)} %all-gather.3.cloned.1.call-done.gate_ref.up_ref.down_ref, ...), custom_call_target="tpu_custom_call" | custom-call | flops 6000000000 | bytes 20000000 | tf_op jit(solution)/shard_map/ffn_backward/pallas_call | solution.py:637
  496.5 11.0 %ffn_backward.3 = (bf16[1536,2304]{1,0:T(8,128)(2,1)}, bf16[768,1024]{1,0:T(8,128)(2,1)S(1)}) custom-call(bf16[768,1024]{1,0:T(8,128)(2,1)S(1)} %pad_maximum_fusion.18.grad_ref, bf16[1536,3456]{1,0:T(8,128)(2,1)} %get-tuple-element.122.terms_ref, ...), custom_call_target="tpu_custom_call", output_to_operand_aliasing={{0}: (5, {})} | custom-call | flops 6000000000 | bytes 20000000 | tf_op jit(solution)/shard_map/ffn_backward/pallas_call | solution.py:637
  522.9 18.2 %collective-permute-done.49 = bf16[128,768]{0,1:T(8,128)(2,1)S(1)} collective-permute-done((bf16[128,768]{0,1:T(8,128)(2,1)S(1)}, bf16[128,768]{0,1:T(8,128)(2,1)S(1)}, u32[]{:S(2)}, u32[]{:S(2)}) %collective-permute-start.49) | collective-permute-done | bytes 196640 | tf_op jit(solution)/shard_map/ppermute | solution.py:512
  545.8 10.5 %convolution_convert_fusion = bf16[1024,2304]{1,0:T(8,128)(2,1)} fusion(bf16[1536,2304]{1,0:T(8,128)(2,1)S(1)} %copy-done.31, bf16[384,1024]{1,0:T(8,128)(2,1)S(1)} %copy-done.64, bf16[384,1024]{1,0:T(8,128)(2,1)} %collective-permute-done.17, bf16[384,1024]{1,0:T(8,128)(2,1)S(1)} %copy-done.62, bf16[384,1024]{1,0:T(8,128)(2,1)S(1)} %copy-done.41), kind=kOutput, calls=%fused_computation.11 | convolution fusion | flops 7262699520 | bytes 14942208 | tf_op jit(solution)/shard_map/dot_general | solution.py:19
  598.3 10.7 %collective-permute-start.58 = (bf16[128,3456]{1,0:T(8,128)(2,1)}, bf16[128,3456]{1,0:T(8,128)(2,1)}, u32[]{:S(2)}, u32[]{:S(2)}) collective-permute-start(bf16[128,3456]{1,0:T(8,128)(2,1)} %reduce-scatter.5.cloned.1.call-done), channel_id=1, source_target_pairs={{0,16},{8,24},{16,0},{24,8},{1,17},{9,25},{17,1},{25,9},{2,18},{10... | collective-permute-start | bytes 2654216 | tf_op jit(solution)/shard_map/ppermute | solution.py:76
  660.1 11.0 %collective-permute-done.61 = bf16[384,1024]{1,0:T(8,128)(2,1)} collective-permute-done((bf16[384,1024]{1,0:T(8,128)(2,1)}, bf16[384,1024]{1,0:T(8,128)(2,1)}, u32[]{:S(2)}, u32[]{:S(2)}) %collective-permute-start.61) | collective-permute-done | bytes 786464 | tf_op jit(solution)/shard_map/ppermute | solution.py:76
  683.2 11.6 %collective-permute-done.72 = bf16[128,1152]{0,1:T(8,128)(2,1)S(1)} collective-permute-done((bf16[128,1152]{0,1:T(8,128)(2,1)S(1)}, bf16[128,1152]{0,1:T(8,128)(2,1)S(1)}, u32[]{:S(2)}, u32[]{:S(2)}) %collective-permute-start.72) | collective-permute-done | bytes 294944 | tf_op jit(solution)/shard_map/ppermute | solution.py:512
  703.4 12.2 %collective-permute-done.69 = bf16[128,1152]{0,1:T(8,128)(2,1)S(1)} collective-permute-done((bf16[128,1152]{0,1:T(8,128)(2,1)S(1)}, bf16[128,1152]{0,1:T(8,128)(2,1)S(1)}, u32[]{:S(2)}, u32[]{:S(2)}) %collective-permute-start.69) | collective-permute-done | bytes 294944 | tf_op jit(solution)/shard_map/ppermute | solution.py:512
  723.5 22.0 %collective-permute-start.76 = (bf16[128,1920]{0,1:T(8,128)(2,1)S(1)}, bf16[128,1920]{0,1:T(8,128)(2,1)S(1)}, u32[]{:S(2)}, u32[]{:S(2)}) collective-permute-start(bf16[128,1920]{0,1:T(8,128)(2,1)S(1)} %get-tuple-element.396), channel_id=1, source_target_pairs={{0,16},{8,24},{16,0},{24,8},{1,17},{9,25},{17,1},{25,9},{2,18},{10... | collective-permute-start | bytes 1474568 | tf_op jit(solution)/shard_map/ppermute | solution.py:76
  760.2 21.1 %collective-permute-done.79 = bf16[128,3456]{1,0:T(8,128)(2,1)} collective-permute-done((bf16[128,3456]{1,0:T(8,128)(2,1)}, bf16[128,3456]{1,0:T(8,128)(2,1)}, u32[]{:S(2)}, u32[]{:S(2)}) %collective-permute-start.79) | collective-permute-done | bytes 884768 | tf_op jit(solution)/shard_map/ppermute | solution.py:76
  (651 shorter events, 391.4 us)
Async XLA Ops:
  7.3 176.1 %all-gather.3.cloned.1.call-start = ((), (), s32[]{:S(2)}) async-start(), calls=%async_computation.2 | async-start | bytes 9732096 | tf_op jit(solution)/shard_map/all_gather | solution.py:503
  29.8 295.6 %all-gather.5.cloned.1.call-start = ((), (), s32[]{:S(2)}) async-start(), calls=%async_computation.3 | async-start | bytes 7962624 | tf_op jit(solution)/shard_map/all_gather | solution.py:503
  30.5 52.1 %collective-permute-start.1 = (bf16[384,1024]{1,0:T(8,128)(2,1)S(1)}, bf16[384,1024]{1,0:T(8,128)(2,1)S(1)}, u32[]{:S(2)}, u32[]{:S(2)}) collective-permute-start(bf16[384,1024]{1,0:T(8,128)(2,1)S(1)} %bitcast.196), channel_id=1, source_target_pairs={{0,16},{8,24},{16,0},{24,8},{1,17},{9,25},{17,1},{25,9},{2,18},{10... | collective-permute-start | bytes 2359304 | tf_op jit(solution)/shard_map/ppermute | solution.py:76
  36.0 67.5 %collective-permute-start = (bf16[384,1024]{1,0:T(8,128)(2,1)S(1)}, bf16[384,1024]{1,0:T(8,128)(2,1)}, u32[]{:S(2)}, u32[]{:S(2)}) collective-permute-start(bf16[384,1024]{1,0:T(8,128)(2,1)S(1)} %bitcast.197), channel_id=1, source_target_pairs={{0,8},{8,0},{16,24},{24,16},{1,9},{9,1},{17,25},{25,17},{2,10},{10... | collective-permute-start | bytes 2359304 | tf_op jit(solution)/shard_map/ppermute | solution.py:76
  38.8 39.3 %collective-permute-start.7 = (bf16[128,1152]{0,1:T(8,128)(2,1)}, bf16[128,1152]{0,1:T(8,128)(2,1)S(1)}, u32[]{:S(2)}, u32[]{:S(2)}) collective-permute-start(bf16[128,1152]{0,1:T(8,128)(2,1)} %copy-done.69), channel_id=1, source_target_pairs={{0,4},{1,5},{2,6},{3,7},{4,0},{5,1},{6,2},{7,3},{8,12},{9,13},{10,... | collective-permute-start | bytes 884744 | tf_op jit(solution)/shard_map/ppermute | solution.py:512
  41.3 36.8 %collective-permute-start.9 = (bf16[128,1152]{0,1:T(8,128)(2,1)}, bf16[128,1152]{0,1:T(8,128)(2,1)S(1)}, u32[]{:S(2)}, u32[]{:S(2)}) collective-permute-start(bf16[128,1152]{0,1:T(8,128)(2,1)} %copy-done.69), channel_id=1, source_target_pairs={{0,6},{1,7},{2,4},{3,5},{4,2},{5,3},{6,0},{7,1},{8,14},{9,15},{10,... | collective-permute-start | bytes 884744 | tf_op jit(solution)/shard_map/ppermute | solution.py:512
  48.1 35.2 %collective-permute-start.6 = (bf16[128,1152]{0,1:T(8,128)(2,1)}, bf16[128,1152]{0,1:T(8,128)(2,1)S(1)}, u32[]{:S(2)}, u32[]{:S(2)}) collective-permute-start(bf16[128,1152]{0,1:T(8,128)(2,1)} %copy-done.68), channel_id=1, source_target_pairs={{0,1},{1,0},{2,3},{3,2},{4,5},{5,4},{6,7},{7,6},{8,9},{9,8},{10,11... | collective-permute-start | bytes 884744 | tf_op jit(solution)/shard_map/ppermute | solution.py:512
  78.1 23.3 %collective-permute-start.10 = (bf16[128,1152]{0,1:T(8,128)(2,1)S(1)}, bf16[128,1152]{0,1:T(8,128)(2,1)S(1)}, u32[]{:S(2)}, u32[]{:S(2)}) collective-permute-start(bf16[128,1152]{0,1:T(8,128)(2,1)S(1)} %collective-permute-done.9), channel_id=1, source_target_pairs={{0,1},{1,0},{2,3},{3,2},{4,5},{5,4},{6,7},{7,6},{8,9},{9,8},{10,11... | collective-permute-start | bytes 884744 | tf_op jit(solution)/shard_map/ppermute | solution.py:512
  156.2 40.4 %collective-permute-start.17 = (bf16[384,1024]{1,0:T(8,128)(2,1)S(1)}, bf16[384,1024]{1,0:T(8,128)(2,1)}, u32[]{:S(2)}, u32[]{:S(2)}) collective-permute-start(bf16[384,1024]{1,0:T(8,128)(2,1)S(1)} %multiply_convert_fusion.3), channel_id=1, source_target_pairs={{0,16},{8,24},{16,0},{24,8},{1,17},{9,25},{17,1},{25,9},{2,18},{10... | collective-permute-start | bytes 2359304 | tf_op jit(solution)/shard_map/ppermute | solution.py:76
  197.7 394.7 %reduce-scatter.5.cloned.1.call-start = ((), (), s32[]{:S(2)}) async-start(), calls=%async_computation.5 | async-start | bytes 7962624 | tf_op jit(solution)/shard_map/reduce_scatter | solution.py:507
  237.3 24.8 %collective-permute-start.23 = (bf16[384,1024]{1,0:T(8,128)(2,1)}, bf16[384,1024]{1,0:T(8,128)(2,1)}, u32[]{:S(2)}, u32[]{:S(2)}) collective-permute-start(bf16[384,1024]{1,0:T(8,128)(2,1)} %multiply_convert_fusion.2), channel_id=1, source_target_pairs={{0,8},{8,0},{16,24},{24,16},{1,9},{9,1},{17,25},{25,17},{2,10},{10... | collective-permute-start | bytes 2359304 | tf_op jit(solution)/shard_map/ppermute | solution.py:76
  404.3 354.7 %reduce-scatter.3.cloned.1.call-start = ((), (), s32[]{:S(2)}) async-start(), calls=%async_computation.4 | async-start | bytes 7962624 | tf_op jit(solution)/shard_map/reduce_scatter | solution.py:507
  507.6 36.4 %collective-permute-start.44 = (bf16[384,1024]{1,0:T(8,128)(2,1)S(1)}, bf16[384,1024]{1,0:T(8,128)(2,1)S(1)}, u32[]{:S(2)}, u32[]{:S(2)}) collective-permute-start(bf16[384,1024]{1,0:T(8,128)(2,1)S(1)} %slice.639), channel_id=1, source_target_pairs={{0,8},{8,0},{16,24},{24,16},{1,9},{9,1},{17,25},{25,17},{2,10},{10... | collective-permute-start | bytes 2359304 | tf_op jit(solution)/shard_map/ppermute | solution.py:76
  519.5 23.5 %collective-permute-start.53 = (bf16[128,768]{0,1:T(8,128)(2,1)S(1)}, bf16[128,768]{0,1:T(8,128)(2,1)S(1)}, u32[]{:S(2)}, u32[]{:S(2)}) collective-permute-start(bf16[128,768]{0,1:T(8,128)(2,1)S(1)} %get-tuple-element.340), channel_id=1, source_target_pairs={{0,2},{1,3},{2,0},{3,1},{4,6},{5,7},{6,4},{7,5},{8,10},{9,11},{10,... | collective-permute-start | bytes 589832 | tf_op jit(solution)/shard_map/ppermute | solution.py:512
  598.3 48.7 %collective-permute-start.58 = (bf16[128,3456]{1,0:T(8,128)(2,1)}, bf16[128,3456]{1,0:T(8,128)(2,1)}, u32[]{:S(2)}, u32[]{:S(2)}) collective-permute-start(bf16[128,3456]{1,0:T(8,128)(2,1)} %reduce-scatter.5.cloned.1.call-done), channel_id=1, source_target_pairs={{0,16},{8,24},{16,0},{24,8},{1,17},{9,25},{17,1},{25,9},{2,18},{10... | collective-permute-start | bytes 2654216 | tf_op jit(solution)/shard_map/ppermute | solution.py:76
  609.0 67.0 %collective-permute-start.57 = (bf16[128,3456]{1,0:T(8,128)(2,1)}, bf16[128,3456]{1,0:T(8,128)(2,1)}, u32[]{:S(2)}, u32[]{:S(2)}) collective-permute-start(bf16[128,3456]{1,0:T(8,128)(2,1)} %reduce-scatter.5.cloned.1.call-done), channel_id=1, source_target_pairs={{0,8},{8,0},{16,24},{24,16},{1,9},{9,1},{17,25},{25,17},{2,10},{10... | collective-permute-start | bytes 2654216 | tf_op jit(solution)/shard_map/ppermute | solution.py:76
  646.0 25.1 %collective-permute-start.61 = (bf16[384,1024]{1,0:T(8,128)(2,1)}, bf16[384,1024]{1,0:T(8,128)(2,1)}, u32[]{:S(2)}, u32[]{:S(2)}) collective-permute-start(bf16[384,1024]{1,0:T(8,128)(2,1)} %get-tuple-element.296), channel_id=1, source_target_pairs={{0,16},{8,24},{16,0},{24,8},{1,17},{9,25},{17,1},{25,9},{2,18},{10... | collective-permute-start | bytes 2359304 | tf_op jit(solution)/shard_map/ppermute | solution.py:76
  647.0 30.4 %collective-permute-start.59 = (bf16[128,3456]{1,0:T(8,128)(2,1)}, bf16[128,3456]{1,0:T(8,128)(2,1)}, u32[]{:S(2)}, u32[]{:S(2)}) collective-permute-start(bf16[128,3456]{1,0:T(8,128)(2,1)} %collective-permute-done.58), channel_id=1, source_target_pairs={{0,8},{8,0},{16,24},{24,16},{1,9},{9,1},{17,25},{25,17},{2,10},{10... | collective-permute-start | bytes 2654216 | tf_op jit(solution)/shard_map/ppermute | solution.py:76
  658.0 22.8 %collective-permute-start.68 = (bf16[128,1152]{0,1:T(8,128)(2,1)S(1)}, bf16[128,1152]{0,1:T(8,128)(2,1)S(1)}, u32[]{:S(2)}, u32[]{:S(2)}) collective-permute-start(bf16[128,1152]{0,1:T(8,128)(2,1)S(1)} %get-tuple-element.326), channel_id=1, source_target_pairs={{0,1},{1,0},{2,3},{3,2},{4,5},{5,4},{6,7},{7,6},{8,9},{9,8},{10,11... | collective-permute-start | bytes 884744 | tf_op jit(solution)/shard_map/ppermute | solution.py:512
  658.7 24.5 %collective-permute-start.70 = (bf16[128,1152]{0,1:T(8,128)(2,1)S(1)}, bf16[128,1152]{0,1:T(8,128)(2,1)S(1)}, u32[]{:S(2)}, u32[]{:S(2)}) collective-permute-start(bf16[128,1152]{0,1:T(8,128)(2,1)S(1)} %get-tuple-element.325), channel_id=1, source_target_pairs={{0,1},{1,0},{2,3},{3,2},{4,5},{5,4},{6,7},{7,6},{8,9},{9,8},{10,11... | collective-permute-start | bytes 884744 | tf_op jit(solution)/shard_map/ppermute | solution.py:512
  671.1 23.7 %collective-permute-start.72 = (bf16[128,1152]{0,1:T(8,128)(2,1)S(1)}, bf16[128,1152]{0,1:T(8,128)(2,1)S(1)}, u32[]{:S(2)}, u32[]{:S(2)}) collective-permute-start(bf16[128,1152]{0,1:T(8,128)(2,1)S(1)} %get-tuple-element.324), channel_id=1, source_target_pairs={{0,1},{1,0},{2,3},{3,2},{4,5},{5,4},{6,7},{7,6},{8,9},{9,8},{10,11... | collective-permute-start | bytes 884744 | tf_op jit(solution)/shard_map/ppermute | solution.py:512
  676.0 27.4 %collective-permute-start.67 = (bf16[128,1152]{0,1:T(8,128)(2,1)S(1)}, bf16[128,1152]{0,1:T(8,128)(2,1)S(1)}, u32[]{:S(2)}, u32[]{:S(2)}) collective-permute-start(bf16[128,1152]{0,1:T(8,128)(2,1)S(1)} %get-tuple-element.323), channel_id=1, source_target_pairs={{0,1},{1,0},{2,3},{3,2},{4,5},{5,4},{6,7},{7,6},{8,9},{9,8},{10,11... | collective-permute-start | bytes 884744 | tf_op jit(solution)/shard_map/ppermute | solution.py:512
  723.5 31.2 %collective-permute-start.76 = (bf16[128,1920]{0,1:T(8,128)(2,1)S(1)}, bf16[128,1920]{0,1:T(8,128)(2,1)S(1)}, u32[]{:S(2)}, u32[]{:S(2)}) collective-permute-start(bf16[128,1920]{0,1:T(8,128)(2,1)S(1)} %get-tuple-element.396), channel_id=1, source_target_pairs={{0,16},{8,24},{16,0},{24,8},{1,17},{9,25},{17,1},{25,9},{2,18},{10... | collective-permute-start | bytes 1474568 | tf_op jit(solution)/shard_map/ppermute | solution.py:76
  760.1 28.4 %collective-permute-start.78 = (bf16[128,3456]{1,0:T(8,128)(2,1)}, bf16[128,3456]{1,0:T(8,128)(2,1)S(1)}, u32[]{:S(2)}, u32[]{:S(2)}) collective-permute-start(bf16[128,3456]{1,0:T(8,128)(2,1)} %reduce-scatter.3.cloned.1.call-done), channel_id=1, source_target_pairs={{0,8},{8,0},{16,24},{24,16},{1,9},{9,1},{17,25},{25,17},{2,10},{10... | collective-permute-start | bytes 2654216 | tf_op jit(solution)/shard_map/ppermute | solution.py:76
  (172 other events, 2006.7 us)
Sparse Core Ops, SparseCore 0:
  29.9 153.3 all-gather.2
  197.8 107.1 all-gather.4
  404.4 143.8 reduce-scatter.4
  589.7 161.4 reduce-scatter.2

commit v3 on v2

--- a/solution.py
+++ b/solution.py
@@ -162,8 +162,7 @@
     return (low, pltpu.roll(low, LANES // 2, 1))
 
 
-def load_heads(raw_ref, cos_ref, sin_ref, gains_ref, source, target, length, pairs):
-    rows = pl.ds(source, length)
+def load_heads(raw_ref, cos_ref, sin_ref, gains_ref, rows, target, length, pairs):
     cosine = cos_ref[pl.ds(target, length), :]
     sine = sin_ref[pl.ds(target, length), :]
     groups = raw_ref.shape[1] // LANES
@@ -197,18 +196,26 @@
     return (key >= start) & (key <= query)
 
 
-def attention_forward_kernel(
-    place_ref, raw_ref, cos_ref, sin_ref, start_ref, gains_ref,
-    out_ref, wide_ref, total_ref, query_ref, key_ref, value_ref,
-    *, length, pairs,
-):
+def block_rows(block, count, length):
+    half, offset = divmod(block, count // 2)
+    return (half, slice(offset * length, (offset + 1) * length))
+
+
+def attention_forward_kernel(place_ref, *refs, length, pairs, tokens):
+    token_refs = refs[:tokens]
+    (
+        qkv_ref, o_ref, cos_ref, sin_ref, start_ref, gains_ref,
+        raw_ref, out_ref, wide_ref, total_ref, near_out_ref, far_out_ref,
+        query_ref, key_ref, value_ref,
+    ) = refs[tokens:]
     full = raw_ref.shape[0]
     count = full // length
     place = place_ref[0]
 
-    def prepare(block, _):
-        target = pl.multiple_of(block * length, 8)
-        source = pl.multiple_of((block ^ place) * length, 8)
+    for block in range(count):
+        target = pl.multiple_of((block ^ place) * length, 8)
+        source = slice(block * length, (block + 1) * length)
+        raw_ref[source, :] = plain_dot(token_refs[block][...], qkv_ref[...])
         queries, keys, values = load_heads(
             raw_ref, cos_ref, sin_ref, gains_ref, source, target, length, pairs
         )
@@ -217,9 +224,7 @@
             for h in range(2):
                 key_ref[2 * g + h, pl.ds(target, length), :] = keys[g][h]
                 value_ref[2 * g + h, pl.ds(target, length), :] = values[g][h]
-        return 0
-
-    lax.fori_loop(0, count, prepare, 0)
+
     half = LANES // 2
 
     def query_tile(i, _):
@@ -264,49 +269,47 @@
 
     lax.fori_loop(0, full // TILE, query_tile, 0)
 
-    def finish(block, _):
-        source = pl.multiple_of(block * length, 8)
-        target = pl.multiple_of((block ^ place) * length, 8)
+    for block in range(count):
+        side, rows = block_rows(block, count, length)
+        source = pl.multiple_of((block ^ place) * length, 8)
+        target = slice(block * length, (block + 1) * length)
         for g in range(pairs):
-            out_ref[pl.ds(target, length), g * LANES : (g + 1) * LANES] = query_ref[
+            out_ref[target, g * LANES : (g + 1) * LANES] = query_ref[
                 g, pl.ds(source, length), :
             ]
-        return 0
-
-    lax.fori_loop(0, count, finish, 0)
-
-
-def attention_backward_kernel(
-    place_ref, raw_ref, cos_ref, sin_ref, start_ref, gains_ref, wide_ref, total_ref, grad_ref,
-    out_ref, gain_grad_ref,
-    query_ref, key_ref, value_ref, hold_ref, dq_ref, dk_ref, dv_ref,
-    *, length, pairs,
-):
+        partial = plain_dot(out_ref[target, :], o_ref[...])
+        (near_out_ref, far_out_ref)[side][rows, :] = partial.astype(BF16)
+
+
+def attention_backward_kernel(place_ref, *refs, length, pairs, tokens):
+    token_refs = refs[:tokens]
+    (
+        qkv_ref, o_ref, cos_ref, sin_ref, start_ref, gains_ref, raw_ref, wide_ref, total_ref,
+        out_ref, near_out_ref, far_out_ref, gain_grad_ref,
+        query_ref, key_ref, value_ref, hold_ref, dq_ref, dk_ref, dv_ref,
+    ) = refs[tokens:]
     full = raw_ref.shape[0]
     count = full // length
     place = place_ref[0]
     half = LANES // 2
 
-    def prepare(block, _):
-        target = pl.multiple_of(block * length, 8)
-        source = pl.multiple_of((block ^ place) * length, 8)
+    for block in range(count):
+        target = pl.multiple_of((block ^ place) * length, 8)
+        source = slice(block * length, (block + 1) * length)
+        grads = right_dot(token_refs[block][...], o_ref[...]).astype(BF16)
         queries, keys, values = load_heads(
             raw_ref, cos_ref, sin_ref, gains_ref, source, target, length, pairs
         )
         rows = pl.ds(target, length)
         for g in range(pairs):
             query_ref[g, rows, :] = queries[g]
-            hold_ref[g, rows, :] = grad_ref[
-                pl.ds(source, length), g * LANES : (g + 1) * LANES
-            ]
+            hold_ref[g, rows, :] = grads[:, g * LANES : (g + 1) * LANES]
             dk_ref[g, rows, :] = jnp.zeros((length, LANES), F32)
             dv_ref[g, rows, :] = jnp.zeros((length, LANES), F32)
             for h in range(2):
                 key_ref[2 * g + h, rows, :] = keys[g][h]
                 value_ref[2 * g + h, rows, :] = values[g][h]
-        return 0
-
-    lax.fori_loop(0, count, prepare, 0)
+
     lower = half_lanes((TILE, LANES))
 
     def query_tile(i, _):
@@ -362,29 +365,28 @@
     lax.fori_loop(0, full // TILE, query_tile, 0)
     scale = half ** (-0.5)
 
-    def finish(block, carry):
-        source = pl.multiple_of(block * length, 8)
-        target = pl.multiple_of((block ^ place) * length, 8)
-        rows = pl.ds(source, length)
+    low = half_lanes((length, LANES))
+    query_gain = jnp.zeros((1, LANES), F32)
+    key_gain = jnp.zeros((1, LANES), F32)
+    for block in range(count):
+        side, side_rows = block_rows(block, count, length)
+        rows = pl.ds(pl.multiple_of((block ^ place) * length, 8), length)
+        target = slice(block * length, (block + 1) * length)
         cosine = cos_ref[rows, :]
         sine = sin_ref[rows, :]
-        low = half_lanes((length, LANES))
 
         def back(grad, group, gain):
             grad = grad.astype(BF16).astype(F32)
-            unit, inverse = head_unit(
-                raw_ref[pl.ds(target, length), group * LANES : (group + 1) * LANES]
-            )
+            unit, inverse = head_unit(raw_ref[target, group * LANES : (group + 1) * LANES])
             d_rot = grad * cosine + swap_quarters(grad * sine)
             weighted = d_rot * gain
             d_raw = inverse * (weighted - unit * head_mean(weighted * unit))
             return (d_raw, d_rot * unit)
 
-        query_gain, key_gain = carry
         for g in range(pairs):
             d_raw, terms = back(dq_ref[g, rows, :] * scale, g, gains_ref[0:1, :])
             query_gain = query_gain + jnp.sum(terms, 0, keepdims=True)
-            out_ref[pl.ds(target, length), g * LANES : (g + 1) * LANES] = d_raw.astype(BF16)
+            out_ref[target, g * LANES : (g + 1) * LANES] = d_raw.astype(BF16)
         groups = {}
         for kind, held in ((0, dk_ref), (1, dv_ref)):
             for g in range(pairs):
@@ -404,13 +406,9 @@
                     terms = jnp.where(low, terms, 0.0)
                 result = d_raw
                 key_gain = key_gain + jnp.sum(terms, 0, keepdims=True)
-            out_ref[pl.ds(target, length), group * LANES : (group + 1) * LANES] = result.astype(
-                BF16
-            )
-        return (query_gain, key_gain)
-
-    zero = jnp.zeros((1, LANES), F32)
-    query_gain, key_gain = lax.fori_loop(0, count, finish, (zero, zero))
+            out_ref[target, group * LANES : (group + 1) * LANES] = result.astype(BF16)
+        partial = right_dot(out_ref[target, :], qkv_ref[...])
+        (near_out_ref, far_out_ref)[side][side_rows, :] = partial.astype(BF16)
     gain_grad_ref[0:1, :] = query_gain
     gain_grad_ref[1:2, :] = key_gain
 
@@ -419,38 +417,53 @@
     return [pl.BlockSpec(memory_space=pltpu.VMEM)] * count
 
 
-def attention_forward(place, raw, cosine, sine, start, gains, length):
-    full, columns = raw.shape
+def attention_forward(place, tokens, qkv, o, cosine, sine, start, gains):
+    length = tokens[0].shape[0]
+    full = len(tokens) * length
+    width, columns = qkv.shape
     pairs = columns // (2 * LANES)
     return pl.pallas_call(
-        lambda *refs: attention_forward_kernel(*refs, length=length, pairs=pairs),
-        in_specs=[pl.BlockSpec(memory_space=pltpu.SMEM)] + whole(5),
-        out_specs=tuple(whole(3)),
+        lambda *refs: attention_forward_kernel(
+            *refs, length=length, pairs=pairs, tokens=len(tokens)
+        ),
+        in_specs=[pl.BlockSpec(memory_space=pltpu.SMEM)] + whole(6 + len(tokens)),
+        out_specs=tuple(whole(6)),
         out_shape=(
+            jax.ShapeDtypeStruct((full, columns), F32),
             jax.ShapeDtypeStruct((full, pairs * LANES), BF16),
             jax.ShapeDtypeStruct((pairs * LANES, full), F32),
             jax.ShapeDtypeStruct((8, full), F32),
+            jax.ShapeDtypeStruct((full // 2, width), BF16),
+            jax.ShapeDtypeStruct((full // 2, width), BF16),
         ),
         scratch_shapes=[
             pltpu.VMEM((pairs, full, LANES), BF16),
             pltpu.VMEM((2 * pairs, full, LANES), BF16),
             pltpu.VMEM((2 * pairs, full, LANES), BF16),
         ],
+        cost_estimate=pl.CostEstimate(
+            flops=20_000_000_000, transcendentals=6_000_000, bytes_accessed=20_000_000
+        ),
         compiler_params=pltpu.CompilerParams(vmem_limit_bytes=VMEM_LIMIT),
-        cost_estimate=pl.CostEstimate(flops=20_000_000_000, transcendentals=6000000, bytes_accessed=20000000),
         name="attention_forward",
-    )(place, raw, cosine, sine, start, gains)
-
-
-def attention_backward(place, raw, cosine, sine, start, gains, wide, totals, grads, length):
-    full, columns = raw.shape
+    )(place, *tokens, qkv, o, cosine, sine, start, gains)
+
+
+def attention_backward(place, tokens, qkv, o, cosine, sine, start, gains, raw, wide, totals):
+    length = tokens[0].shape[0]
+    full = len(tokens) * length
+    width, columns = qkv.shape
     pairs = columns // (2 * LANES)
     return pl.pallas_call(
-        lambda *refs: attention_backward_kernel(*refs, length=length, pairs=pairs),
-        in_specs=[pl.BlockSpec(memory_space=pltpu.SMEM)] + whole(8),
-        out_specs=tuple(whole(2)),
+        lambda *refs: attention_backward_kernel(
+            *refs, length=length, pairs=pairs, tokens=len(tokens)
+        ),
+        in_specs=[pl.BlockSpec(memory_space=pltpu.SMEM)] + whole(9 + len(tokens)),
+        out_specs=tuple(whole(4)),
         out_shape=(
             jax.ShapeDtypeStruct((full, columns), BF16),
+            jax.ShapeDtypeStruct((full // 2, width), BF16),
+            jax.ShapeDtypeStruct((full // 2, width), BF16),
             jax.ShapeDtypeStruct((2, LANES), F32),
         ),
         scratch_shapes=[
@@ -462,10 +475,13 @@
             pltpu.VMEM((pairs, full, LANES), F32),
             pltpu.VMEM((pairs, full, LANES), F32),
         ],
+        cost_estimate=pl.CostEstimate(
+            flops=20_000_000_000, transcendentals=6_000_000, bytes_accessed=20_000_000
+        ),
         compiler_params=pltpu.CompilerParams(vmem_limit_bytes=VMEM_LIMIT),
-        cost_estimate=pl.CostEstimate(flops=20_000_000_000, transcendentals=6000000, bytes_accessed=20000000),
         name="attention_backward",
-    )(place, raw, cosine, sine, start, gains, wide, totals, grads)
+    )(place, *tokens, qkv, o, cosine, sine, start, gains, raw, wide, totals)
+
 
 def column_block(weight, parts):
     size = lax.axis_size("seq")
@@ -495,6 +511,32 @@
     return lax.ppermute(part, ("seq", "dp"), deal_pairs())
 
 
+def pack_piece(piece, columns):
+    count = piece.shape[1] // columns
+    return jnp.concatenate(
+        [piece[:, n * columns : (n + 1) * columns] for n in range(count)], 0
+    )
+
+
+def unpack_piece(block, width):
+    count = width // block.shape[1]
+    rows = block.shape[0] // count
+    return jnp.concatenate([block[n * rows : (n + 1) * rows] for n in range(count)], 1)
+
+
+def pack_rows(rows_block, parts):
+    rows, width = rows_block.shape
+    piece = rows // parts
+    split = rows_block.reshape(parts, piece, width // rows, rows)
+    return jnp.swapaxes(split, 1, 2).reshape(width, rows)
+
+
+def unpack_rows(block, parts):
+    width, rows = block.shape
+    split = block.reshape(parts, width // rows, rows // parts, rows)
+    return jnp.swapaxes(split, 1, 2).reshape(rows, width)
+
+
 def undeal_rows(part):
     return lax.ppermute(part, ("seq", "dp"), [(b, a) for a, b in deal_pairs()])
 
@@ -512,61 +554,93 @@
     return lax.ppermute(array, "dp", [(i, i ^ bit) for i in range(size)])
 
 
+def dp_bits():
+    return [1, 2, 4] if lax.axis_size("dp") == 8 else []
+
+
 def dp_gather_small(block, later):
+    if not dp_bits():
+        return (dp_gather(block), later)
     size = lax.axis_size("dp")
-    if size != 8:
-        return (dp_gather(block), later)
     place = lax.axis_index("dp")
     rows = block.shape[0]
-    have = {0: block}
-    for far in (2, 4, 6):
-        have[far] = swap_dp(block, far)
-    have[2], later = tie(have[2], later)
-    for far in (0, 2, 4, 6):
-        have[far ^ 1] = swap_dp(have[far], 1)
+    turns = [0]
+    held = block
+    for bit in reversed(dp_bits()):
+        got = swap_dp(held, bit)
+        if bit == dp_bits()[1]:
+            got, later = tie(got, later)
+        held = jnp.concatenate([held, got], 0)
+        turns = turns + [turn | bit for turn in turns]
     result = jnp.zeros((size * rows, block.shape[1]), block.dtype)
-    for turn in range(size):
-        result = lax.dynamic_update_slice_in_dim(result, have[turn], (place ^ turn) * rows, 0)
+    for number, turn in enumerate(turns):
+        piece = held[number * rows : (number + 1) * rows]
+        result = lax.dynamic_update_slice_in_dim(result, piece, (place ^ turn) * rows, 0)
     return (result, later)
 
 
-def dp_scatter_small(grads):
-    size = lax.axis_size("dp")
-    if size != 8:
-        return dp_scatter(grads)
-    place = lax.axis_index("dp")
-    rows = grads.shape[0] // size
-
-    def part(turn):
-        return lax.dynamic_slice_in_dim(grads, (place ^ turn) * rows, rows, 0)
-
-    sums = {}
-    for far in (4, 6, 2, 0):
-        sums[far] = part(far).astype(F32) + swap_dp(part(far ^ 1), 1).astype(F32)
-    total = sums[0]
-    for far in (4, 6, 2):
-        total = total + swap_dp(sums[far].astype(BF16), far).astype(F32)
-    return total.astype(BF16)
-
-
 def share(owned):
-    size = lax.axis_size("seq")
-    place = lax.axis_index("seq")
-    everywhere = jnp.stack(near_blocks(owned) + near_blocks(far_half(owned)), 0)
-    return [lax.dynamic_index_in_dim(everywhere, place ^ i, 0, False) for i in range(size)]
-
-
-def split_columns(blocks, parts):
+    return near_blocks(owned) + near_blocks(far_half(owned))
+
+
+def assemble_kernel(place_ref, *refs, count, tasks):
+    blocks = refs[:count]
+    outs = refs[count:]
+    place = place_ref[0]
+    for turn in range(count):
+        for target in range(count):
+
+            @pl.when((place ^ turn) == target)
+            def _():
+                for (start, columns, split, by_rows), out_ref in zip(tasks, outs):
+                    if by_rows:
+                        rows = blocks[turn].shape[0] // count
+                        for part in range(count):
+                            out_ref[
+                                target * rows : (target + 1) * rows,
+                                part * columns : (part + 1) * columns,
+                            ] = blocks[turn][
+                                part * rows : (part + 1) * rows, start : start + columns
+                            ].astype(F32)
+                    else:
+                        step = columns // split
+                        for part in range(split):
+                            first = (part * count + target) * step
+                            out_ref[:, first : first + step] = blocks[turn][
+                                :, start + part * step : start + (part + 1) * step
+                            ].astype(F32)
+
+
+def assemble(place, blocks, tasks):
+    count = len(blocks)
+    rows = blocks[0].shape[0]
+    if all(columns // split % LANES == 0 for _, columns, split, _ in tasks):
+        return pl.pallas_call(
+            lambda *refs: assemble_kernel(*refs, count=count, tasks=tasks),
+            in_specs=[pl.BlockSpec(memory_space=pltpu.SMEM)] + whole(count),
+            out_specs=tuple(whole(len(tasks))),
+            out_shape=tuple(
+                jax.ShapeDtypeStruct((rows, count * columns), F32) for _, columns, _, _ in tasks
+            ),
+            compiler_params=pltpu.CompilerParams(vmem_limit_bytes=VMEM_LIMIT),
+            name="assemble",
+        )(place, *blocks)
+    stacked = jnp.stack(blocks, 0)
+    ordered = [
+        lax.dynamic_index_in_dim(stacked, place[0] ^ i, 0, False) for i in range(count)
+    ]
     results = []
-    offset = 0
-    for split, columns in parts:
-        pieces = []
-        for number in range(split):
-            start = offset + number * columns
-            pieces = pieces + [block[:, start : start + columns] for block in blocks]
-        results.append(jnp.concatenate(pieces, 1).astype(F32))
-        offset = offset + split * columns
-    return (results, [block[:, offset:] for block in blocks])
+    for start, columns, split, by_rows in tasks:
+        parts = [block[:, start : start + columns] for block in ordered]
+        if by_rows:
+            joined = jnp.concatenate([unpack_piece(p, count * columns) for p in parts], 0)
+        else:
+            step = columns // split
+            joined = jnp.concatenate(
+                [p[:, n * step : (n + 1) * step] for n in range(split) for p in parts], 1
+            )
+        results.append(joined.astype(F32))
+    return results
 
 
 def gate_terms(normed, w_gate, w_up):
@@ -577,10 +651,19 @@
     return (upper * (sigma + swish * (1.0 - sigma)), swish, swish * upper)
 
 
-def ffn_forward_kernel(normed_ref, gate_ref, up_ref, down_ref, *rest):
-    kept_ref, partial_ref = rest[-2:]
+def block_here(refs):
+    value = refs[0][...]
+    for number, ref in enumerate(refs[1:]):
+        value = jnp.where(pl.program_id(0) == number + 1, ref[...], value)
+    return value
+
+
+def ffn_forward_kernel(*refs, count):
+    normed_refs = refs[:count]
+    gate_ref, up_ref, down_ref = refs[count : count + 3]
+    kept_ref, partial_ref = refs[-2:]
     hidden = gate_ref.shape[1]
-    slope, swish, act = gate_terms(normed_ref[...], gate_ref[...], up_ref[...])
+    slope, swish, act = gate_terms(block_here(normed_refs), gate_ref[...], up_ref[...])
     act = act.astype(BF16)
     kept_ref[:, :hidden] = slope.astype(BF16)
     kept_ref[:, hidden : 2 * hidden] = swish.astype(BF16)
@@ -588,11 +671,14 @@
     partial_ref[...] = right_dot(act, down_ref[...]).astype(BF16)
 
 
-def ffn_turn_kernel(normed_ref, grad_ref, gate_ref, up_ref, down_ref, *rest):
-    kept_ref, partial_ref = rest[-2:]
+def ffn_turn_kernel(*refs, count):
+    normed_refs = refs[:count]
+    grad_refs = refs[count : 2 * count]
+    gate_ref, up_ref, down_ref = refs[2 * count : 2 * count + 3]
+    kept_ref, partial_ref = refs[-2:]
     hidden = gate_ref.shape[1]
-    slope, swish, act = gate_terms(normed_ref[...], gate_ref[...], up_ref[...])
-    d_act = plain_dot(grad_ref[...], down_ref[...])
+    slope, swish, act = gate_terms(block_here(normed_refs), gate_ref[...], up_ref[...])
+    d_act = plain_dot(block_here(grad_refs), down_ref[...])
     d_gate = (d_act * slope).astype(BF16)
     d_up = (d_act * swish).astype(BF16)
     kept_ref[:, :hidden] = d_gate
@@ -602,10 +688,12 @@
     partial_ref[...] = partial.astype(BF16)
 
 
-def ffn_backward_kernel(grad_ref, terms_ref, gate_ref, up_ref, down_ref, *rest):
-    kept_ref, partial_ref = rest[-2:]
+def ffn_backward_kernel(*refs, count):
+    grad_refs = refs[:count]
+    terms_ref, gate_ref, up_ref, down_ref = refs[count : count + 4]
+    kept_ref, partial_ref = refs[-2:]
     hidden = gate_ref.shape[1]
-    d_act = plain_dot(grad_ref[...], down_ref[...])
+    d_act = plain_dot(block_here(grad_refs), down_ref[...])
     d_gate = (d_act * terms_ref[:, :hidden].astype(F32)).astype(BF16)
     d_up = (d_act * terms_ref[:, hidden:].astype(F32)).astype(BF16)
     kept_ref[:, :hidden] = d_gate
@@ -614,11 +702,15 @@
     partial_ref[...] = partial.astype(BF16)
 
 
-def ffn_call(kernel, name, tokens, terms, weights, hidden, length, first, full, kept_width, kept):
+def ffn_call(kernel, name, tokens, terms, weights, hidden, first, full, kept_width, kept):
     width = weights.shape[0]
-    count = tokens[0].shape[0] // length
-    in_specs = [pl.BlockSpec((length, width), lambda i: (i, 0)) for _ in tokens]
-    operands = list(tokens)
+    count = len(tokens[0])
+    length = tokens[0][0].shape[0]
+    operands = [block for blocks in tokens for block in blocks]
+    in_specs = [
+        pl.BlockSpec((length, width), lambda i: (0, 0), pipeline_mode=pl.Buffered(1))
+        for _ in operands
+    ]
     if terms is not None:
         in_specs.append(pl.BlockSpec((length, 2 * hidden), lambda i: (i + first, 0)))
         operands.append(terms)
@@ -635,7 +727,7 @@
         in_specs.append(pl.BlockSpec(memory_space=pl.ANY))
         operands.append(kept)
     return pl.pallas_call(
-        kernel,
+        lambda *refs: kernel(*refs, count=count),
         grid=(count,),
         in_specs=in_specs,
         out_specs=(
@@ -647,8 +739,10 @@
             jax.ShapeDtypeStruct((count * length, width), BF16),
         ),
         input_output_aliases=aliases,
+        cost_estimate=pl.CostEstimate(
+            flops=6_000_000_000, transcendentals=1_000_000, bytes_accessed=20_000_000
+        ),
         compiler_params=pltpu.CompilerParams(vmem_limit_bytes=VMEM_LIMIT),
-        cost_estimate=pl.CostEstimate(flops=6_000_000_000, transcendentals=1000000, bytes_accessed=20000000),
         name=name,
     )(*operands)
 
@@ -660,10 +754,6 @@
 def halves_of(array):
     half = array.shape[0] // 2
     return (array[:half], array[half:])
-
-
-def first_block(number, full, length):
-    return number * (full // length // 2)
 
 
 def place_rows(kept, part, number):
@@ -672,49 +762,117 @@
     return lax.dynamic_update_slice_in_dim(kept, part, number * part.shape[0], 0)
 
 
-def ffn_forward(normed, weights, hidden, length, number, kept):
-    full = 2 * normed.shape[0]
+def ffn_forward(normed, weights, hidden):
     if hidden % LANES:
         w_gate, w_up, w_down = split_weights(weights, hidden)
-        terms = jnp.concatenate(gate_terms(normed, w_gate, w_up), 1).astype(BF16)
-        partial = right_dot(terms[:, 2 * hidden :], w_down).astype(BF16)
-        return (place_rows(kept, terms, number), partial)
+        terms = gate_terms(jnp.concatenate(normed, 0), w_gate, w_up)
+        terms = jnp.concatenate(terms, 1).astype(BF16)
+        return (terms, right_dot(terms[:, 2 * hidden :], w_down).astype(BF16))
     return ffn_call(
-        ffn_forward_kernel, "ffn_forward", [normed], None, weights, hidden, length,
-        first_block(number, full, length), full, 3 * hidden, kept,
-    )
-
-
-def ffn_turn(normed, grads, weights, hidden, length, number, kept):
-    full = 2 * normed.shape[0]
+        ffn_forward_kernel, "ffn_forward", [normed], None, weights, hidden,
+        0, len(normed) * normed[0].shape[0], 3 * hidden, None,
+    )
+
+
+def ffn_turn(normed, grads, weights, hidden, number, kept):
     if hidden % LANES:
         w_gate, w_up, w_down = split_weights(weights, hidden)
-        slope, swish, act = gate_terms(normed, w_gate, w_up)
-        d_act = plain_dot(grads, w_down)
+        slope, swish, act = gate_terms(jnp.concatenate(normed, 0), w_gate, w_up)
+        d_act = plain_dot(jnp.concatenate(grads, 0), w_down)
         part = jnp.concatenate([d_act * slope, d_act * swish, act], 1).astype(BF16)
         partial = right_dot(part[:, : 2 * hidden], weights[:, : 2 * hidden]).astype(BF16)
         return (place_rows(kept, part, number), partial)
+    count = len(normed)
     return ffn_call(
-        ffn_turn_kernel, "ffn_turn", [normed, grads], None, weights, hidden, length,
-        first_block(number, full, length), full, 3 * hidden, kept,
-    )
-
-
-def ffn_backward(grads, terms, weights, hidden, length, number, kept):
-    full = 2 * grads.shape[0]
+        ffn_turn_kernel, "ffn_turn", [normed, grads], None, weights, hidden,
+        number * count, 2 * count * normed[0].shape[0], 3 * hidden, kept,
+    )
+
+
+def ffn_backward(grads, terms, weights, hidden, number, kept):
+    count = len(grads)
+    length = grads[0].shape[0]
     if hidden % LANES:
         w_gate, w_up, w_down = split_weights(weights, hidden)
-        rows = slice(number * grads.shape[0], (number + 1) * grads.shape[0])
-        d_act = plain_dot(grads, w_down)
+        rows = slice(number * count * length, (number + 1) * count * length)
+        d_act = plain_dot(jnp.concatenate(grads, 0), w_down)
         slope = terms[rows, :hidden].astype(F32)
         swish = terms[rows, hidden : 2 * hidden].astype(F32)
         part = jnp.concatenate([d_act * slope, d_act * swish], 1).astype(BF16)
         partial = right_dot(part, weights[:, : 2 * hidden]).astype(BF16)
         return (place_rows(kept, part, number), partial)
     return ffn_call(
-        ffn_backward_kernel, "ffn_backward", [grads], terms, weights, hidden, length,
-        first_block(number, full, length), full, 2 * hidden, kept,
-    )
+        ffn_backward_kernel, "ffn_backward", [grads], terms, weights, hidden,
+        number * count, 2 * count * length, 2 * hidden, kept,
+    )
+
+
+def conv_forward_kernel(*refs, length, tokens, taps):
+    place_ref, bounds_ref = refs[:2]
+    token_refs = refs[2 : 2 + tokens]
+    (
+        in_ref, out_w_ref, tap_ref, gain_ref,
+        normed_ref, projected_ref, gated_ref, near_out_ref, far_out_ref, product_ref,
+    ) = refs[2 + tokens :]
+    place = place_ref[0]
+    channels = gated_ref.shape[1]
+    product_ref[0:8, :] = jnp.zeros((8, channels), F32)
+    for block in range(tokens):
+        rows = slice(block * length, (block + 1) * length)
+        value = token_refs[block][...].astype(F32)
+        scale = lax.rsqrt(jnp.mean(value * value, -1, keepdims=True) + EPS)
+        normed = (value * scale * gain_ref[...]).astype(BF16)
+        normed_ref[rows, :] = normed
+        projected = plain_dot(normed, in_ref[:, : 3 * channels])
+        projected_ref[rows, :] = projected
+        product = (projected[:, :channels] * projected[:, 2 * channels :]).astype(BF16)
+        target = pl.multiple_of(8 + (block ^ place) * length, 8)
+        product_ref[pl.ds(target, length), :] = product.astype(F32)
+    for block in range(tokens):
+        side, side_rows = block_rows(block, tokens, length)
+        rows = slice(block * length, (block + 1) * length)
+        first = pl.multiple_of((block ^ place) * length, 8)
+        window = product_ref[pl.ds(first, length + 8), :]
+        token = first + lax.broadcasted_iota(jnp.int32, (length, channels), 0)
+        start = jnp.zeros((length, channels), jnp.int32)
+        for number in range(1, bounds_ref.shape[0]):
+            bound = bounds_ref[number]
+            start = jnp.where(bound <= token, jnp.maximum(start, bound), start)
+        conv = tap_ref[0:1, :] * window[8:, :]
+        for tap in range(1, taps):
+            moved = window[8 - tap : 8 - tap + length, :]
+            moved = jnp.where(token - tap >= start, moved, 0.0)
+            conv = conv + tap_ref[tap : tap + 1, :] * moved
+        gated = (projected_ref[rows, channels : 2 * channels] * conv).astype(BF16)
+        gated_ref[rows, :] = gated
+        partial = plain_dot(gated, out_w_ref[...]).astype(BF16)
+        (near_out_ref, far_out_ref)[side][side_rows, :] = partial
+
+
+def conv_forward(place, bounds, tokens, in_weights, out_weights, kernel, gain):
+    length, width = tokens[0].shape
+    full = len(tokens) * length
+    channels = out_weights.shape[0]
+    taps = kernel.shape[0]
+    scalar = pl.BlockSpec(memory_space=pltpu.SMEM)
+    return pl.pallas_call(
+        lambda *refs: conv_forward_kernel(*refs, length=length, tokens=len(tokens), taps=taps),
+        in_specs=[scalar, scalar] + whole(len(tokens) + 4),
+        out_specs=tuple(whole(5)),
+        out_shape=(
+            jax.ShapeDtypeStruct((full, width), BF16),
+            jax.ShapeDtypeStruct((full, 3 * channels), F32),
+            jax.ShapeDtypeStruct((full, channels), BF16),
+            jax.ShapeDtypeStruct((full // 2, width), BF16),
+            jax.ShapeDtypeStruct((full // 2, width), BF16),
+        ),
+        scratch_shapes=[pltpu.VMEM((full + 8, channels), F32)],
+        cost_estimate=pl.CostEstimate(
+            flops=4_000_000_000, transcendentals=2_000, bytes_accessed=20_000_000
+        ),
+        compiler_params=pltpu.CompilerParams(vmem_limit_bytes=VMEM_LIMIT),
+        name="conv_forward",
+    )(place, bounds, *tokens, in_weights, out_weights, kernel, gain)
 
 
 def local(
@@ -756,49 +914,40 @@
 
     x_far = far_half(x_in.reshape(length, width))
     cotangent_low, x_far = tie(cotangent.reshape(length, width), x_far)
-    x_all = jnp.concatenate([near_half(x_in.reshape(length, width)), near_half(x_far)], 0)
-    cotangent_halves = [near_half(cotangent_low), near_half(far_half(cotangent_low))]
+    x_blocks = near_blocks(x_in.reshape(length, width)) + near_blocks(x_far)
+    cotangent_blocks = near_blocks(cotangent_low) + near_blocks(far_half(cotangent_low))
     head_gains = jnp.pad(jnp.stack([g_q, g_k], 1), ((0, slots - head // dp_count), (0, 0)))
     small = jnp.concatenate(
         [conv_w.T, jnp.stack([g_mix1, g_ffn1, g_attn2, g_ffn2], 1), head_gains], 1
     )
     small = jnp.pad(small, ((0, 0), (0, 128 - small.shape[1])))
     dealt = deal_rows(jnp.stack([w_out, w_o], 1))
-    out_piece = dealt[:, 0].reshape(slots, -1)
-    o_piece = dealt[:, 1].reshape(slots, -1)
-    ffn_columns = 3 * w_gate1.shape[1] // seq_count
-    both = jnp.concatenate(
-        [column_block(w, 1) for w in (w_gate1, w_up1, w_down1)]
-        + [
-            column_block(w_q, 1),
-            column_block(key_projection_weight, 1),
-            column_block(value_projection_weight, 1),
-            o_piece,
-        ],
+    out_piece = pack_piece(dealt[:, 0], channels)
+    o_piece = pack_piece(dealt[:, 1], channels)
+    mix_block = jnp.concatenate([column_block(w_in, 3), small, out_piece], 1)
+    mix_block, w_gate1, w_up1, w_down1, w_q, key_projection_weight, value_projection_weight = tie(
+        mix_block, w_gate1, w_up1, w_down1, w_q, key_projection_weight, value_projection_weight
+    )
+    hidden = w_gate1.shape[1] // seq_count
+    ffn_one = jnp.concatenate(
+        [
+            column_block(w, 1)
+            for w in (
+                w_gate1, w_up1, w_down1, w_q, key_projection_weight, value_projection_weight
+            )
+        ]
+        + [o_piece],
         1,
     )
-    mix_all, both = dp_gather_small(
-        jnp.concatenate([column_block(w_in, 3), small, out_piece], 1), both
-    )
-    both = dp_gather(both)
-    mix_all, *cotangent_halves = tie(mix_all, *cotangent_halves)
-    ffn_one = both
-    hidden = ffn_columns // 3
-    attn_all = both[:, ffn_columns:]
+    mix_all, ffn_one = dp_gather_small(mix_block, ffn_one)
+    ffn_one = dp_gather(ffn_one)
+    attn_all = ffn_one[:, 3 * hidden :]
     ffn_two = dp_gather(
         jnp.concatenate([column_block(w, 1) for w in (w_gate2, w_up2, w_down2)], 1)
     )
-    in_block = mix_all[:, : 3 * channels]
-    out_block = mix_all[:, 3 * channels + 128 :].reshape(channels, width)
     qkv_width = attn_all.shape[1] - channels
     qkv_block = attn_all[:, :qkv_width]
-    o_block = attn_all[:, qkv_width:].reshape(channels, width)
-    small_all = mix_all[:, 3 * channels : 3 * channels + 128].astype(F32).T
-    kernel = lax.dynamic_slice_in_dim(small_all[:taps], seq_place * channels, channels, 1)
-    gain_mix, gain_ffn_one, gain_attn, gain_ffn_two = (small_all[taps + i] for i in range(4))
-    head_gains = small_all[taps + 4 : taps + 6].reshape(2, dp_count, slots)
-    head_gains = jnp.tile(head_gains[:, :, : head // dp_count].reshape(2, head), (1, 2))
-
+    o_block = unpack_rows(attn_all[:, qkv_width:], dp_count)
     bounds = cu_seqlens[0]
     turn = seq_place ^ jnp.arange(seq_count, dtype=jnp.int32)
     places = turn[:, None] * length + jnp.arange(length, dtype=jnp.int32)[None, :]
@@ -813,11 +962,103 @@
     cosine, sine = rope_tables(order - starts, head)
     starts = starts[None, :]
     place = seq_place.reshape(1).astype(jnp.int32)
+    mix_all, cosine, sine, starts, *cotangent_blocks = tie(
+        mix_all, cosine, sine, starts, *cotangent_blocks
+    )
+    in_block = mix_all[:, : 3 * channels]
+    out_block = unpack_rows(mix_all[:, 3 * channels + 128 :], dp_count)
+    small_all = mix_all[:, 3 * channels : 3 * channels + 128].astype(F32).T
+    kernel = lax.dynamic_slice_in_dim(small_all[:taps], seq_place * channels, channels, 1)
+    gain_mix, gain_ffn_one, gain_attn, gain_ffn_two = (small_all[taps + i] for i in range(4))
+    head_gains = small_all[taps + 4 : taps + 6].reshape(2, dp_count, slots)
+    head_gains = jnp.tile(head_gains[:, :, : head // dp_count].reshape(2, head), (1, 2))
 
     x_flat = x_in.reshape(length, width).astype(F32)
-    unit_one, scale_one = unit_scale(x_flat)
-    normed_one = (unit_scale(x_all.astype(F32))[0] * gain_mix).astype(BF16)
-    projected = plain_dot(normed_one, in_block).reshape(seq_count, length, 3 * channels)
+    normed_one, projected, gated, near_out, far_out = conv_forward(
+        place, bounds, x_blocks, mix_all, out_block, kernel, gain_mix[None, :]
+    )
+    hidden_one = x_flat + seq_scatter(near_out, far_out)
+
+    unit_two, scale_two = unit_scale(hidden_one)
+    near_two = (unit_two * gain_ffn_one).astype(BF16)
+    far_two = far_half(near_two)
+    blocks_two = near_blocks(near_two) + near_blocks(far_two)
+    terms_one, partial_one = ffn_forward(blocks_two, ffn_one, hidden)
+    hidden_two = hidden_one + seq_scatter(*halves_of(partial_one))
+
+    unit_three, scale_three = unit_scale(hidden_two)
+    near_three = (unit_three * gain_attn).astype(BF16)
+    blocks_three = near_blocks(near_three) + near_blocks(far_half(near_three))
+    kv_width = (qkv_width - channels) // 2
+    raw, attended_low, wide, totals, near_out, far_out = attention_forward(
+        place, blocks_three, qkv_block, o_block, cosine, sine, starts, head_gains
+    )
+    hidden_three = hidden_two + seq_scatter(near_out, far_out)
+
+    unit_four, scale_four = unit_scale(hidden_three)
+    near_four = (unit_four * gain_ffn_two).astype(BF16)
+    far_four = far_half(near_four)
+    near_four = near_blocks(near_four)
+    half = len(near_four)
+    kept_two, near_out = ffn_turn(
+        near_four, cotangent_blocks[:half], ffn_two, hidden, 0, None
+    )
+    far_four, near_out = tie(far_four, near_out)
+    far_four = near_blocks(far_four)
+    kept_two, far_out = ffn_turn(
+        far_four, cotangent_blocks[half:], ffn_two, hidden, 1, kept_two
+    )
+
+    grad_four = cotangent.reshape(length, width).astype(F32)
+    kept_two, far_out = tie(kept_two, far_out)
+    normed_four = jnp.concatenate(near_four + far_four, 0)
+    d_gate_up = left_dot(normed_four, kept_two[:, : 2 * hidden]).astype(BF16)
+    d_ffn_in, d_gate_up = seq_scatter(near_out, far_out, d_gate_up)
+    d_hidden, d_gain_ffn_two = norm_back(d_ffn_in, gain_ffn_two, unit_four, scale_four)
+    grad_three = grad_four + d_hidden
+
+    grad_attn = grad_three.astype(BF16)
+    far_attn = far_half(grad_attn)
+    d_down = left_dot(jnp.concatenate(cotangent_blocks, 0), kept_two[:, 2 * hidden :])
+    grads_two = jnp.concatenate([d_gate_up, d_down.astype(BF16)], 1)
+    far_attn, grads_two = tie(far_attn, grads_two)
+    owned_two = dp_scatter(grads_two)
+    grad_blocks = near_blocks(grad_attn) + near_blocks(far_attn)
+    d_raw, near_out, far_out, d_head_gains = attention_backward(
+        place, grad_blocks, qkv_block, o_block, cosine, sine, starts, head_gains,
+        raw, wide, totals,
+    )
+    d_head_gains = d_head_gains[:, :head] + d_head_gains[:, head:]
+    d_qkv = left_dot(jnp.concatenate(blocks_three, 0), d_raw)
+    d_w_o = left_dot(attended_low, jnp.concatenate(grad_blocks, 0))
+    d_w_o = pack_rows(d_w_o.astype(BF16), dp_count)
+    d_attn_in, *grads_attn = seq_scatter(near_out, far_out, d_qkv.astype(BF16), d_w_o)
+    d_attn_h, d_gain_attn = norm_back(d_attn_in, gain_attn, unit_three, scale_three)
+    grad_two = grad_three + d_attn_h
+
+    near_grad = grad_two.astype(BF16)
+    far_grad = far_half(near_grad)
+    near_grad = near_blocks(near_grad)
+    kept_one, near_out = ffn_backward(near_grad, terms_one, ffn_one, hidden, 0, None)
+    far_grad, near_out = tie(far_grad, near_out)
+    far_grad = near_blocks(far_grad)
+    kept_one, far_out = ffn_backward(far_grad, terms_one, ffn_one, hidden, 1, kept_one)
+    kept_one, far_out = tie(kept_one, far_out)
+    d_gate_up = left_dot(jnp.concatenate(blocks_two, 0), kept_one).astype(BF16)
+    d_down = left_dot(
+        jnp.concatenate(near_grad + far_grad, 0), terms_one[:, 2 * hidden :]
+    ).astype(BF16)
+    owned_one = dp_scatter(jnp.concatenate([d_gate_up, *grads_attn], 1))
+    d_ffn_in_one, d_down = seq_scatter(near_out, far_out, d_down)
+    d_hidden_one, d_gain_ffn_one = norm_back(d_ffn_in_one, gain_ffn_one, unit_two, scale_two)
+    grad_one = grad_two + d_hidden_one
+
+    grad_mix = grad_one.astype(BF16)
+    far_mix = far_half(grad_mix)
+    far_mix, d_down = tie(far_mix, d_down)
+    grad_mix = jnp.concatenate([near_half(grad_mix), near_half(far_mix)], 0)
+    grad_mix, owned_two = tie(grad_mix, owned_two)
+    projected = projected.reshape(seq_count, length, 3 * channels)
     part_b = projected[..., :channels]
     part_c = projected[..., channels : 2 * channels]
     part_x = projected[..., 2 * channels :]
@@ -831,94 +1072,6 @@
             conv_out
             + kernel[tap] * extended[:, reach - tap : reach - tap + length] * masks[tap - 1]
         )
-    gated = (part_c * conv_out).astype(BF16).reshape(full, channels)
-    hidden_one = x_flat + seq_scatter(*halves_of(plain_dot(gated, out_block)))
-
-    unit_two, scale_two = unit_scale(hidden_one)
-    near_two = (unit_two * gain_ffn_one).astype(BF16)
-    far_two = far_half(near_two)
-    near_two = near_half(near_two)
-    terms_one, near_out = ffn_forward(near_two, ffn_one, hidden, length, 0, None)
-    far_two, near_out = tie(far_two, near_out)
-    far_two = near_half(far_two)
-    terms_one, far_out = ffn_forward(far_two, ffn_one, hidden, length, 1, terms_one)
-    hidden_two = hidden_one + seq_scatter(near_out, far_out)
-
-    unit_three, scale_three = unit_scale(hidden_two)
-    normed_three = (unit_three * gain_attn).astype(BF16)
-    normed_three = jnp.concatenate(
-        [near_half(normed_three), near_half(far_half(normed_three))], 0
-    )
-    raw = plain_dot(normed_three, qkv_block)
-    kv_width = (qkv_width - channels) // 2
-    attended_low, wide, totals = attention_forward(
-        place, raw, cosine, sine, starts, head_gains, length
-    )
-    hidden_three = hidden_two + seq_scatter(*halves_of(plain_dot(attended_low, o_block)))
-
-    unit_four, scale_four = unit_scale(hidden_three)
-    near_four = (unit_four * gain_ffn_two).astype(BF16)
-    far_four = far_half(near_four)
-    near_four = near_half(near_four)
-    kept_two, near_out = ffn_turn(near_four, cotangent_halves[0], ffn_two, hidden, length, 0, None)
-    far_four, near_out = tie(far_four, near_out)
-    far_four = near_half(far_four)
-    kept_two, far_out = ffn_turn(far_four, cotangent_halves[1], ffn_two, hidden, length, 1, kept_two)
-
-    grad_four = cotangent.reshape(length, width).astype(F32)
-    kept_two, far_out = tie(kept_two, far_out)
-    normed_four = jnp.concatenate([near_four, far_four], 0)
-    d_gate_up = left_dot(normed_four, kept_two[:, : 2 * hidden]).astype(BF16)
-    d_ffn_in, d_gate_up = seq_scatter(near_out, far_out, d_gate_up)
-    d_hidden, d_gain_ffn_two = norm_back(d_ffn_in, gain_ffn_two, unit_four, scale_four)
-    grad_three = grad_four + d_hidden
-
-    grad_attn = grad_three.astype(BF16)
-    far_attn = far_half(grad_attn)
-    d_down = left_dot(jnp.concatenate(cotangent_halves, 0), kept_two[:, 2 * hidden :])
-    grads_two = jnp.concatenate([d_gate_up, d_down.astype(BF16)], 1)
-    far_attn, grads_two = tie(far_attn, grads_two)
-    owned_two = dp_scatter(grads_two)
-    grad_attn = jnp.concatenate([near_half(grad_attn), near_half(far_attn)], 0)
-    d_w_o = left_dot(attended_low, grad_attn)
-    d_attended = right_dot(grad_attn, o_block).astype(BF16)
-    d_raw, d_head_gains = attention_backward(
-        place, raw, cosine, sine, starts, head_gains, wide, totals, d_attended, length
-    )
-    d_head_gains = d_head_gains[:, :head] + d_head_gains[:, head:]
-    partial_attn = right_dot(d_raw, qkv_block)
-    d_raw, partial_attn = tie(d_raw, partial_attn)
-    d_qkv = left_dot(normed_three, d_raw)
-    grads_attn = jnp.concatenate(
-        [d_qkv.astype(BF16), d_w_o.astype(BF16).reshape(width, channels)], 1
-    )
-    d_attn_in, grads_attn = seq_scatter(*halves_of(partial_attn), grads_attn)
-    d_attn_h, d_gain_attn = norm_back(d_attn_in, gain_attn, unit_three, scale_three)
-    grad_two = grad_three + d_attn_h
-
-    owned_attn = dp_scatter_small(grads_attn)
-    near_grad = grad_two.astype(BF16)
-    far_grad = far_half(near_grad)
-    near_grad = near_half(near_grad)
-    kept_one, near_out = ffn_backward(near_grad, terms_one, ffn_one, hidden, length, 0, None)
-    far_grad, near_out = tie(far_grad, near_out)
-    far_grad = near_half(far_grad)
-    kept_one, far_out = ffn_backward(far_grad, terms_one, ffn_one, hidden, length, 1, kept_one)
-    kept_one, far_out = tie(kept_one, far_out)
-    d_gate_up = left_dot(jnp.concatenate([near_two, far_two], 0), kept_one).astype(BF16)
-    d_ffn_in_one, d_gate_up, owned_attn = seq_scatter(near_out, far_out, d_gate_up, owned_attn)
-    d_hidden_one, d_gain_ffn_one = norm_back(d_ffn_in_one, gain_ffn_one, unit_two, scale_two)
-    grad_one = grad_two + d_hidden_one
-
-    grad_mix = grad_one.astype(BF16)
-    far_mix = far_half(grad_mix)
-    d_down = left_dot(
-        jnp.concatenate([near_grad, far_grad], 0), terms_one[:, 2 * hidden :]
-    ).astype(BF16)
-    far_mix, grads_one = tie(far_mix, jnp.concatenate([d_gate_up, d_down], 1))
-    owned_one = dp_scatter(grads_one)
-    grad_mix = jnp.concatenate([near_half(grad_mix), near_half(far_mix)], 0)
-    grad_mix, owned_two = tie(grad_mix, owned_two)
     d_w_out = left_dot(gated, grad_mix)
     d_gated = right_dot(grad_mix, out_block).reshape(seq_count, length, channels)
     d_part_c = d_gated * conv_out
@@ -937,12 +1090,9 @@
     d_product = lax.optimization_barrier(d_product_sum.astype(BF16)).astype(F32)
     d_projected = jnp.concatenate([d_product * part_x, d_part_c, d_product * part_b], -1)
     d_projected = d_projected.astype(BF16).reshape(full, 3 * channels)
-    kept_two, d_projected = tie(kept_two, d_projected)
-    ffn_out = right_dot(kept_two[:, 2 * hidden :], ffn_two[:, 2 * hidden :])
-    hidden_four = hidden_three + seq_scatter(*halves_of(ffn_out))
-    out = hidden_four.astype(BF16).reshape(rows, length, width)
     d_w_in = left_dot(normed_one, d_projected)
     d_normed = seq_scatter(*halves_of(right_dot(d_projected, in_block)))
+    unit_one, scale_one = unit_scale(x_flat)
     d_x_part, d_gain_mix = norm_back(d_normed, gain_mix, unit_one, scale_one)
     d_x = (grad_one + d_x_part).reshape(rows, length, width)
 
@@ -964,37 +1114,46 @@
     vector_columns = jnp.pad(vectors.T, ((0, 0), (0, 128 - vectors.shape[0])))
     grads_mix = jnp.concatenate(
         [
+            d_down,
             d_w_in.astype(BF16),
             vector_columns.astype(BF16),
-            d_w_out.astype(BF16).reshape(width, channels),
+            pack_rows(d_w_out.astype(BF16), dp_count),
         ],
         1,
     )
-    owned_mix = dp_scatter_small(grads_mix)
-
-    def redeal(owned):
-        block = owned[:, owned.shape[1] - channels :].reshape(-1, width)
-        back = undeal_rows(block).reshape(slots, channels)
-        return jnp.concatenate([owned[:, : owned.shape[1] - channels], back], 1)
-
-    attn_cut = owned_attn.shape[1]
-    shared_small = share(jnp.concatenate([redeal(owned_attn), redeal(owned_mix)], 1))
-    (d_w_q, d_w_k, d_w_v), _ = split_columns(
-        shared_small, [(1, channels), (1, kv_width), (1, kv_width)]
-    )
-    (d_w_in_full,), rest_mix = split_columns(
-        [b[:, attn_cut:] for b in shared_small], [(3, channels)]
-    )
-    rest_attn = [b[:, attn_cut - channels : attn_cut] for b in shared_small]
-    (d_wgate_two, d_wup_two, d_down_two), _ = split_columns(share(owned_two), [(1, hidden)] * 3)
-    owned_one, d_wgate_two, d_wup_two, d_down_two, out = tie(
-        owned_one, d_wgate_two, d_wup_two, d_down_two, out
-    )
-    (d_wgate_one, d_wup_one, d_down_one), _ = split_columns(share(owned_one), [(1, hidden)] * 3)
-    d_w_o_full = jnp.concatenate([b.reshape(-1, width) for b in rest_attn], 0).astype(F32)
-    d_w_out_full = jnp.concatenate([b[:, 128:].reshape(-1, width) for b in rest_mix], 0)
-    d_w_out_full = d_w_out_full.astype(F32)
-    sums = sum(b[:, :128].astype(F32) for b in rest_mix).T
+    grads_mix, owned_one = tie(grads_mix, owned_one)
+    owned_mix = dp_scatter(grads_mix)
+
+    def redeal(block):
+        return pack_piece(undeal_rows(unpack_piece(block, width)), channels)
+
+    owned_two, owned_one, kept_two = tie(owned_two, owned_one, kept_two)
+    ffn_out = right_dot(kept_two[:, 2 * hidden :], ffn_two[:, 2 * hidden :])
+    hidden_four = hidden_three + seq_scatter(*halves_of(ffn_out))
+    out = hidden_four.astype(BF16).reshape(rows, length, width)
+    d_wgate_two, d_wup_two, d_down_two = assemble(
+        place, share(owned_two), [(n * hidden, hidden, 1, False) for n in range(3)]
+    )
+    tasks = [(n * hidden, hidden, 1, False) for n in range(2)]
+    for columns in (channels, kv_width, kv_width):
+        tasks.append((tasks[-1][0] + tasks[-1][1], columns, 1, False))
+    d_wgate_one, d_wup_one, d_w_q, d_w_k, d_w_v = assemble(
+        place, share(owned_one[:, :-channels]), tasks
+    )
+    (d_w_o_full,) = assemble(
+        place, share(redeal(owned_one[:, -channels:])), [(0, channels, 1, True)]
+    )
+    owned_mix, out, d_x, d_wgate_two, d_wup_two, d_down_two, d_wgate_one, d_w_o_full = tie(
+        owned_mix, out, d_x, d_wgate_two, d_wup_two, d_down_two, d_wgate_one, d_w_o_full
+    )
+    shared_mix = share(owned_mix[:, :-channels])
+    shared_out = share(redeal(owned_mix[:, -channels:]))
+    d_down_one, d_w_in_full = assemble(
+        place, shared_mix, [(0, hidden, 1, False), (hidden, 3 * channels, 3, False)]
+    )
+    (d_w_out_full,) = assemble(place, shared_out, [(0, channels, 1, True)])
+    vectors_all = [block[:, hidden + 3 * channels :] for block in shared_mix]
+    sums = sum(block.astype(F32) for block in vectors_all).T
     small_head = head // dp_count
     return (
         out,

time: 817 us -> 786 us (0.962)
  other arithmetic: 96.2 us -> 64.3 us
  starting transfers between devices: 97.1 us -> 66.5 us
  waiting for transfers between devices: 307 us -> 332 us
  Pallas kernels: 130 us -> 154 us
  matrix products: 86.5 us -> 73 us
    ppermute x21 -> x3, waiting for transfers between devices: 96.7 us -> 24.7 us  [swap_dp(): return lax.ppermute(array, 'dp', [(i, i ^ bit) for i in range(size)])]
    ppermute x57 -> x63, waiting for transfers between devices: 188 us -> 247 us  [swap_seq(): return lax.ppermute(array, 'seq', [(i, i ^ bit) for i in range(size)])]
    reduce_scatter x2 -> x3, waiting for transfers between devices: 0.02 us -> 51.7 us  [dp_scatter(): return lax.psum_scatter(grads, 'dp', scatter_dimension=0, tiled=True)]
    convert_element_type x18 -> x1, other arithmetic: 22.3 us -> 0.19 us  [local(): near_three = (unit_three * gain_attn).astype(BF16)]
    pallas_call x6 -> x11, Pallas kernels: 71.6 us -> 89.1 us  [the longest x5 68.5 us: ffn_call(): pl.pallas_call(lambda *refs: kernel(*refs, count=count), grid=(count,), i...]
    ppermute x57 -> x63, starting transfers between devices: 61.6 us -> 45 us  [swap_seq(): return lax.ppermute(array, 'seq', [(i, i ^ bit) for i in range(size)])]
    all_gather x2, waiting for transfers between devices: 22.5 us -> 8.4 us  [dp_gather(): return lax.all_gather(block, 'dp', axis=0, tiled=True)]
    ppermute x21 -> x3, starting transfers between devices: 31.4 us -> 18.8 us  [swap_dp(): return lax.ppermute(array, 'dp', [(i, i ^ bit) for i in range(size)])]
  transfers between devices with their start and end apart: 85 -> 74, of which waited for: 43 -> 39; matrix products, arithmetic and copies ran while one was open for 27% -> 23% of each run, Pallas kernels for 14% -> 18%
where the time goes in v3:
time: 786 us; the launch traced here: 775 us
  waiting for transfers between devices  332 us (42%)
  Pallas kernels  154 us (20%)
  matrix products  73 us (9%)
  local copies, waits for them, and re-layouts  68.8 us (9%)
  starting transfers between devices  66.5 us (8%)
  other arithmetic  64.3 us (8%)
  between operations  15.7 us (2%)
    ppermute x63, waiting for transfers between devices, swap_seq(): return lax.ppermute(array, 'seq', [(i, i ^ bit) for i in range(size)])  247 us
    pallas_call x5, Pallas kernels, ffn_call(): pl.pallas_call(lambda *refs: kernel(*refs, count=count), grid=(count,), i...  68.5 us
    dot_general x8, matrix products, left_dot(): lax.dot_general(left, right, (((0,), (0,)), ((), ())), preferred_element_...  55.5 us
    reduce_scatter x3, waiting for transfers between devices, dp_scatter(): return lax.psum_scatter(grads, 'dp', scatter_dimension=0, tiled=True)  51.7 us
    ppermute x63, starting transfers between devices, swap_seq(): return lax.ppermute(array, 'seq', [(i, i ^ bit) for i in range(size)])  45 us
    pallas_call x1, Pallas kernels, attention_backward(): pl.pallas_call(lambda *refs: attention_backward_kernel(*refs, length=leng...  38.2 us
    unnamed x204, local copies, waits for them, and re-layouts  29.8 us
    pallas_call x1, Pallas kernels, attention_forward(): pl.pallas_call(lambda *refs: attention_forward_kernel(*refs, length=lengt...  26.7 us
  transfers between devices with their start and end apart: 74, of which 39 were waited for; matrix products, arithmetic and copies ran while one was open for 23% of the time, Pallas kernels for 18%

profile of v3, /device:TPU:0, one launch (start us, length us, event | category | flops | bytes accessed | tf_op | source)
XLA Modules:
  0.0 774.7 jit_solution(10902853231852857588)
XLA Ops:
  11.6 10.7 %collective-permute-start.4 = (bf16[128,1152]{0,1:T(8,128)(2,1)S(1)}, bf16[128,1152]{0,1:T(8,128)(2,1)S(1)}, u32[]{:S(2)}, u32[]{:S(2)}) collective-permute-start(bf16[128,1152]{0,1:T(8,128)(2,1)S(1)} %fusion.87), channel_id=1, source_target_pairs={{0,4},{1,5},{2,6},{3,7},{4,0},{5,1},{6,2},{7,3},{8,12},{9,13},{10,... | collective-permute-start | bytes 884744 | tf_op jit(solution)/shard_map/ppermute | solution.py:554
  74.7 17.7 %collective-permute-done.8.refs_2_ = bf16[384,1024]{1,0:T(8,128)(2,1)S(1)} collective-permute-done((bf16[384,1024]{1,0:T(8,128)(2,1)S(1)}, bf16[384,1024]{1,0:T(8,128)(2,1)S(1)}, u32[]{:S(2)}, u32[]{:S(2)}) %collective-permute-start.8) | collective-permute-done | bytes 786464 | tf_op jit(solution)/shard_map/ppermute | solution.py:76
  92.4 9.0 %collective-permute-done.6 = bf16[512,1152]{0,1:T(8,128)(2,1)S(1)} collective-permute-done((bf16[512,1152]{0,1:T(8,128)(2,1)S(1)}, bf16[512,1152]{0,1:T(8,128)(2,1)S(1)}, u32[]{:S(2)}, u32[]{:S(2)}) %collective-permute-start.6) | collective-permute-done | bytes 1179680 | tf_op jit(solution)/shard_map/ppermute | solution.py:554
  116.1 10.2 %conv_forward.1 = (bf16[1536,1024]{1,0:T(8,128)(2,1)}, f32[1536,768]{1,0:T(8,128)}, bf16[1536,256]{1,0:T(8,128)(2,1)S(1)}, bf16[768,1024]{1,0:T(8,128)(2,1)S(1)}, bf16[768,1024]{1,0:T(8,128)(2,1)}) custom-call(s32[1]{0:T(128)} %bitcast.2.refs_0_, s32[4]{0:T(128)S(1)} %bitcast.177, bf16[384,1024]{1,0:T(8,128)(2,1)S(1)} %bitcast.166, ...), custom_call_target="tpu_custom_call" | custom-call | flops 4000000000 | bytes 20000000 | tf_op jit(solution)/shard_map/conv_forward/pallas_call | solution.py:858
  136.2 15.7 %collective-permute-done.11 = bf16[384,1024]{1,0:T(8,128)(2,1)} collective-permute-done((bf16[384,1024]{1,0:T(8,128)(2,1)}, bf16[384,1024]{1,0:T(8,128)(2,1)}, u32[]{:S(2)}, u32[]{:S(2)}) %collective-permute-start.11) | collective-permute-done | bytes 786464 | tf_op jit(solution)/shard_map/ppermute | solution.py:76
  155.8 17.5 %collective-permute-done.14.refs_2_ = bf16[384,1024]{1,0:T(8,128)(2,1)S(1)} collective-permute-done((bf16[384,1024]{1,0:T(8,128)(2,1)S(1)}, bf16[384,1024]{1,0:T(8,128)(2,1)S(1)}, u32[]{:S(2)}, u32[]{:S(2)}) %collective-permute-start.14) | collective-permute-done | bytes 786464 | tf_op jit(solution)/shard_map/ppermute | solution.py:76
  187.2 18.2 %ffn_forward.1 = (bf16[1536,3456]{1,0:T(8,128)(2,1)}, bf16[1536,1024]{1,0:T(8,128)(2,1)}) custom-call(bf16[384,1024]{1,0:T(8,128)(2,1)S(1)} %multiply_convert_fusion.4.refs_0_, bf16[384,1024]{1,0:T(8,128)(2,1)S(1)} %copy-done.18, bf16[384,1024]{1,0:T(8,128)(2,1)S(1)} %collective-permute-done.14.refs_2_, bf16[384,1024]{1,0:T(8,128)(2,1)S(1)} %copy-done.21, ...), custom_call_target="tpu_custom_call" | custom-call | flops 6000000000 | bytes 20000000 | tf_op jit(solution)/shard_map/ffn_forward/pallas_call | solution.py:729
  212.6 18.1 %collective-permute-done.17 = bf16[384,1024]{1,0:T(8,128)(2,1)S(1)} collective-permute-done((bf16[384,1024]{1,0:T(8,128)(2,1)S(1)}, bf16[384,1024]{1,0:T(8,128)(2,1)S(1)}, u32[]{:S(2)}, u32[]{:S(2)}) %collective-permute-start.17) | collective-permute-done | bytes 786464 | tf_op jit(solution)/shard_map/ppermute | solution.py:76
  233.2 17.4 %collective-permute-done.20.refs_3_ = bf16[384,1024]{1,0:T(8,128)(2,1)} collective-permute-done((bf16[384,1024]{1,0:T(8,128)(2,1)S(1)}, bf16[384,1024]{1,0:T(8,128)(2,1)}, u32[]{:S(2)}, u32[]{:S(2)}) %collective-permute-start.20) | collective-permute-done | bytes 786464 | tf_op jit(solution)/shard_map/ppermute | solution.py:76
  255.8 26.7 %attention_forward.1 = (f32[1536,512]{1,0:T(8,128)}, bf16[1536,256]{1,0:T(8,128)(2,1)S(1)}, f32[256,1536]{1,0:T(8,128)}, f32[8,1536]{1,0:T(8,128)S(1)}, bf16[768...) custom-call(s32[1]{0:T(128)} %bitcast.2.refs_0_, bf16[384,1024]{1,0:T(8,128)(2,1)S(1)} %multiply_convert_fusion.3.refs_1_, ...), custom_call_target="tpu_custom_call" | custom-call | flops 20000000000 | bytes 20000000 | tf_op jit(solution)/shard_map/attention_forward/pallas_call | solution.py:425
  288.7 18.0 %collective-permute-done.23 = bf16[384,1024]{1,0:T(8,128)(2,1)S(1)} collective-permute-done((bf16[384,1024]{1,0:T(8,128)(2,1)S(1)}, bf16[384,1024]{1,0:T(8,128)(2,1)S(1)}, u32[]{:S(2)}, u32[]{:S(2)}) %collective-permute-start.23) | collective-permute-done | bytes 786464 | tf_op jit(solution)/shard_map/ppermute | solution.py:76
  310.6 14.6 %ffn_turn.2 = (bf16[1536,3456]{1,0:T(8,128)(2,1)}, bf16[768,1024]{1,0:T(8,128)(2,1)S(1)}) custom-call(bf16[384,1024]{1,0:T(8,128)(2,1)S(1)} %multiply_convert_fusion.2.refs_0_, bf16[384,1024]{1,0:T(8,128)(2,1)} %collective-permute-done.26.refs_1_, bf16[384,1024]{1,0:T(8,128)(2,1)S(1)} %bitcast.169, bf16[384,1024]{1,0:T(8,128)(2,1)S(1)} %collective-permute-done.7.refs_3_, ...), custom_call_target="tpu_custom_call" | custom-call | flops 6000000000 | bytes 20000000 | tf_op jit(solution)/shard_map/ffn_turn/pallas_call | solution.py:729
  330.8 14.4 %ffn_turn.3 = (bf16[1536,3456]{1,0:T(8,128)(2,1)}, bf16[768,1024]{1,0:T(8,128)(2,1)S(1)}) custom-call(bf16[384,1024]{1,0:T(8,128)(2,1)} %collective-permute-done.25.refs_0_, bf16[384,1024]{1,0:T(8,128)(2,1)S(1)} %collective-permute-done.27.refs_1_, bf16[384,1024]{1,0:T(8,128)(2,1)S(1)} %copy-done.24, ...), custom_call_target="tpu_custom_call", output_to_operand_aliasing={{0}: (7, {})} | custom-call | flops 6000000000 | bytes 20000000 | tf_op jit(solution)/shard_map/ffn_turn/pallas_call | solution.py:729
  349.4 12.9 %fusion.4 = bf16[1024,2304]{1,0:T(8,128)(2,1)} fusion(bf16[1536,3456]{1,0:T(8,128)(2,1)} %get-tuple-element.192, bf16[384,1024]{1,0:T(8,128)(2,1)S(1)} %collective-permute-done.27.refs_1_, bf16[384,1024]{1,0:T(8,128)(2,1)} %collective-permute-done.25.refs_0_, bf16[384,1024]{1,0:T(8,128)(2,1)} %collective-permute-done.26.refs_1_, ...), kind=kOutput, calls=%fused_computation.9 | convolution fusion | flops 7262699520 | bytes 14942208 | tf_op jit(solution)/shard_map/dot_general | solution.py:19
  392.9 38.2 %attention_backward.1 = (bf16[1536,512]{1,0:T(8,128)(2,1)}, bf16[768,1024]{1,0:T(8,128)(2,1)}, bf16[768,1024]{1,0:T(8,128)(2,1)}, f32[2,128]{1,0:T(2,128)S(1)}) custom-call(s32[1]{0:T(128)} %bitcast.2.refs_0_, bf16[384,1024]{1,0:T(8,128)(2,1)} %get-tuple-element.347.refs_1_, bf16[384,1024]{1,0:T(8,128)(2,1)S(1)} %collective-permute-done.31.refs_2_, ...), custom_call_target="tpu_custom_call" | custom-call | flops 20000000000 | bytes 20000000 | tf_op jit(solution)/shard_map/attention_backward/pallas_call | solution.py:457
  447.5 13.7 %collective-permute-done.35 = bf16[384,1024]{1,0:T(8,128)(2,1)S(1)} collective-permute-done((bf16[384,1024]{1,0:T(8,128)(2,1)S(1)}, bf16[384,1024]{1,0:T(8,128)(2,1)S(1)}, u32[]{:S(2)}, u32[]{:S(2)}) %collective-permute-start.35) | collective-permute-done | bytes 786464 | tf_op jit(solution)/shard_map/ppermute | solution.py:76
  466.6 10.5 %ffn_backward.2 = (bf16[1536,2304]{1,0:T(8,128)(2,1)}, bf16[768,1024]{1,0:T(8,128)(2,1)S(1)}) custom-call(bf16[384,1024]{1,0:T(8,128)(2,1)S(1)} %get-tuple-element.345.refs_0_, bf16[384,1024]{1,0:T(8,128)(2,1)S(1)} %collective-permute-done.38.refs_1_, bf16[1536,3456]{1,0:T(8,128)(2,1)} %get-tuple-element.167.refs_2_, ...), custom_call_target="tpu_custom_call" | custom-call | flops 6000000000 | bytes 20000000 | tf_op jit(solution)/shard_map/ffn_backward/pallas_call | solution.py:729
  488.2 10.8 %ffn_backward.3 = (bf16[1536,2304]{1,0:T(8,128)(2,1)}, bf16[768,1024]{1,0:T(8,128)(2,1)S(1)}) custom-call(bf16[384,1024]{1,0:T(8,128)(2,1)} %collective-permute-done.37.refs_0_, bf16[384,1024]{1,0:T(8,128)(2,1)} %collective-permute-done.39.refs_1_, bf16[1536,3456]{1,0:T(8,128)(2,1)} %get-tuple-element.167.refs_2_, ...), custom_call_target="tpu_custom_call", output_to_operand_aliasing={{0}: (6, {})} | custom-call | flops 6000000000 | bytes 20000000 | tf_op jit(solution)/shard_map/ffn_backward/pallas_call | solution.py:729
  501.3 10.9 %convolution_convert_fusion = bf16[1024,2304]{1,0:T(8,128)(2,1)S(1)} fusion(bf16[1536,2304]{1,0:T(8,128)(2,1)} %get-tuple-element.186, bf16[384,1024]{1,0:T(8,128)(2,1)S(1)} %copy-done.22, bf16[384,1024]{1,0:T(8,128)(2,1)S(1)} %copy-done.16, bf16[384,1024]{1,0:T(8,128)(2,1)S(1)} %copy-done.19, bf16[384,1024]{1,0:T(8,128)(2,1)S(1)} %multiply_convert_fusion.4.refs_0_), kind=kOutput, calls=%fused_computation.8 | convolution fusion | flops 7262699520 | bytes 14942208 | tf_op jit(solution)/shard_map/dot_general | solution.py:19
  530.5 9.7 %collective-permute-done.41 = bf16[384,1024]{1,0:T(8,128)(2,1)S(1)} collective-permute-done((bf16[384,1024]{1,0:T(8,128)(2,1)S(1)}, bf16[384,1024]{1,0:T(8,128)(2,1)S(1)}, u32[]{:S(2)}, u32[]{:S(2)}) %collective-permute-start.41) | collective-permute-done | bytes 786464 | tf_op jit(solution)/shard_map/ppermute | solution.py:76
  545.3 15.9 %collective-permute-done.43 = bf16[384,1024]{1,0:T(8,128)(2,1)S(1)} collective-permute-done((bf16[384,1024]{1,0:T(8,128)(2,1)S(1)}, bf16[384,1024]{1,0:T(8,128)(2,1)S(1)}, u32[]{:S(2)}, u32[]{:S(2)}) %collective-permute-start.43) | collective-permute-done | bytes 786464 | tf_op jit(solution)/shard_map/ppermute | solution.py:76
  616.0 21.4 %reduce-scatter.6.cloned.1.call-done = bf16[128,3072]{1,0:T(8,128)(2,1)} async-done(((bf16[1024,3072]{1,0:T(8,128)(2,1)}), bf16[128,3072]{1,0:T(8,128)(2,1)}) %reduce-scatter.6.cloned.1.call-update) | async-done | bytes 786448 | tf_op jit(solution)/shard_map/reduce_scatter | solution.py:549
  657.7 31.1 %collective-permute-done.60.refs_3_ = bf16[128,256]{1,0:T(8,128)(2,1)S(1)} collective-permute-done((bf16[128,256]{1,0:T(8,128)(2,1)S(1)}, bf16[128,256]{1,0:T(8,128)(2,1)S(1)}, u32[]{:S(2)}, u32[]{:S(2)}) %collective-permute-start.60) | collective-permute-done | bytes 65568 | tf_op jit(solution)/shard_map/ppermute | solution.py:76
  709.8 30.2 %reduce-scatter.8.cloned.1.call-done = bf16[128,2304]{1,0:T(8,128)(2,1)} async-done(((bf16[1024,2304]{1,0:T(8,128)(2,1)}), bf16[128,2304]{1,0:T(8,128)(2,1)}) %reduce-scatter.8.cloned.1.call-update) | async-done | bytes 589840 | tf_op jit(solution)/shard_map/reduce_scatter | solution.py:549
  (533 shorter events, 345.4 us)
Async XLA Ops:
  7.3 177.6 %all-gather.3.cloned.1.call-start = ((), (), s32[]{:S(2)}) async-start(), calls=%async_computation.3 | async-start | bytes 9732096 | tf_op jit(solution)/shard_map/all_gather | solution.py:545
  11.6 22.1 %collective-permute-start.4 = (bf16[128,1152]{0,1:T(8,128)(2,1)S(1)}, bf16[128,1152]{0,1:T(8,128)(2,1)S(1)}, u32[]{:S(2)}, u32[]{:S(2)}) collective-permute-start(bf16[128,1152]{0,1:T(8,128)(2,1)S(1)} %fusion.87), channel_id=1, source_target_pairs={{0,4},{1,5},{2,6},{3,7},{4,0},{5,1},{6,2},{7,3},{8,12},{9,13},{10,... | collective-permute-start | bytes 884744 | tf_op jit(solution)/shard_map/ppermute | solution.py:554
  52.6 257.1 %all-gather.5.cloned.1.call-start = ((), (), s32[]{:S(2)}) async-start(), calls=%async_computation.4 | async-start | bytes 7962624 | tf_op jit(solution)/shard_map/all_gather | solution.py:545
  53.4 62.7 %collective-permute-start = (bf16[384,1024]{1,0:T(8,128)(2,1)S(1)}, bf16[384,1024]{1,0:T(8,128)(2,1)}, u32[]{:S(2)}, u32[]{:S(2)}) collective-permute-start(bf16[384,1024]{1,0:T(8,128)(2,1)S(1)} %bitcast.165), channel_id=1, source_target_pairs={{0,8},{8,0},{16,24},{24,16},{1,9},{9,1},{17,25},{25,17},{2,10},{10... | collective-permute-start | bytes 2359304 | tf_op jit(solution)/shard_map/ppermute | solution.py:76
  61.2 40.2 %collective-permute-start.6 = (bf16[512,1152]{0,1:T(8,128)(2,1)S(1)}, bf16[512,1152]{0,1:T(8,128)(2,1)S(1)}, u32[]{:S(2)}, u32[]{:S(2)}) collective-permute-start(bf16[512,1152]{0,1:T(8,128)(2,1)S(1)} %pad_maximum_fusion.4), channel_id=1, source_target_pairs={{0,1},{1,0},{2,3},{3,2},{4,5},{5,4},{6,7},{7,6},{8,9},{9,8},{10,11... | collective-permute-start | bytes 3538952 | tf_op jit(solution)/shard_map/ppermute | solution.py:554
  74.0 27.9 %collective-permute-start.7 = (bf16[384,1024]{1,0:T(8,128)(2,1)S(1)}, bf16[384,1024]{1,0:T(8,128)(2,1)S(1)}, u32[]{:S(2)}, u32[]{:S(2)}) collective-permute-start(bf16[384,1024]{1,0:T(8,128)(2,1)S(1)} %bitcast.168), channel_id=1, source_target_pairs={{0,8},{8,0},{16,24},{24,16},{1,9},{9,1},{17,25},{25,17},{2,10},{10... | collective-permute-start | bytes 2359304 | tf_op jit(solution)/shard_map/ppermute | solution.py:76
  74.0 42.1 %collective-permute-start.2 = (bf16[384,1024]{1,0:T(8,128)(2,1)}, bf16[384,1024]{1,0:T(8,128)(2,1)}, u32[]{:S(2)}, u32[]{:S(2)}) collective-permute-start(bf16[384,1024]{1,0:T(8,128)(2,1)} %copy-done.34), channel_id=1, source_target_pairs={{0,8},{8,0},{16,24},{24,16},{1,9},{9,1},{17,25},{25,17},{2,10},{10... | collective-permute-start | bytes 2359304 | tf_op jit(solution)/shard_map/ppermute | solution.py:76
  131.9 20.0 %collective-permute-start.11 = (bf16[384,1024]{1,0:T(8,128)(2,1)}, bf16[384,1024]{1,0:T(8,128)(2,1)}, u32[]{:S(2)}, u32[]{:S(2)}) collective-permute-start(bf16[384,1024]{1,0:T(8,128)(2,1)} %add_convert_fusion.6), channel_id=1, source_target_pairs={{0,16},{8,24},{16,0},{24,8},{1,17},{9,25},{17,1},{25,9},{2,18},{10... | collective-permute-start | bytes 2359304 | tf_op jit(solution)/shard_map/ppermute | solution.py:76
  134.3 431.4 %reduce-scatter.4.cloned.1.call-start = ((), (), s32[]{:S(2)}) async-start(), calls=%async_computation.5 | async-start | bytes 7962624 | tf_op jit(solution)/shard_map/reduce_scatter | solution.py:549
  211.1 19.6 %collective-permute-start.17 = (bf16[384,1024]{1,0:T(8,128)(2,1)S(1)}, bf16[384,1024]{1,0:T(8,128)(2,1)S(1)}, u32[]{:S(2)}, u32[]{:S(2)}) collective-permute-start(bf16[384,1024]{1,0:T(8,128)(2,1)S(1)} %get-tuple-element.367), channel_id=1, source_target_pairs={{0,16},{8,24},{16,0},{24,8},{1,17},{9,25},{17,1},{25,9},{2,18},{10... | collective-permute-start | bytes 2359304 | tf_op jit(solution)/shard_map/ppermute | solution.py:76
  233.2 22.6 %collective-permute-start.19 = (bf16[384,1024]{1,0:T(8,128)(2,1)S(1)}, bf16[384,1024]{1,0:T(8,128)(2,1)}, u32[]{:S(2)}, u32[]{:S(2)}) collective-permute-start(bf16[384,1024]{1,0:T(8,128)(2,1)S(1)} %multiply_convert_fusion.3.refs_1_), channel_id=1, source_target_pairs={{0,8},{8,0},{16,24},{24,16},{1,9},{9,1},{17,25},{25,17},{2,10},{10... | collective-permute-start | bytes 2359304 | tf_op jit(solution)/shard_map/ppermute | solution.py:76
  286.9 19.9 %collective-permute-start.23 = (bf16[384,1024]{1,0:T(8,128)(2,1)S(1)}, bf16[384,1024]{1,0:T(8,128)(2,1)S(1)}, u32[]{:S(2)}, u32[]{:S(2)}) collective-permute-start(bf16[384,1024]{1,0:T(8,128)(2,1)S(1)} %add_convert_fusion.4), channel_id=1, source_target_pairs={{0,16},{8,24},{16,0},{24,8},{1,17},{9,25},{17,1},{25,9},{2,18},{10... | collective-permute-start | bytes 2359304 | tf_op jit(solution)/shard_map/ppermute | solution.py:76
  308.2 20.1 %collective-permute-start.25 = (bf16[384,1024]{1,0:T(8,128)(2,1)S(1)}, bf16[384,1024]{1,0:T(8,128)(2,1)}, u32[]{:S(2)}, u32[]{:S(2)}) collective-permute-start(bf16[384,1024]{1,0:T(8,128)(2,1)S(1)} %multiply_convert_fusion.2.refs_0_), channel_id=1, source_target_pairs={{0,16},{8,24},{16,0},{24,8},{1,17},{9,25},{17,1},{25,9},{2,18},{10... | collective-permute-start | bytes 2359304 | tf_op jit(solution)/shard_map/ppermute | solution.py:76
  389.1 248.3 %reduce-scatter.6.cloned.1.call-start = ((), (), s32[]{:S(2)}) async-start(), calls=%async_computation.6 | async-start | bytes 7077888 | tf_op jit(solution)/shard_map/reduce_scatter | solution.py:549
  441.3 19.9 %collective-permute-start.35 = (bf16[384,1024]{1,0:T(8,128)(2,1)S(1)}, bf16[384,1024]{1,0:T(8,128)(2,1)S(1)}, u32[]{:S(2)}, u32[]{:S(2)}) collective-permute-start(bf16[384,1024]{1,0:T(8,128)(2,1)S(1)} %add_convert_fusion.2), channel_id=1, source_target_pairs={{0,16},{8,24},{16,0},{24,8},{1,17},{9,25},{17,1},{25,9},{2,18},{10... | collective-permute-start | bytes 2359304 | tf_op jit(solution)/shard_map/ppermute | solution.py:76
  464.4 20.1 %collective-permute-start.37 = (bf16[384,1024]{1,0:T(8,128)(2,1)S(1)}, bf16[384,1024]{1,0:T(8,128)(2,1)}, u32[]{:S(2)}, u32[]{:S(2)}) collective-permute-start(bf16[384,1024]{1,0:T(8,128)(2,1)S(1)} %get-tuple-element.345.refs_0_), channel_id=1, source_target_pairs={{0,16},{8,24},{16,0},{24,8},{1,17},{9,25},{17,1},{25,9},{2,18},{10... | collective-permute-start | bytes 2359304 | tf_op jit(solution)/shard_map/ppermute | solution.py:76
  487.7 29.9 %collective-permute-start.42 = (bf16[384,1024]{1,0:T(8,128)(2,1)}, bf16[384,1024]{1,0:T(8,128)(2,1)}, u32[]{:S(2)}, u32[]{:S(2)}) collective-permute-start(bf16[384,1024]{1,0:T(8,128)(2,1)} %slice.511), channel_id=1, source_target_pairs={{0,8},{8,0},{16,24},{24,16},{1,9},{9,1},{17,25},{25,17},{2,10},{10... | collective-permute-start | bytes 2359304 | tf_op jit(solution)/shard_map/ppermute | solution.py:76
  517.1 223.0 %reduce-scatter.8.cloned.1.call-start = ((), (), s32[]{:S(2)}) async-start(), calls=%async_computation.7 | async-start | bytes 5308416 | tf_op jit(solution)/shard_map/reduce_scatter | solution.py:549
  589.4 20.0 %collective-permute-start.47 = (bf16[384,1024]{1,0:T(8,128)(2,1)}, bf16[384,1024]{1,0:T(8,128)(2,1)S(1)}, u32[]{:S(2)}, u32[]{:S(2)}) collective-permute-start(bf16[384,1024]{1,0:T(8,128)(2,1)} %get-tuple-element.358), channel_id=1, source_target_pairs={{0,16},{8,24},{16,0},{24,8},{1,17},{9,25},{17,1},{25,9},{2,18},{10... | collective-permute-start | bytes 2359304 | tf_op jit(solution)/shard_map/ppermute | solution.py:76
  646.4 45.9 %collective-permute-start.53 = (bf16[128,3456]{1,0:T(8,128)(2,1)S(1)}, bf16[128,3456]{1,0:T(8,128)(2,1)S(1)}, u32[]{:S(2)}, u32[]{:S(2)}) collective-permute-start(bf16[128,3456]{1,0:T(8,128)(2,1)S(1)} %copy-done.8), channel_id=1, source_target_pairs={{0,16},{8,24},{16,0},{24,8},{1,17},{9,25},{17,1},{25,9},{2,18},{10... | collective-permute-start | bytes 2654216 | tf_op jit(solution)/shard_map/ppermute | solution.py:76
  650.8 38.0 %collective-permute-start.56 = (bf16[128,2816]{1,0:T(8,128)(2,1)S(1)}, bf16[128,2816]{1,0:T(8,128)(2,1)S(1)}, u32[]{:S(2)}, u32[]{:S(2)}) collective-permute-start(bf16[128,2816]{1,0:T(8,128)(2,1)S(1)} %slice.568.refs_1_), channel_id=1, source_target_pairs={{0,16},{8,24},{16,0},{24,8},{1,17},{9,25},{17,1},{25,9},{2,18},{10... | collective-permute-start | bytes 2162696 | tf_op jit(solution)/shard_map/ppermute | solution.py:76
  650.9 37.9 %collective-permute-start.60 = (bf16[128,256]{1,0:T(8,128)(2,1)S(1)}, bf16[128,256]{1,0:T(8,128)(2,1)S(1)}, u32[]{:S(2)}, u32[]{:S(2)}) collective-permute-start(bf16[128,256]{1,0:T(8,128)(2,1)S(1)} %pad_maximum_fusion.13.refs_1_), channel_id=1, source_target_pairs={{0,16},{8,24},{16,0},{24,8},{1,17},{9,25},{17,1},{25,9},{2,18},{10... | collective-permute-start | bytes 196616 | tf_op jit(solution)/shard_map/ppermute | solution.py:76
  657.2 47.8 %collective-permute-start.50 = (bf16[384,1024]{1,0:T(8,128)(2,1)S(1)}, bf16[384,1024]{1,0:T(8,128)(2,1)S(1)}, u32[]{:S(2)}, u32[]{:S(2)}) collective-permute-start(bf16[384,1024]{1,0:T(8,128)(2,1)S(1)} %get-tuple-element.356), channel_id=1, source_target_pairs={{0,16},{8,24},{16,0},{24,8},{1,17},{9,25},{17,1},{25,9},{2,18},{10... | collective-permute-start | bytes 2359304 | tf_op jit(solution)/shard_map/ppermute | solution.py:76
  657.3 32.1 %collective-permute-start.59 = (bf16[128,256]{1,0:T(8,128)(2,1)S(1)}, bf16[128,256]{1,0:T(8,128)(2,1)S(1)}, u32[]{:S(2)}, u32[]{:S(2)}) collective-permute-start(bf16[128,256]{1,0:T(8,128)(2,1)S(1)} %pad_maximum_fusion.13.refs_1_), channel_id=1, source_target_pairs={{0,8},{8,0},{16,24},{24,16},{1,9},{9,1},{17,25},{25,17},{2,10},{10... | collective-permute-start | bytes 196616 | tf_op jit(solution)/shard_map/ppermute | solution.py:76
  (145 other events, 1467.3 us)
Sparse Core Ops, SparseCore 0:
  52.7 132.0 all-gather.2
  187.7 106.9 all-gather.4
  389.3 127.2 reduce-scatter.3
  520.4 116.9 reduce-scatter.5
  641.4 98.6 reduce-scatter.7

commit v4 on v3

--- a/solution.py
+++ b/solution.py
@@ -37,12 +37,6 @@
     grad_in = scale * (weighted - unit * jnp.mean(weighted * unit, -1, keepdims=True))
     gain_grad = jnp.sum((grad_out * unit).reshape(-1, unit.shape[-1]), 0)
     return (grad_in, gain_grad)
-
-
-def doc_index(bounds, places):
-    later = bounds[1:]
-    passed = (later <= places[..., None]) & (later > 0)
-    return jnp.sum(passed.astype(jnp.int32), -1)
 
 
 def doc_starts(bounds, places):
@@ -86,10 +80,6 @@
         for place in sorted(have):
             have[place | bit] = swap_seq(have[place], bit)
     return [have[place] for place in sorted(have)]
-
-
-def near_half(block):
-    return jnp.concatenate(near_blocks(block), 0)
 
 
 def far_half(block):
@@ -114,16 +104,6 @@
     sent, kept, *work = tie(sent, kept, *work)
     total = kept + sent.astype(F32)
     return (total, *work) if work else total
-
-
-def flip_blocks(array):
-    place = lax.axis_index("seq")
-    for bit in seq_bits():
-        shape = array.shape
-        split = array.reshape((shape[0] // (2 * bit), 2, bit) + shape[1:])
-        turned = jnp.concatenate([split[:, 1:], split[:, :1]], 1)
-        array = jnp.where((place & bit) > 0, turned, split).reshape(shape)
-    return array
 
 
 def half_lanes(shape):
@@ -503,12 +483,13 @@
     return pairs
 
 
-def deal_rows(weight):
+def deal_rows(*weights):
     size = lax.axis_size("seq")
     place = lax.axis_index("seq")
-    piece = weight.shape[0] // size
-    part = lax.dynamic_slice_in_dim(weight, place * piece, piece, 0)
-    return lax.ppermute(part, ("seq", "dp"), deal_pairs())
+    piece = weights[0].shape[0] // size
+    parts = [lax.dynamic_slice_in_dim(w, place * piece, piece, 0) for w in weights]
+    dealt = lax.ppermute(jnp.concatenate(parts, 0), ("seq", "dp"), deal_pairs())
+    return [dealt[n * piece : (n + 1) * piece] for n in range(len(weights))]
 
 
 def pack_piece(piece, columns):
@@ -564,19 +545,52 @@
     size = lax.axis_size("dp")
     place = lax.axis_index("dp")
     rows = block.shape[0]
-    turns = [0]
-    held = block
-    for bit in reversed(dp_bits()):
-        got = swap_dp(held, bit)
-        if bit == dp_bits()[1]:
-            got, later = tie(got, later)
-        held = jnp.concatenate([held, got], 0)
-        turns = turns + [turn | bit for turn in turns]
+    near, middle, far = dp_bits()
+    have = {0: block, far: swap_dp(block, far), middle: swap_dp(block, middle)}
+    have[near] = swap_dp(block, near)
+    have[far], later = tie(have[far], later)
+    have[far | middle] = swap_dp(have[far], middle)
+    for turn in (middle, far, far | middle):
+        have[turn | near] = swap_dp(have[turn], near)
     result = jnp.zeros((size * rows, block.shape[1]), block.dtype)
-    for number, turn in enumerate(turns):
-        piece = held[number * rows : (number + 1) * rows]
-        result = lax.dynamic_update_slice_in_dim(result, piece, (place ^ turn) * rows, 0)
+    for turn in range(size):
+        result = lax.dynamic_update_slice_in_dim(result, have[turn], (place ^ turn) * rows, 0)
     return (result, later)
+
+
+def dp_scatter_small(grads):
+    if not dp_bits():
+        return dp_scatter(grads)
+    size = lax.axis_size("dp")
+    place = lax.axis_index("dp")
+    sums = grads.reshape(size, -1, grads.shape[1]).astype(F32)
+    for bit in dp_bits():
+        split = sums.reshape(-1, 2, *sums.shape[1:])
+        side = (place // bit) % 2
+        kept = lax.dynamic_index_in_dim(split, side, 1, False)
+        sent = lax.dynamic_index_in_dim(split, 1 - side, 1, False).astype(BF16)
+        sums = kept + swap_dp(sent, bit).astype(F32)
+    return sums[0].astype(BF16)
+
+
+def dp_scatter_pairs(grads, work, later):
+    if not dp_bits():
+        grads, later, *work = tie(grads, later, *work)
+        return (dp_scatter(grads), work, later)
+    size = lax.axis_size("dp")
+    side = lax.axis_index("dp") % 2
+    columns = grads.shape[1]
+    blocks = grads.reshape(size // 2, 2, -1, columns)
+    kept = lax.dynamic_index_in_dim(blocks, side, 1, False).reshape(-1, columns)
+    sent = lax.dynamic_index_in_dim(blocks, 1 - side, 1, False).reshape(-1, columns)
+    got, *work = tie(swap_dp(sent, 1), *work)
+    sums = (kept.astype(F32) + got.astype(F32)).astype(BF16)
+    sums, later = tie(sums, later)
+    groups = [list(range(n, size, 2)) for n in range(2)]
+    owned = lax.psum_scatter(
+        sums, "dp", scatter_dimension=0, tiled=True, axis_index_groups=groups
+    )
+    return (owned, work, later)
 
 
 def share(owned):
@@ -807,6 +821,102 @@
     )
 
 
+def row_starts(bounds_ref, token):
+    start = jnp.zeros(token.shape, jnp.int32)
+    for number in range(1, bounds_ref.shape[0]):
+        bound = bounds_ref[number]
+        start = jnp.where(bound <= token, jnp.maximum(start, bound), start)
+    return start
+
+
+def conv_backward_kernel(*refs, length, tokens, taps):
+    place_ref, bounds_ref = refs[:2]
+    grad_refs = refs[2 : 2 + tokens]
+    (
+        projected_ref, in_ref, out_w_ref, tap_ref,
+        d_projected_ref, near_out_ref, far_out_ref, tap_grad_ref,
+        product_ref, d_gated_ref, d_conv_ref,
+    ) = refs[2 + tokens :]
+    place = place_ref[0]
+    channels = out_w_ref.shape[0]
+    full = tokens * length
+    product_ref[0:8, :] = jnp.zeros((8, channels), F32)
+    d_conv_ref[full : full + 8, :] = jnp.zeros((8, channels), F32)
+    for block in range(tokens):
+        rows = slice(block * length, (block + 1) * length)
+        first = pl.multiple_of((block ^ place) * length, 8)
+        d_gated_ref[rows, :] = right_dot(grad_refs[block][...], out_w_ref[...])
+        product = projected_ref[rows, :channels] * projected_ref[rows, 2 * channels :]
+        product_ref[pl.ds(pl.multiple_of(8 + first, 8), length), :] = product.astype(BF16).astype(F32)
+    tap_grads = [jnp.zeros((1, channels), F32) for _ in range(taps)]
+    for block in range(tokens):
+        rows = slice(block * length, (block + 1) * length)
+        first = pl.multiple_of((block ^ place) * length, 8)
+        window = product_ref[pl.ds(first, length + 8), :]
+        token = first + lax.broadcasted_iota(jnp.int32, (length, channels), 0)
+        start = row_starts(bounds_ref, token)
+        d_gated = d_gated_ref[rows, :]
+        d_conv = d_gated * projected_ref[rows, channels : 2 * channels]
+        conv = jnp.zeros((length, channels), F32)
+        for tap in range(taps):
+            moved = window[8 - tap : 8 - tap + length, :]
+            moved = jnp.where(token - tap >= start, moved, 0.0)
+            conv = conv + tap_ref[tap : tap + 1, :] * moved
+            tap_grads[tap] = tap_grads[tap] + jnp.sum(d_conv * moved, 0, keepdims=True)
+        d_projected_ref[rows, channels : 2 * channels] = (d_gated * conv).astype(BF16)
+        d_conv_ref[pl.ds(first, length), :] = d_conv
+    for tap in range(taps):
+        tap_grad_ref[tap : tap + 1, :] = tap_grads[tap]
+    for block in range(tokens):
+        side, side_rows = block_rows(block, tokens, length)
+        rows = slice(block * length, (block + 1) * length)
+        first = pl.multiple_of((block ^ place) * length, 8)
+        window = d_conv_ref[pl.ds(first, length + 8), :]
+        token = first + lax.broadcasted_iota(jnp.int32, (length, channels), 0)
+        total = tap_ref[0:1, :] * window[:length, :]
+        for tap in range(1, taps):
+            same = token >= row_starts(bounds_ref, token + tap)
+            total = total + tap_ref[tap : tap + 1, :] * jnp.where(
+                same, window[tap : tap + length, :], 0.0
+            )
+        d_product = total.astype(BF16).astype(F32)
+        d_projected_ref[rows, :channels] = (
+            d_product * projected_ref[rows, 2 * channels :]
+        ).astype(BF16)
+        d_projected_ref[rows, 2 * channels :] = (
+            d_product * projected_ref[rows, :channels]
+        ).astype(BF16)
+        partial = right_dot(d_projected_ref[rows, :], in_ref[:, : 3 * channels])
+        (near_out_ref, far_out_ref)[side][side_rows, :] = partial.astype(BF16)
+
+
+def conv_backward(place, bounds, grads, projected, in_weights, out_weights, kernel):
+    length, width = grads[0].shape
+    full = len(grads) * length
+    channels = out_weights.shape[0]
+    taps = kernel.shape[0]
+    scalar = pl.BlockSpec(memory_space=pltpu.SMEM)
+    return pl.pallas_call(
+        lambda *refs: conv_backward_kernel(*refs, length=length, tokens=len(grads), taps=taps),
+        in_specs=[scalar, scalar] + whole(len(grads) + 4),
+        out_specs=tuple(whole(4)),
+        out_shape=(
+            jax.ShapeDtypeStruct((full, 3 * channels), BF16),
+            jax.ShapeDtypeStruct((full // 2, width), BF16),
+            jax.ShapeDtypeStruct((full // 2, width), BF16),
+            jax.ShapeDtypeStruct((taps, channels), F32),
+        ),
+        scratch_shapes=[
+            pltpu.VMEM((full + 8, channels), F32),
+            pltpu.VMEM((full, channels), F32),
+            pltpu.VMEM((full + 8, channels), F32),
+        ],
+        cost_estimate=pl.CostEstimate(flops=0, transcendentals=0, bytes_accessed=100_000),
+        compiler_params=pltpu.CompilerParams(vmem_limit_bytes=VMEM_LIMIT),
+        name="conv_backward",
+    )(place, bounds, *grads, projected, in_weights, out_weights, kernel)
+
+
 def conv_forward_kernel(*refs, length, tokens, taps):
     place_ref, bounds_ref = refs[:2]
     token_refs = refs[2 : 2 + tokens]
@@ -834,10 +944,7 @@
         first = pl.multiple_of((block ^ place) * length, 8)
         window = product_ref[pl.ds(first, length + 8), :]
         token = first + lax.broadcasted_iota(jnp.int32, (length, channels), 0)
-        start = jnp.zeros((length, channels), jnp.int32)
-        for number in range(1, bounds_ref.shape[0]):
-            bound = bounds_ref[number]
-            start = jnp.where(bound <= token, jnp.maximum(start, bound), start)
+        start = row_starts(bounds_ref, token)
         conv = tap_ref[0:1, :] * window[8:, :]
         for tap in range(1, taps):
             moved = window[8 - tap : 8 - tap + length, :]
@@ -910,20 +1017,20 @@
     slots = width // dp_count
     head = g_q.shape[0] * dp_count
     taps = conv_w.shape[0]
-    reach = taps - 1
-
-    x_far = far_half(x_in.reshape(length, width))
+
+    dealt_out, dealt_o = deal_rows(w_out, w_o)
+    x_low, dealt_out, dealt_o = tie(x_in.reshape(length, width), dealt_out, dealt_o)
+    x_far = far_half(x_low)
     cotangent_low, x_far = tie(cotangent.reshape(length, width), x_far)
-    x_blocks = near_blocks(x_in.reshape(length, width)) + near_blocks(x_far)
+    x_blocks = near_blocks(x_low) + near_blocks(x_far)
     cotangent_blocks = near_blocks(cotangent_low) + near_blocks(far_half(cotangent_low))
     head_gains = jnp.pad(jnp.stack([g_q, g_k], 1), ((0, slots - head // dp_count), (0, 0)))
     small = jnp.concatenate(
         [conv_w.T, jnp.stack([g_mix1, g_ffn1, g_attn2, g_ffn2], 1), head_gains], 1
     )
     small = jnp.pad(small, ((0, 0), (0, 128 - small.shape[1])))
-    dealt = deal_rows(jnp.stack([w_out, w_o], 1))
-    out_piece = pack_piece(dealt[:, 0], channels)
-    o_piece = pack_piece(dealt[:, 1], channels)
+    out_piece = pack_piece(dealt_out, channels)
+    o_piece = pack_piece(dealt_o, channels)
     mix_block = jnp.concatenate([column_block(w_in, 3), small, out_piece], 1)
     mix_block, w_gate1, w_up1, w_down1, w_q, key_projection_weight, value_projection_weight = tie(
         mix_block, w_gate1, w_up1, w_down1, w_q, key_projection_weight, value_projection_weight
@@ -949,23 +1056,7 @@
     qkv_block = attn_all[:, :qkv_width]
     o_block = unpack_rows(attn_all[:, qkv_width:], dp_count)
     bounds = cu_seqlens[0]
-    turn = seq_place ^ jnp.arange(seq_count, dtype=jnp.int32)
-    places = turn[:, None] * length + jnp.arange(length, dtype=jnp.int32)[None, :]
-    docs_here = doc_index(bounds, places)
-    masks = [
-        (doc_index(bounds, places - tap) == docs_here).astype(F32)[..., None]
-        for tap in range(1, reach + 1)
-    ]
-
-    order = jnp.arange(full, dtype=jnp.int32)
-    starts = doc_starts(bounds, order)
-    cosine, sine = rope_tables(order - starts, head)
-    starts = starts[None, :]
     place = seq_place.reshape(1).astype(jnp.int32)
-    mix_all, cosine, sine, starts, *cotangent_blocks = tie(
-        mix_all, cosine, sine, starts, *cotangent_blocks
-    )
-    in_block = mix_all[:, : 3 * channels]
     out_block = unpack_rows(mix_all[:, 3 * channels + 128 :], dp_count)
     small_all = mix_all[:, 3 * channels : 3 * channels + 128].astype(F32).T
     kernel = lax.dynamic_slice_in_dim(small_all[:taps], seq_place * channels, channels, 1)
@@ -977,14 +1068,21 @@
     normed_one, projected, gated, near_out, far_out = conv_forward(
         place, bounds, x_blocks, mix_all, out_block, kernel, gain_mix[None, :]
     )
-    hidden_one = x_flat + seq_scatter(near_out, far_out)
+    near_out, late_bounds, *cotangent_blocks = tie(near_out, bounds, *cotangent_blocks)
+    order = jnp.arange(full, dtype=jnp.int32)
+    starts = doc_starts(late_bounds, order)
+    cosine, sine = rope_tables(order - starts, head)
+    mixed, cosine, sine = seq_scatter(near_out, far_out, cosine, sine)
+    hidden_one = x_flat + mixed
+    starts = starts[None, :]
 
     unit_two, scale_two = unit_scale(hidden_one)
     near_two = (unit_two * gain_ffn_one).astype(BF16)
     far_two = far_half(near_two)
     blocks_two = near_blocks(near_two) + near_blocks(far_two)
     terms_one, partial_one = ffn_forward(blocks_two, ffn_one, hidden)
-    hidden_two = hidden_one + seq_scatter(*halves_of(partial_one))
+    mixed, qkv_block, o_block = seq_scatter(*halves_of(partial_one), qkv_block, o_block)
+    hidden_two = hidden_one + mixed
 
     unit_three, scale_three = unit_scale(hidden_two)
     near_three = (unit_three * gain_attn).astype(BF16)
@@ -1045,59 +1143,35 @@
     kept_one, far_out = ffn_backward(far_grad, terms_one, ffn_one, hidden, 1, kept_one)
     kept_one, far_out = tie(kept_one, far_out)
     d_gate_up = left_dot(jnp.concatenate(blocks_two, 0), kept_one).astype(BF16)
+    d_ffn_in_one, d_gate_up = seq_scatter(near_out, far_out, d_gate_up)
+    owned_one = dp_scatter(jnp.concatenate([d_gate_up, *grads_attn], 1))
+    d_hidden_one, d_gain_ffn_one = norm_back(d_ffn_in_one, gain_ffn_one, unit_two, scale_two)
+    grad_one = grad_two + d_hidden_one
+
+    grad_mix = grad_one.astype(BF16)
+    far_mix = far_half(grad_mix)
     d_down = left_dot(
         jnp.concatenate(near_grad + far_grad, 0), terms_one[:, 2 * hidden :]
     ).astype(BF16)
-    owned_one = dp_scatter(jnp.concatenate([d_gate_up, *grads_attn], 1))
-    d_ffn_in_one, d_down = seq_scatter(near_out, far_out, d_down)
-    d_hidden_one, d_gain_ffn_one = norm_back(d_ffn_in_one, gain_ffn_one, unit_two, scale_two)
-    grad_one = grad_two + d_hidden_one
-
-    grad_mix = grad_one.astype(BF16)
-    far_mix = far_half(grad_mix)
     far_mix, d_down = tie(far_mix, d_down)
-    grad_mix = jnp.concatenate([near_half(grad_mix), near_half(far_mix)], 0)
-    grad_mix, owned_two = tie(grad_mix, owned_two)
-    projected = projected.reshape(seq_count, length, 3 * channels)
-    part_b = projected[..., :channels]
-    part_c = projected[..., channels : 2 * channels]
-    part_x = projected[..., 2 * channels :]
-    product = (part_b * part_x).astype(BF16)
-    tails = flip_blocks(product[:, length - reach :])
-    before = flip_blocks(jnp.concatenate([jnp.zeros_like(tails[:1]), tails[:-1]], 0))
-    extended = jnp.concatenate([before, product], 1).astype(F32)
-    conv_out = kernel[0] * extended[:, reach:]
-    for tap in range(1, reach + 1):
-        conv_out = (
-            conv_out
-            + kernel[tap] * extended[:, reach - tap : reach - tap + length] * masks[tap - 1]
-        )
-    d_w_out = left_dot(gated, grad_mix)
-    d_gated = right_dot(grad_mix, out_block).reshape(seq_count, length, channels)
-    d_part_c = d_gated * conv_out
-    d_conv = d_gated * part_c
-    sent = [d_conv * masks[tap - 1] for tap in range(1, reach + 1)]
-    kernel_grads = [jnp.sum((d_conv * extended[:, reach:]).reshape(-1, channels), 0)]
-    for tap in range(1, reach + 1):
-        piece = extended[:, reach - tap : reach - tap + length]
-        kernel_grads.append(jnp.sum((sent[tap - 1] * piece).reshape(-1, channels), 0))
-    d_product_sum = kernel[0] * d_conv
-    for tap in range(1, reach + 1):
-        heads = flip_blocks(sent[tap - 1][:, :tap])
-        after = flip_blocks(jnp.concatenate([heads[1:], jnp.zeros_like(heads[:1])], 0))
-        moved = jnp.concatenate([sent[tap - 1][:, tap:], after], 1)
-        d_product_sum = d_product_sum + kernel[tap] * moved
-    d_product = lax.optimization_barrier(d_product_sum.astype(BF16)).astype(F32)
-    d_projected = jnp.concatenate([d_product * part_x, d_part_c, d_product * part_b], -1)
-    d_projected = d_projected.astype(BF16).reshape(full, 3 * channels)
+    mix_blocks = near_blocks(grad_mix) + near_blocks(far_mix)
+    mix_blocks[-1], owned_two = tie(mix_blocks[-1], owned_two)
+    d_projected, near_out, far_out, kernel_grads = conv_backward(
+        place, bounds, mix_blocks, projected, mix_all, out_block, kernel
+    )
     d_w_in = left_dot(normed_one, d_projected)
-    d_normed = seq_scatter(*halves_of(right_dot(d_projected, in_block)))
+    d_w_out = left_dot(gated, jnp.concatenate(mix_blocks, 0))
+    grads_mix = jnp.concatenate(
+        [d_down, d_w_in.astype(BF16), pack_rows(d_w_out.astype(BF16), dp_count)], 1
+    )
+    grads_mix, kept_two = tie(grads_mix, kept_two)
+    d_normed = seq_scatter(near_out, far_out)
     unit_one, scale_one = unit_scale(x_flat)
     d_x_part, d_gain_mix = norm_back(d_normed, gain_mix, unit_one, scale_one)
     d_x = (grad_one + d_x_part).reshape(rows, length, width)
 
     kernel_wide = lax.dynamic_update_slice_in_dim(
-        jnp.zeros((taps, width), F32), jnp.stack(kernel_grads), seq_place * channels, 1
+        jnp.zeros((taps, width), F32), kernel_grads, seq_place * channels, 1
     )
     head_wide = jnp.pad(
         d_head_gains.reshape(2, dp_count, -1),
@@ -1112,28 +1186,20 @@
         0,
     )
     vector_columns = jnp.pad(vectors.T, ((0, 0), (0, 128 - vectors.shape[0])))
-    grads_mix = jnp.concatenate(
-        [
-            d_down,
-            d_w_in.astype(BF16),
-            vector_columns.astype(BF16),
-            pack_rows(d_w_out.astype(BF16), dp_count),
-        ],
-        1,
-    )
-    grads_mix, owned_one = tie(grads_mix, owned_one)
-    owned_mix = dp_scatter(grads_mix)
+    owned_vectors = dp_scatter_small(vector_columns.astype(BF16))
 
     def redeal(block):
         return pack_piece(undeal_rows(unpack_piece(block, width)), channels)
 
-    owned_two, owned_one, kept_two = tie(owned_two, owned_one, kept_two)
     ffn_out = right_dot(kept_two[:, 2 * hidden :], ffn_two[:, 2 * hidden :])
     hidden_four = hidden_three + seq_scatter(*halves_of(ffn_out))
     out = hidden_four.astype(BF16).reshape(rows, length, width)
     d_wgate_two, d_wup_two, d_down_two = assemble(
         place, share(owned_two), [(n * hidden, hidden, 1, False) for n in range(3)]
     )
+    owned_mix, (out, d_x, d_wgate_two, d_wup_two, d_down_two), owned_one = dp_scatter_pairs(
+        grads_mix, (out, d_x, d_wgate_two, d_wup_two, d_down_two), owned_one
+    )
     tasks = [(n * hidden, hidden, 1, False) for n in range(2)]
     for columns in (channels, kv_width, kv_width):
         tasks.append((tasks[-1][0] + tasks[-1][1], columns, 1, False))
@@ -1143,8 +1209,9 @@
     (d_w_o_full,) = assemble(
         place, share(redeal(owned_one[:, -channels:])), [(0, channels, 1, True)]
     )
-    owned_mix, out, d_x, d_wgate_two, d_wup_two, d_down_two, d_wgate_one, d_w_o_full = tie(
-        owned_mix, out, d_x, d_wgate_two, d_wup_two, d_down_two, d_wgate_one, d_w_o_full
+    shared_vectors = share(owned_vectors)
+    owned_mix, d_wgate_one, d_w_o_full, *shared_vectors = tie(
+        owned_mix, d_wgate_one, d_w_o_full, *shared_vectors
     )
     shared_mix = share(owned_mix[:, :-channels])
     shared_out = share(redeal(owned_mix[:, -channels:]))
@@ -1152,8 +1219,7 @@
         place, shared_mix, [(0, hidden, 1, False), (hidden, 3 * channels, 3, False)]
     )
     (d_w_out_full,) = assemble(place, shared_out, [(0, channels, 1, True)])
-    vectors_all = [block[:, hidden + 3 * channels :] for block in shared_mix]
-    sums = sum(block.astype(F32) for block in vectors_all).T
+    sums = sum(block.astype(F32) for block in shared_vectors).T
     small_head = head // dp_count
     return (
         out,

time: 786 us -> 748 us (0.952)
  waiting for transfers between devices: 332 us -> 285 us
  starting transfers between devices: 66.5 us -> 82.2 us
  Pallas kernels: 154 us -> 165 us
  other arithmetic: 64.3 us -> 53.8 us
  matrix products: 73 us -> 63.6 us
    reduce_scatter x3 -> x2, waiting for transfers between devices: 51.7 us -> 0.01 us  [dp_scatter(): return lax.psum_scatter(grads, 'dp', scatter_dimension=0, tiled=True)]
    ppermute x63 -> x66, waiting for transfers between devices: 247 us -> 227 us  [swap_seq(): return lax.ppermute(array, 'seq', [(i, i ^ bit) for i in range(size)])]
    ppermute x3 -> x11, starting transfers between devices: 18.8 us -> 37.6 us  [swap_dp(): return lax.ppermute(array, 'dp', [(i, i ^ bit) for i in range(size)])]
    dynamic_update_slice x8 -> x10, local copies, waits for them, and re-layouts: 0.81 us -> 13.1 us  [the longest x9 13.1 us: dp_gather_small(): lax.dynamic_update_slice_in_dim(result, have[turn], (place ^ turn) * rows...]
    pallas_call x0 -> x1, Pallas kernels: none -> 10.3 us  [conv_backward(): pl.pallas_call(lambda *refs: conv_backward_kernel(*refs, length=length, t...]
    ppermute x3 -> x11, waiting for transfers between devices: 24.7 us -> 34.8 us  [swap_dp(): return lax.ppermute(array, 'dp', [(i, i ^ bit) for i in range(size)])]
    reduce_scatter x0 -> x1, waiting for transfers between devices: none -> 9.9 us  [dp_scatter_pairs(): lax.psum_scatter(sums, 'dp', scatter_dimension=0, tiled=True, axis_index_...]
    dot_general x3 -> x1, matrix products: 17.5 us -> 9.81 us  [right_dot(): lax.dot_general(left, right, (((1,), (1,)), ((), ())), preferred_element_...]
  transfers between devices with their start and end apart: 74 -> 85, of which waited for: 39 -> 45; matrix products, arithmetic and copies ran while one was open for 23% -> 22% of each run, Pallas kernels for 18% -> 20%
where the time goes in v4:
time: 748 us; the launch traced here: 740 us
  waiting for transfers between devices  285 us (38%)
  Pallas kernels  165 us (22%)
  starting transfers between devices  82.2 us (11%)
  local copies, waits for them, and re-layouts  73.8 us (10%)
  matrix products  63.6 us (9%)
  other arithmetic  53.8 us (7%)
  between operations  15.7 us (2%)
    ppermute x66, waiting for transfers between devices, swap_seq(): return lax.ppermute(array, 'seq', [(i, i ^ bit) for i in range(size)])  227 us
    pallas_call x5, Pallas kernels, ffn_call(): pl.pallas_call(lambda *refs: kernel(*refs, count=count), grid=(count,), i...  69.1 us
    dot_general x8, matrix products, left_dot(): lax.dot_general(left, right, (((0,), (0,)), ((), ())), preferred_element_...  53.8 us
    ppermute x66, starting transfers between devices, swap_seq(): return lax.ppermute(array, 'seq', [(i, i ^ bit) for i in range(size)])  42 us
    ppermute x11, starting transfers between devices, swap_dp(): return lax.ppermute(array, 'dp', [(i, i ^ bit) for i in range(size)])  37.6 us
    pallas_call x1, Pallas kernels, attention_backward(): pl.pallas_call(lambda *refs: attention_backward_kernel(*refs, length=leng...  37.2 us
    ppermute x11, waiting for transfers between devices, swap_dp(): return lax.ppermute(array, 'dp', [(i, i ^ bit) for i in range(size)])  34.8 us
    unnamed x194, local copies, waits for them, and re-layouts  27.4 us
  transfers between devices with their start and end apart: 85, of which 45 were waited for; matrix products, arithmetic and copies ran while one was open for 22% of the time, Pallas kernels for 20%

profile of v4, /device:TPU:0, one launch (start us, length us, event | category | flops | bytes accessed | tf_op | source)
XLA Modules:
  0.0 739.7 jit_solution(12962181242826208364)
XLA Ops:
  11.5 18.0 %collective-permute-start.7 = (bf16[128,1152]{0,1:T(8,128)(2,1)}, bf16[128,1152]{0,1:T(8,128)(2,1)S(1)}, u32[]{:S(2)}, u32[]{:S(2)}) collective-permute-start(bf16[128,1152]{0,1:T(8,128)(2,1)} %fusion.87), channel_id=1, source_target_pairs={{0,4},{1,5},{2,6},{3,7},{4,0},{5,1},{6,2},{7,3},{8,12},{9,13},{10,... | collective-permute-start | bytes 884744 | tf_op jit(solution)/shard_map/ppermute | solution.py:535
  65.3 19.1 %collective-permute-done.9 = bf16[128,1152]{0,1:T(8,128)(2,1)S(1)} collective-permute-done((bf16[128,1152]{0,1:T(8,128)(2,1)S(1)}, bf16[128,1152]{0,1:T(8,128)(2,1)S(1)}, u32[]{:S(2)}, u32[]{:S(2)}) %collective-permute-start.9) | collective-permute-done | bytes 294944 | tf_op jit(solution)/shard_map/ppermute | solution.py:535
  110.5 9.9 %conv_forward.1 = (bf16[1536,1024]{1,0:T(8,128)(2,1)}, f32[1536,768]{1,0:T(8,128)}, bf16[1536,256]{1,0:T(8,128)(2,1)S(1)}, bf16[768,1024]{1,0:T(8,128)(2,1)S(1)}, bf16[768,1024]{1,0:T(8,128)(2,1)}) custom-call(s32[1]{0:T(128)} %bitcast.2.refs_0_, s32[4]{0:T(128)S(1)} %bitcast.104, bf16[384,1024]{1,0:T(8,128)(2,1)S(1)} %bitcast.93, ...), custom_call_target="tpu_custom_call" | custom-call | flops 4000000000 | bytes 20000000 | tf_op jit(solution)/shard_map/conv_forward/pallas_call | solution.py:965
  135.1 12.5 %collective-permute-done.12 = bf16[384,1024]{1,0:T(8,128)(2,1)S(1)} collective-permute-done((bf16[384,1024]{1,0:T(8,128)(2,1)S(1)}, bf16[384,1024]{1,0:T(8,128)(2,1)S(1)}, u32[]{:S(2)}, u32[]{:S(2)}) %collective-permute-start.12) | collective-permute-done | bytes 786464 | tf_op jit(solution)/shard_map/ppermute | solution.py:70
  149.7 18.0 %collective-permute-done.18.refs_2_ = bf16[384,1024]{1,0:T(8,128)(2,1)S(1)} collective-permute-done((bf16[384,1024]{1,0:T(8,128)(2,1)S(1)}, bf16[384,1024]{1,0:T(8,128)(2,1)S(1)}, u32[]{:S(2)}, u32[]{:S(2)}) %collective-permute-start.18) | collective-permute-done | bytes 786464 | tf_op jit(solution)/shard_map/ppermute | solution.py:70
  170.9 13.4 %all-gather.3.cloned.1.call-done.refs_4_.refs_5_.refs_6_.refs_3_ = bf16[1024,4224]{1,0:T(8,128)(2,1)} async-done(((bf16[128,4224]{1,0:T(8,128)(2,1)}), bf16[1024,4224]{1,0:T(8,128)(2,1)}) %all-gather.3.cloned.1.call-update) | async-done | bytes 8650768 | tf_op jit(solution)/shard_map/all_gather | solution.py:526
  185.4 18.3 %ffn_forward.1 = (bf16[1536,3456]{1,0:T(8,128)(2,1)}, bf16[1536,1024]{1,0:T(8,128)(2,1)}) custom-call(bf16[384,1024]{1,0:T(8,128)(2,1)S(1)} %multiply_convert_fusion.2.refs_0_, bf16[384,1024]{1,0:T(8,128)(2,1)S(1)} %collective-permute-done.17.refs_1_, bf16[384,1024]{1,0:T(8,128)(2,1)S(1)} %collective-permute-done.18.refs_2_, ...), custom_call_target="tpu_custom_call" | custom-call | flops 6000000000 | bytes 20000000 | tf_op jit(solution)/shard_map/ffn_forward/pallas_call | solution.py:743
  214.8 15.7 %collective-permute-done.21 = bf16[384,1024]{1,0:T(8,128)(2,1)S(1)} collective-permute-done((bf16[384,1024]{1,0:T(8,128)(2,1)S(1)}, bf16[384,1024]{1,0:T(8,128)(2,1)S(1)}, u32[]{:S(2)}, u32[]{:S(2)}) %collective-permute-start.21) | collective-permute-done | bytes 786464 | tf_op jit(solution)/shard_map/ppermute | solution.py:70
  234.6 17.6 %collective-permute-done.24.refs_3_ = bf16[384,1024]{1,0:T(8,128)(2,1)} collective-permute-done((bf16[384,1024]{1,0:T(8,128)(2,1)}, bf16[384,1024]{1,0:T(8,128)(2,1)}, u32[]{:S(2)}, u32[]{:S(2)}) %collective-permute-start.24) | collective-permute-done | bytes 786464 | tf_op jit(solution)/shard_map/ppermute | solution.py:70
  255.8 27.0 %attention_forward.1 = (f32[1536,512]{1,0:T(8,128)}, bf16[1536,256]{1,0:T(8,128)(2,1)S(1)}, f32[256,1536]{1,0:T(8,128)}, f32[8,1536]{1,0:T(8,128)S(1)}, bf16[768...) custom-call(s32[1]{0:T(128)} %bitcast.2.refs_0_, bf16[384,1024]{1,0:T(8,128)(2,1)} %multiply_convert_fusion.1.refs_1_, ...), custom_call_target="tpu_custom_call" | custom-call | flops 20000000000 | bytes 20000000 | tf_op jit(solution)/shard_map/attention_forward/pallas_call | solution.py:405
  288.8 17.8 %collective-permute-done.27 = bf16[384,1024]{1,0:T(8,128)(2,1)S(1)} collective-permute-done((bf16[384,1024]{1,0:T(8,128)(2,1)S(1)}, bf16[384,1024]{1,0:T(8,128)(2,1)S(1)}, u32[]{:S(2)}, u32[]{:S(2)}) %collective-permute-start.27) | collective-permute-done | bytes 786464 | tf_op jit(solution)/shard_map/ppermute | solution.py:70
  310.4 14.8 %ffn_turn.2 = (bf16[1536,3456]{1,0:T(8,128)(2,1)}, bf16[768,1024]{1,0:T(8,128)(2,1)S(1)}) custom-call(bf16[384,1024]{1,0:T(8,128)(2,1)S(1)} %multiply_convert_fusion.refs_0_, bf16[384,1024]{1,0:T(8,128)(2,1)S(1)} %collective-permute-done.30.refs_1_, bf16[384,1024]{1,0:T(8,128)(2,1)S(1)} %bitcast.96, bf16[384,1024]{1,0:T(8,128)(2,1)} %collective-permute-done.13.refs_3_, ...), custom_call_target="tpu_custom_call" | custom-call | flops 6000000000 | bytes 20000000 | tf_op jit(solution)/shard_map/ffn_turn/pallas_call | solution.py:743
  330.7 14.8 %ffn_turn.3 = (bf16[1536,3456]{1,0:T(8,128)(2,1)}, bf16[768,1024]{1,0:T(8,128)(2,1)S(1)}) custom-call(bf16[384,1024]{1,0:T(8,128)(2,1)} %collective-permute-done.29.refs_0_, bf16[384,1024]{1,0:T(8,128)(2,1)S(1)} %collective-permute-done.31.refs_1_, bf16[384,1024]{1,0:T(8,128)(2,1)} %collective-permute-done.14.refs_2_, ...), custom_call_target="tpu_custom_call", output_to_operand_aliasing={{0}: (7, {})} | custom-call | flops 6000000000 | bytes 20000000 | tf_op jit(solution)/shard_map/ffn_turn/pallas_call | solution.py:743
  349.8 12.6 %fusion.2 = bf16[1024,2304]{1,0:T(8,128)(2,1)} fusion(bf16[1536,3456]{1,0:T(8,128)(2,1)} %get-tuple-element.203, bf16[384,1024]{1,0:T(8,128)(2,1)S(1)} %collective-permute-done.31.refs_1_, bf16[384,1024]{1,0:T(8,128)(2,1)} %collective-permute-done.29.refs_0_, bf16[384,1024]{1,0:T(8,128)(2,1)S(1)} %collective-permute-done.30.refs_1_, ...), kind=kOutput, calls=%fused_computation.5 | convolution fusion | flops 7262699520 | bytes 14942208 | tf_op jit(solution)/shard_map/dot_general | solution.py:19
  394.0 37.2 %attention_backward.1 = (bf16[1536,512]{1,0:T(8,128)(2,1)}, bf16[768,1024]{1,0:T(8,128)(2,1)}, bf16[768,1024]{1,0:T(8,128)(2,1)}, f32[2,128]{1,0:T(2,128)S(1)}) custom-call(s32[1]{0:T(128)} %bitcast.2.refs_0_, bf16[384,1024]{1,0:T(8,128)(2,1)S(1)} %get-tuple-element.385.refs_1_, bf16[384,1024]{1,0:T(8,128)(2,1)S(1)} %collective-permute-done.35.refs_2_, ...), custom_call_target="tpu_custom_call" | custom-call | flops 20000000000 | bytes 20000000 | tf_op jit(solution)/shard_map/attention_backward/pallas_call | solution.py:437
  446.7 14.0 %collective-permute-done.39 = bf16[384,1024]{1,0:T(8,128)(2,1)S(1)} collective-permute-done((bf16[384,1024]{1,0:T(8,128)(2,1)S(1)}, bf16[384,1024]{1,0:T(8,128)(2,1)S(1)}, u32[]{:S(2)}, u32[]{:S(2)}) %collective-permute-start.39) | collective-permute-done | bytes 786464 | tf_op jit(solution)/shard_map/ppermute | solution.py:70
  466.1 10.7 %ffn_backward.2 = (bf16[1536,2304]{1,0:T(8,128)(2,1)}, bf16[768,1024]{1,0:T(8,128)(2,1)S(1)}) custom-call(bf16[384,1024]{1,0:T(8,128)(2,1)S(1)} %get-tuple-element.383.refs_0_, bf16[384,1024]{1,0:T(8,128)(2,1)S(1)} %collective-permute-done.42.refs_1_, bf16[1536,3456]{1,0:T(8,128)(2,1)} %get-tuple-element.185.refs_2_, ...), custom_call_target="tpu_custom_call" | custom-call | flops 6000000000 | bytes 20000000 | tf_op jit(solution)/shard_map/ffn_backward/pallas_call | solution.py:743
  486.1 10.5 %ffn_backward.3 = (bf16[1536,2304]{1,0:T(8,128)(2,1)}, bf16[768,1024]{1,0:T(8,128)(2,1)S(1)}) custom-call(bf16[384,1024]{1,0:T(8,128)(2,1)S(1)} %collective-permute-done.41.refs_0_, bf16[384,1024]{1,0:T(8,128)(2,1)S(1)} %collective-permute-done.43.refs_1_, bf16[1536,3456]{1,0:T(8,128)(2,1)} %get-tuple-element.185.refs_2_, ...), custom_call_target="tpu_custom_call", output_to_operand_aliasing={{0}: (6, {})} | custom-call | flops 6000000000 | bytes 20000000 | tf_op jit(solution)/shard_map/ffn_backward/pallas_call | solution.py:743
  501.1 10.7 %convolution_convert_fusion = bf16[1024,2304]{1,0:T(8,128)(2,1)S(1)} fusion(bf16[1536,2304]{1,0:T(8,128)(2,1)} %get-tuple-element.191, bf16[384,1024]{1,0:T(8,128)(2,1)S(1)} %copy-done.21, bf16[384,1024]{1,0:T(8,128)(2,1)S(1)} %copy-done.16, bf16[384,1024]{1,0:T(8,128)(2,1)S(1)} %copy-done.18, bf16[384,1024]{1,0:T(8,128)(2,1)S(1)} %multiply_convert_fusion.2.refs_0_), kind=kOutput, calls=%fused_computation.4 | convolution fusion | flops 7262699520 | bytes 14942208 | tf_op jit(solution)/shard_map/dot_general | solution.py:19
  555.1 10.3 %conv_backward.1 = (bf16[1536,768]{1,0:T(8,128)(2,1)}, bf16[768,1024]{1,0:T(8,128)(2,1)S(1)}, bf16[768,1024]{1,0:T(8,128)(2,1)}, f32[3,256]{1,0:T(4,128)S(1)}) custom-call(s32[1]{0:T(128)} %bitcast.2.refs_0_, s32[4]{0:T(128)S(1)} %bitcast.106, bf16[384,1024]{1,0:T(8,128)(2,1)S(1)} %get-tuple-element.381.refs_2_, ...), custom_call_target="tpu_custom_call" | custom-call | bytes 100000 | tf_op jit(solution)/shard_map/conv_backward/pallas_call | solution.py:899
  601.6 12.8 %collective-permute-done.58.refs_3_ = bf16[128,3456]{1,0:T(8,128)(2,1)S(1)} collective-permute-done((bf16[128,3456]{1,0:T(8,128)(2,1)}, bf16[128,3456]{1,0:T(8,128)(2,1)S(1)}, u32[]{:S(2)}, u32[]{:S(2)}) %collective-permute-start.58) | collective-permute-done | bytes 884768 | tf_op jit(solution)/shard_map/ppermute | solution.py:70
  614.4 16.8 %collective-permute-done.55 = bf16[384,1024]{1,0:T(8,128)(2,1)S(1)} collective-permute-done((bf16[384,1024]{1,0:T(8,128)(2,1)S(1)}, bf16[384,1024]{1,0:T(8,128)(2,1)S(1)}, u32[]{:S(2)}, u32[]{:S(2)}) %collective-permute-start.55) | collective-permute-done | bytes 786464 | tf_op jit(solution)/shard_map/ppermute | solution.py:70
  631.3 16.1 %collective-permute-done.52 = bf16[384,1024]{1,0:T(8,128)(2,1)S(1)} collective-permute-done((bf16[384,1024]{1,0:T(8,128)(2,1)S(1)}, bf16[384,1024]{1,0:T(8,128)(2,1)S(1)}, u32[]{:S(2)}, u32[]{:S(2)}) %collective-permute-start.52) | collective-permute-done | bytes 786464 | tf_op jit(solution)/shard_map/ppermute | solution.py:70
  699.5 9.9 %reduce-scatter.8.cloned.1.call-done = bf16[128,2176]{1,0:T(8,128)(2,1)} async-done(((bf16[512,2176]{1,0:T(8,128)(2,1)}), bf16[128,2176]{1,0:T(8,128)(2,1)}) %reduce-scatter.8.cloned.1.call-update) | async-done | bytes 557072 | tf_op jit(solution)/shard_map/reduce_scatter | solution.py:590
  (507 shorter events, 345.5 us)
Async XLA Ops:
  7.2 177.0 %all-gather.3.cloned.1.call-start = ((), (), s32[]{:S(2)}) async-start(), calls=%async_computation.3 | async-start | bytes 9732096 | tf_op jit(solution)/shard_map/all_gather | solution.py:526
  11.5 23.5 %collective-permute-start.7 = (bf16[128,1152]{0,1:T(8,128)(2,1)}, bf16[128,1152]{0,1:T(8,128)(2,1)S(1)}, u32[]{:S(2)}, u32[]{:S(2)}) collective-permute-start(bf16[128,1152]{0,1:T(8,128)(2,1)} %fusion.87), channel_id=1, source_target_pairs={{0,4},{1,5},{2,6},{3,7},{4,0},{5,1},{6,2},{7,3},{8,12},{9,13},{10,... | collective-permute-start | bytes 884744 | tf_op jit(solution)/shard_map/ppermute | solution.py:535
  36.0 273.6 %all-gather.5.cloned.1.call-start = ((), (), s32[]{:S(2)}) async-start(), calls=%async_computation.4 | async-start | bytes 7962624 | tf_op jit(solution)/shard_map/all_gather | solution.py:526
  37.9 20.7 %collective-permute-start.4 = (bf16[128,1152]{0,1:T(8,128)(2,1)}, bf16[128,1152]{0,1:T(8,128)(2,1)}, u32[]{:S(2)}, u32[]{:S(2)}) collective-permute-start(bf16[128,1152]{0,1:T(8,128)(2,1)} %fusion.87), channel_id=1, source_target_pairs={{0,1},{1,0},{2,3},{3,2},{4,5},{5,4},{6,7},{7,6},{8,9},{9,8},{10,11... | collective-permute-start | bytes 884744 | tf_op jit(solution)/shard_map/ppermute | solution.py:535
  49.3 40.0 %collective-permute-start.2 = (bf16[384,1024]{1,0:T(8,128)(2,1)S(1)}, bf16[384,1024]{1,0:T(8,128)(2,1)S(1)}, u32[]{:S(2)}, u32[]{:S(2)}) collective-permute-start(bf16[384,1024]{1,0:T(8,128)(2,1)S(1)} %bitcast.91), channel_id=1, source_target_pairs={{0,16},{8,24},{16,0},{24,8},{1,17},{9,25},{17,1},{25,9},{2,18},{10... | collective-permute-start | bytes 2359304 | tf_op jit(solution)/shard_map/ppermute | solution.py:70
  55.2 53.2 %collective-permute-start.1 = (bf16[384,1024]{1,0:T(8,128)(2,1)S(1)}, bf16[384,1024]{1,0:T(8,128)(2,1)S(1)}, u32[]{:S(2)}, u32[]{:S(2)}) collective-permute-start(bf16[384,1024]{1,0:T(8,128)(2,1)S(1)} %bitcast.92), channel_id=1, source_target_pairs={{0,8},{8,0},{16,24},{24,16},{1,9},{9,1},{17,25},{25,17},{2,10},{10... | collective-permute-start | bytes 2359304 | tf_op jit(solution)/shard_map/ppermute | solution.py:70
  58.6 29.3 %collective-permute-start.8 = (bf16[128,1152]{0,1:T(8,128)(2,1)S(1)}, bf16[128,1152]{0,1:T(8,128)(2,1)S(1)}, u32[]{:S(2)}, u32[]{:S(2)}) collective-permute-start(bf16[128,1152]{0,1:T(8,128)(2,1)S(1)} %copy-done.73), channel_id=1, source_target_pairs={{0,1},{1,0},{2,3},{3,2},{4,5},{5,4},{6,7},{7,6},{8,9},{9,8},{10,11... | collective-permute-start | bytes 884744 | tf_op jit(solution)/shard_map/ppermute | solution.py:535
  58.6 25.8 %collective-permute-start.9 = (bf16[128,1152]{0,1:T(8,128)(2,1)S(1)}, bf16[128,1152]{0,1:T(8,128)(2,1)S(1)}, u32[]{:S(2)}, u32[]{:S(2)}) collective-permute-start(bf16[128,1152]{0,1:T(8,128)(2,1)S(1)} %copy-done.73), channel_id=1, source_target_pairs={{0,2},{1,3},{2,0},{3,1},{4,6},{5,7},{6,4},{7,5},{8,10},{9,11},{10,... | collective-permute-start | bytes 884744 | tf_op jit(solution)/shard_map/ppermute | solution.py:535
  59.9 26.5 %collective-permute-start.6 = (bf16[128,1152]{0,1:T(8,128)(2,1)}, bf16[128,1152]{0,1:T(8,128)(2,1)S(1)}, u32[]{:S(2)}, u32[]{:S(2)}) collective-permute-start(bf16[128,1152]{0,1:T(8,128)(2,1)} %collective-permute-done.5), channel_id=1, source_target_pairs={{0,1},{1,0},{2,3},{3,2},{4,5},{5,4},{6,7},{7,6},{8,9},{9,8},{10,11... | collective-permute-start | bytes 884744 | tf_op jit(solution)/shard_map/ppermute | solution.py:535
  89.4 35.8 %collective-permute-start.13 = (bf16[384,1024]{1,0:T(8,128)(2,1)S(1)}, bf16[384,1024]{1,0:T(8,128)(2,1)}, u32[]{:S(2)}, u32[]{:S(2)}) collective-permute-start(bf16[384,1024]{1,0:T(8,128)(2,1)S(1)} %bitcast.95), channel_id=1, source_target_pairs={{0,8},{8,0},{16,24},{24,16},{1,9},{9,1},{17,25},{25,17},{2,10},{10... | collective-permute-start | bytes 2359304 | tf_op jit(solution)/shard_map/ppermute | solution.py:70
  125.0 428.9 %reduce-scatter.4.cloned.1.call-start = ((), (), s32[]{:S(2)}) async-start(), calls=%async_computation.5 | async-start | bytes 7962624 | tf_op jit(solution)/shard_map/reduce_scatter | solution.py:530
  308.1 20.1 %collective-permute-start.29 = (bf16[384,1024]{1,0:T(8,128)(2,1)S(1)}, bf16[384,1024]{1,0:T(8,128)(2,1)}, u32[]{:S(2)}, u32[]{:S(2)}) collective-permute-start(bf16[384,1024]{1,0:T(8,128)(2,1)S(1)} %multiply_convert_fusion.refs_0_), channel_id=1, source_target_pairs={{0,16},{8,24},{16,0},{24,8},{1,17},{9,25},{17,1},{25,9},{2,18},{10... | collective-permute-start | bytes 2359304 | tf_op jit(solution)/shard_map/ppermute | solution.py:70
  389.0 271.2 %reduce-scatter.6.cloned.1.call-start = ((), (), s32[]{:S(2)}) async-start(), calls=%async_computation.6 | async-start | bytes 7077888 | tf_op jit(solution)/shard_map/reduce_scatter | solution.py:530
  463.8 20.0 %collective-permute-start.41 = (bf16[384,1024]{1,0:T(8,128)(2,1)S(1)}, bf16[384,1024]{1,0:T(8,128)(2,1)S(1)}, u32[]{:S(2)}, u32[]{:S(2)}) collective-permute-start(bf16[384,1024]{1,0:T(8,128)(2,1)S(1)} %get-tuple-element.383.refs_0_), channel_id=1, source_target_pairs={{0,16},{8,24},{16,0},{24,8},{1,17},{9,25},{17,1},{25,9},{2,18},{10... | collective-permute-start | bytes 2359304 | tf_op jit(solution)/shard_map/ppermute | solution.py:70
  499.3 19.8 %collective-permute-start.45 = (bf16[384,1024]{1,0:T(8,128)(2,1)S(1)}, bf16[384,1024]{1,0:T(8,128)(2,1)}, u32[]{:S(2)}, u32[]{:S(2)}) collective-permute-start(bf16[384,1024]{1,0:T(8,128)(2,1)S(1)} %add_convert_fusion.2), channel_id=1, source_target_pairs={{0,16},{8,24},{16,0},{24,8},{1,17},{9,25},{17,1},{25,9},{2,18},{10... | collective-permute-start | bytes 2359304 | tf_op jit(solution)/shard_map/ppermute | solution.py:70
  524.0 185.4 %reduce-scatter.8.cloned.1.call-start = ((), (), s32[]{:S(2)}) async-start(), calls=%async_computation.7 | async-start | bytes 2785280 | tf_op jit(solution)/shard_map/reduce_scatter | solution.py:590
  568.6 27.7 %collective-permute-start.54 = (bf16[384,1024]{1,0:T(8,128)(2,1)}, bf16[384,1024]{1,0:T(8,128)(2,1)}, u32[]{:S(2)}, u32[]{:S(2)}) collective-permute-start(bf16[384,1024]{1,0:T(8,128)(2,1)} %slice.337), channel_id=1, source_target_pairs={{0,8},{8,0},{16,24},{24,16},{1,9},{9,1},{17,25},{25,17},{2,10},{10... | collective-permute-start | bytes 2359304 | tf_op jit(solution)/shard_map/ppermute | solution.py:70
  591.7 22.7 %collective-permute-start.58 = (bf16[128,3456]{1,0:T(8,128)(2,1)}, bf16[128,3456]{1,0:T(8,128)(2,1)S(1)}, u32[]{:S(2)}, u32[]{:S(2)}) collective-permute-start(bf16[128,3456]{1,0:T(8,128)(2,1)} %reduce-scatter.4.cloned.1.call-done.refs_1_), channel_id=1, source_target_pairs={{0,16},{8,24},{16,0},{24,8},{1,17},{9,25},{17,1},{25,9},{2,18},{10... | collective-permute-start | bytes 2654216 | tf_op jit(solution)/shard_map/ppermute | solution.py:70
  596.4 60.3 %collective-permute-start.50 = (bf16[512,2176]{1,0:T(8,128)(2,1)S(1)}, bf16[512,2176]{1,0:T(8,128)(2,1)}, u32[]{:S(2)}, u32[]{:S(2)}) collective-permute-start(bf16[512,2176]{1,0:T(8,128)(2,1)S(1)} %bitcast.109), channel_id=1, source_target_pairs={{0,1},{1,0},{2,3},{3,2},{4,5},{5,4},{6,7},{7,6},{8,9},{9,8},{10,11... | collective-permute-start | bytes 6684680 | tf_op jit(solution)/shard_map/ppermute | solution.py:535
  598.4 32.9 %collective-permute-start.55 = (bf16[384,1024]{1,0:T(8,128)(2,1)S(1)}, bf16[384,1024]{1,0:T(8,128)(2,1)S(1)}, u32[]{:S(2)}, u32[]{:S(2)}) collective-permute-start(bf16[384,1024]{1,0:T(8,128)(2,1)S(1)} %add_convert_fusion), channel_id=1, source_target_pairs={{0,16},{8,24},{16,0},{24,8},{1,17},{9,25},{17,1},{25,9},{2,18},{10... | collective-permute-start | bytes 2359304 | tf_op jit(solution)/shard_map/ppermute | solution.py:70
  600.2 47.1 %collective-permute-start.52 = (bf16[384,1024]{1,0:T(8,128)(2,1)S(1)}, bf16[384,1024]{1,0:T(8,128)(2,1)S(1)}, u32[]{:S(2)}, u32[]{:S(2)}) collective-permute-start(bf16[384,1024]{1,0:T(8,128)(2,1)S(1)} %get-tuple-element.394), channel_id=1, source_target_pairs={{0,16},{8,24},{16,0},{24,8},{1,17},{9,25},{17,1},{25,9},{2,18},{10... | collective-permute-start | bytes 2359304 | tf_op jit(solution)/shard_map/ppermute | solution.py:70
  601.2 50.6 %collective-permute-start.57 = (bf16[128,3456]{1,0:T(8,128)(2,1)}, bf16[128,3456]{1,0:T(8,128)(2,1)S(1)}, u32[]{:S(2)}, u32[]{:S(2)}) collective-permute-start(bf16[128,3456]{1,0:T(8,128)(2,1)} %reduce-scatter.4.cloned.1.call-done.refs_1_), channel_id=1, source_target_pairs={{0,8},{8,0},{16,24},{24,16},{1,9},{9,1},{17,25},{25,17},{2,10},{10... | collective-permute-start | bytes 2654216 | tf_op jit(solution)/shard_map/ppermute | solution.py:70
  614.4 37.5 %collective-permute-start.59 = (bf16[128,3456]{1,0:T(8,128)(2,1)S(1)}, bf16[128,3456]{1,0:T(8,128)(2,1)S(1)}, u32[]{:S(2)}, u32[]{:S(2)}) collective-permute-start(bf16[128,3456]{1,0:T(8,128)(2,1)S(1)} %collective-permute-done.58.refs_3_), channel_id=1, source_target_pairs={{0,8},{8,0},{16,24},{24,16},{1,9},{9,1},{17,25},{25,17},{2,10},{10... | collective-permute-start | bytes 2654216 | tf_op jit(solution)/shard_map/ppermute | solution.py:70
  673.0 23.3 %collective-permute-start.60 = (bf16[128,2816]{1,0:T(8,128)(2,1)S(1)}, bf16[128,2816]{1,0:T(8,128)(2,1)S(1)}, u32[]{:S(2)}, u32[]{:S(2)}) collective-permute-start(bf16[128,2816]{1,0:T(8,128)(2,1)S(1)} %slice.340.refs_1_), channel_id=1, source_target_pairs={{0,8},{8,0},{16,24},{24,16},{1,9},{9,1},{17,25},{25,17},{2,10},{10... | collective-permute-start | bytes 2162696 | tf_op jit(solution)/shard_map/ppermute | solution.py:70
  (151 other events, 1417.1 us)
Sparse Core Ops, SparseCore 0:
  36.1 148.1 all-gather.2
  187.0 106.9 all-gather.4
  389.1 127.1 reduce-scatter.3
  524.1 125.8 reduce-scatter.5
  660.3 49.0 reduce-scatter.7

commit v5 on v4

--- a/solution.py
+++ b/solution.py
@@ -573,16 +573,23 @@
     return sums[0].astype(BF16)
 
 
-def dp_scatter_pairs(grads, work, later):
+def dp_pair_parts(grads):
     if not dp_bits():
-        grads, later, *work = tie(grads, later, *work)
-        return (dp_scatter(grads), work, later)
+        return (grads, grads[:8])
     size = lax.axis_size("dp")
     side = lax.axis_index("dp") % 2
     columns = grads.shape[1]
     blocks = grads.reshape(size // 2, 2, -1, columns)
     kept = lax.dynamic_index_in_dim(blocks, side, 1, False).reshape(-1, columns)
     sent = lax.dynamic_index_in_dim(blocks, 1 - side, 1, False).reshape(-1, columns)
+    return (kept, sent)
+
+
+def dp_scatter_pairs(kept, sent, work, later):
+    if not dp_bits():
+        kept, later, *work = tie(kept, later, *work)
+        return (dp_scatter(kept), work, later)
+    size = lax.axis_size("dp")
     got, *work = tie(swap_dp(sent, 1), *work)
     sums = (kept.astype(F32) + got.astype(F32)).astype(BF16)
     sums, later = tie(sums, later)
@@ -1164,7 +1171,8 @@
     grads_mix = jnp.concatenate(
         [d_down, d_w_in.astype(BF16), pack_rows(d_w_out.astype(BF16), dp_count)], 1
     )
-    grads_mix, kept_two = tie(grads_mix, kept_two)
+    kept_mix, sent_mix = dp_pair_parts(grads_mix)
+    sent_mix, kept_two = tie(sent_mix, kept_two)
     d_normed = seq_scatter(near_out, far_out)
     unit_one, scale_one = unit_scale(x_flat)
     d_x_part, d_gain_mix = norm_back(d_normed, gain_mix, unit_one, scale_one)
@@ -1194,11 +1202,12 @@
     ffn_out = right_dot(kept_two[:, 2 * hidden :], ffn_two[:, 2 * hidden :])
     hidden_four = hidden_three + seq_scatter(*halves_of(ffn_out))
     out = hidden_four.astype(BF16).reshape(rows, length, width)
+    shared_two = share(owned_two)
+    owned_mix, (out, d_x, *shared_two), owned_one = dp_scatter_pairs(
+        kept_mix, sent_mix, (out, d_x, *shared_two), owned_one
+    )
     d_wgate_two, d_wup_two, d_down_two = assemble(
-        place, share(owned_two), [(n * hidden, hidden, 1, False) for n in range(3)]
-    )
-    owned_mix, (out, d_x, d_wgate_two, d_wup_two, d_down_two), owned_one = dp_scatter_pairs(
-        grads_mix, (out, d_x, d_wgate_two, d_wup_two, d_down_two), owned_one
+        place, shared_two, [(n * hidden, hidden, 1, False) for n in range(3)]
     )
     tasks = [(n * hidden, hidden, 1, False) for n in range(2)]
     for columns in (channels, kv_width, kv_width):
@@ -1210,8 +1219,8 @@
         place, share(redeal(owned_one[:, -channels:])), [(0, channels, 1, True)]
     )
     shared_vectors = share(owned_vectors)
-    owned_mix, d_wgate_one, d_w_o_full, *shared_vectors = tie(
-        owned_mix, d_wgate_one, d_w_o_full, *shared_vectors
+    owned_mix, d_wgate_one, d_w_o_full, d_wgate_two, *shared_vectors = tie(
+        owned_mix, d_wgate_one, d_w_o_full, d_wgate_two, *shared_vectors
     )
     shared_mix = share(owned_mix[:, :-channels])
     shared_out = share(redeal(owned_mix[:, -channels:]))

time: 748 us -> 743 us (level)
    reduce_scatter x1, waiting for transfers between devices: 9.9 us -> 0.63 us  [dp_scatter_pairs(): lax.psum_scatter(sums, 'dp', scatter_dimension=0, tiled=True, axis_index_...]
    unnamed x194 -> x198, local copies, waits for them, and re-layouts: 27.4 us -> 32.2 us
where the time goes in v5:
time: 743 us; the launch traced here: 735 us
  waiting for transfers between devices  285 us (38%)
  Pallas kernels  166 us (22%)
  starting transfers between devices  80.3 us (11%)
  local copies, waits for them, and re-layouts  76.8 us (10%)
  matrix products  61 us (8%)
  other arithmetic  50.7 us (7%)
  between operations  15.7 us (2%)
    ppermute x66, waiting for transfers between devices, swap_seq(): return lax.ppermute(array, 'seq', [(i, i ^ bit) for i in range(size)])  231 us
    pallas_call x5, Pallas kernels, ffn_call(): pl.pallas_call(lambda *refs: kernel(*refs, count=count), grid=(count,), i...  69.1 us
    dot_general x8, matrix products, left_dot(): lax.dot_general(left, right, (((0,), (0,)), ((), ())), preferred_element_...  53.8 us
    ppermute x66, starting transfers between devices, swap_seq(): return lax.ppermute(array, 'seq', [(i, i ^ bit) for i in range(size)])  41.8 us
    ppermute x11, waiting for transfers between devices, swap_dp(): return lax.ppermute(array, 'dp', [(i, i ^ bit) for i in range(size)])  39.3 us
    pallas_call x1, Pallas kernels, attention_backward(): pl.pallas_call(lambda *refs: attention_backward_kernel(*refs, length=leng...  37.2 us
    ppermute x11, starting transfers between devices, swap_dp(): return lax.ppermute(array, 'dp', [(i, i ^ bit) for i in range(size)])  35.8 us
    unnamed x198, local copies, waits for them, and re-layouts  32.2 us
  transfers between devices with their start and end apart: 85, of which 45 were waited for; matrix products, arithmetic and copies ran while one was open for 22% of the time, Pallas kernels for 20%

profile of v5, /device:TPU:0, one launch (start us, length us, event | category | flops | bytes accessed | tf_op | source)
XLA Modules:
  0.0 734.9 jit_solution(16878402731321233704)
XLA Ops:
  11.5 18.0 %collective-permute-start.7 = (bf16[128,1152]{0,1:T(8,128)(2,1)}, bf16[128,1152]{0,1:T(8,128)(2,1)S(1)}, u32[]{:S(2)}, u32[]{:S(2)}) collective-permute-start(bf16[128,1152]{0,1:T(8,128)(2,1)} %fusion.87), channel_id=1, source_target_pairs={{0,4},{1,5},{2,6},{3,7},{4,0},{5,1},{6,2},{7,3},{8,12},{9,13},{10,... | collective-permute-start | bytes 884744 | tf_op jit(solution)/shard_map/ppermute | solution.py:535
  65.3 19.1 %collective-permute-done.9 = bf16[128,1152]{0,1:T(8,128)(2,1)S(1)} collective-permute-done((bf16[128,1152]{0,1:T(8,128)(2,1)S(1)}, bf16[128,1152]{0,1:T(8,128)(2,1)S(1)}, u32[]{:S(2)}, u32[]{:S(2)}) %collective-permute-start.9) | collective-permute-done | bytes 294944 | tf_op jit(solution)/shard_map/ppermute | solution.py:535
  110.5 9.9 %conv_forward.1 = (bf16[1536,1024]{1,0:T(8,128)(2,1)}, f32[1536,768]{1,0:T(8,128)}, bf16[1536,256]{1,0:T(8,128)(2,1)S(1)}, bf16[768,1024]{1,0:T(8,128)(2,1)S(1)}, bf16[768,1024]{1,0:T(8,128)(2,1)}) custom-call(s32[1]{0:T(128)} %bitcast.2.refs_0_, s32[4]{0:T(128)S(1)} %bitcast.105, bf16[384,1024]{1,0:T(8,128)(2,1)S(1)} %bitcast.94, ...), custom_call_target="tpu_custom_call" | custom-call | flops 4000000000 | bytes 20000000 | tf_op jit(solution)/shard_map/conv_forward/pallas_call | solution.py:972
  135.1 12.5 %collective-permute-done.12 = bf16[384,1024]{1,0:T(8,128)(2,1)S(1)} collective-permute-done((bf16[384,1024]{1,0:T(8,128)(2,1)S(1)}, bf16[384,1024]{1,0:T(8,128)(2,1)S(1)}, u32[]{:S(2)}, u32[]{:S(2)}) %collective-permute-start.12) | collective-permute-done | bytes 786464 | tf_op jit(solution)/shard_map/ppermute | solution.py:70
  149.7 18.0 %collective-permute-done.18.refs_2_ = bf16[384,1024]{1,0:T(8,128)(2,1)S(1)} collective-permute-done((bf16[384,1024]{1,0:T(8,128)(2,1)S(1)}, bf16[384,1024]{1,0:T(8,128)(2,1)S(1)}, u32[]{:S(2)}, u32[]{:S(2)}) %collective-permute-start.18) | collective-permute-done | bytes 786464 | tf_op jit(solution)/shard_map/ppermute | solution.py:70
  170.9 13.4 %all-gather.3.cloned.1.call-done.refs_4_.refs_5_.refs_6_.refs_3_ = bf16[1024,4224]{1,0:T(8,128)(2,1)} async-done(((bf16[128,4224]{1,0:T(8,128)(2,1)}), bf16[1024,4224]{1,0:T(8,128)(2,1)}) %all-gather.3.cloned.1.call-update) | async-done | bytes 8650768 | tf_op jit(solution)/shard_map/all_gather | solution.py:526
  185.4 18.3 %ffn_forward.1 = (bf16[1536,3456]{1,0:T(8,128)(2,1)}, bf16[1536,1024]{1,0:T(8,128)(2,1)}) custom-call(bf16[384,1024]{1,0:T(8,128)(2,1)S(1)} %multiply_convert_fusion.2.refs_0_, bf16[384,1024]{1,0:T(8,128)(2,1)S(1)} %collective-permute-done.17.refs_1_, bf16[384,1024]{1,0:T(8,128)(2,1)S(1)} %collective-permute-done.18.refs_2_, ...), custom_call_target="tpu_custom_call" | custom-call | flops 6000000000 | bytes 20000000 | tf_op jit(solution)/shard_map/ffn_forward/pallas_call | solution.py:750
  214.8 15.7 %collective-permute-done.21 = bf16[384,1024]{1,0:T(8,128)(2,1)S(1)} collective-permute-done((bf16[384,1024]{1,0:T(8,128)(2,1)S(1)}, bf16[384,1024]{1,0:T(8,128)(2,1)S(1)}, u32[]{:S(2)}, u32[]{:S(2)}) %collective-permute-start.21) | collective-permute-done | bytes 786464 | tf_op jit(solution)/shard_map/ppermute | solution.py:70
  234.6 17.6 %collective-permute-done.24.refs_3_ = bf16[384,1024]{1,0:T(8,128)(2,1)} collective-permute-done((bf16[384,1024]{1,0:T(8,128)(2,1)}, bf16[384,1024]{1,0:T(8,128)(2,1)}, u32[]{:S(2)}, u32[]{:S(2)}) %collective-permute-start.24) | collective-permute-done | bytes 786464 | tf_op jit(solution)/shard_map/ppermute | solution.py:70
  255.8 27.0 %attention_forward.1 = (f32[1536,512]{1,0:T(8,128)}, bf16[1536,256]{1,0:T(8,128)(2,1)S(1)}, f32[256,1536]{1,0:T(8,128)}, f32[8,1536]{1,0:T(8,128)S(1)}, bf16[768...) custom-call(s32[1]{0:T(128)} %bitcast.2.refs_0_, bf16[384,1024]{1,0:T(8,128)(2,1)} %multiply_convert_fusion.1.refs_1_, ...), custom_call_target="tpu_custom_call" | custom-call | flops 20000000000 | bytes 20000000 | tf_op jit(solution)/shard_map/attention_forward/pallas_call | solution.py:405
  288.8 17.8 %collective-permute-done.27 = bf16[384,1024]{1,0:T(8,128)(2,1)S(1)} collective-permute-done((bf16[384,1024]{1,0:T(8,128)(2,1)S(1)}, bf16[384,1024]{1,0:T(8,128)(2,1)S(1)}, u32[]{:S(2)}, u32[]{:S(2)}) %collective-permute-start.27) | collective-permute-done | bytes 786464 | tf_op jit(solution)/shard_map/ppermute | solution.py:70
  310.4 14.8 %ffn_turn.2 = (bf16[1536,3456]{1,0:T(8,128)(2,1)}, bf16[768,1024]{1,0:T(8,128)(2,1)S(1)}) custom-call(bf16[384,1024]{1,0:T(8,128)(2,1)S(1)} %multiply_convert_fusion.refs_0_, bf16[384,1024]{1,0:T(8,128)(2,1)S(1)} %collective-permute-done.30.refs_1_, bf16[384,1024]{1,0:T(8,128)(2,1)S(1)} %bitcast.97, bf16[384,1024]{1,0:T(8,128)(2,1)} %collective-permute-done.13.refs_3_, ...), custom_call_target="tpu_custom_call" | custom-call | flops 6000000000 | bytes 20000000 | tf_op jit(solution)/shard_map/ffn_turn/pallas_call | solution.py:750
  330.7 14.8 %ffn_turn.3 = (bf16[1536,3456]{1,0:T(8,128)(2,1)}, bf16[768,1024]{1,0:T(8,128)(2,1)S(1)}) custom-call(bf16[384,1024]{1,0:T(8,128)(2,1)} %collective-permute-done.29.refs_0_, bf16[384,1024]{1,0:T(8,128)(2,1)S(1)} %collective-permute-done.31.refs_1_, bf16[384,1024]{1,0:T(8,128)(2,1)} %collective-permute-done.14.refs_2_, ...), custom_call_target="tpu_custom_call", output_to_operand_aliasing={{0}: (7, {})} | custom-call | flops 6000000000 | bytes 20000000 | tf_op jit(solution)/shard_map/ffn_turn/pallas_call | solution.py:750
  349.8 12.6 %fusion.2 = bf16[1024,2304]{1,0:T(8,128)(2,1)} fusion(bf16[1536,3456]{1,0:T(8,128)(2,1)} %get-tuple-element.205, bf16[384,1024]{1,0:T(8,128)(2,1)S(1)} %collective-permute-done.31.refs_1_, bf16[384,1024]{1,0:T(8,128)(2,1)} %collective-permute-done.29.refs_0_, bf16[384,1024]{1,0:T(8,128)(2,1)S(1)} %collective-permute-done.30.refs_1_, ...), kind=kOutput, calls=%fused_computation.5 | convolution fusion | flops 7262699520 | bytes 14942208 | tf_op jit(solution)/shard_map/dot_general | solution.py:19
  394.0 37.2 %attention_backward.1 = (bf16[1536,512]{1,0:T(8,128)(2,1)}, bf16[768,1024]{1,0:T(8,128)(2,1)}, bf16[768,1024]{1,0:T(8,128)(2,1)}, f32[2,128]{1,0:T(2,128)S(1)}) custom-call(s32[1]{0:T(128)} %bitcast.2.refs_0_, bf16[384,1024]{1,0:T(8,128)(2,1)S(1)} %get-tuple-element.389.refs_1_, bf16[384,1024]{1,0:T(8,128)(2,1)S(1)} %collective-permute-done.35.refs_2_, ...), custom_call_target="tpu_custom_call" | custom-call | flops 20000000000 | bytes 20000000 | tf_op jit(solution)/shard_map/attention_backward/pallas_call | solution.py:437
  446.7 14.0 %collective-permute-done.39 = bf16[384,1024]{1,0:T(8,128)(2,1)S(1)} collective-permute-done((bf16[384,1024]{1,0:T(8,128)(2,1)S(1)}, bf16[384,1024]{1,0:T(8,128)(2,1)S(1)}, u32[]{:S(2)}, u32[]{:S(2)}) %collective-permute-start.39) | collective-permute-done | bytes 786464 | tf_op jit(solution)/shard_map/ppermute | solution.py:70
  466.1 10.7 %ffn_backward.2 = (bf16[1536,2304]{1,0:T(8,128)(2,1)}, bf16[768,1024]{1,0:T(8,128)(2,1)S(1)}) custom-call(bf16[384,1024]{1,0:T(8,128)(2,1)S(1)} %get-tuple-element.387.refs_0_, bf16[384,1024]{1,0:T(8,128)(2,1)S(1)} %collective-permute-done.42.refs_1_, bf16[1536,3456]{1,0:T(8,128)(2,1)} %get-tuple-element.187.refs_2_, ...), custom_call_target="tpu_custom_call" | custom-call | flops 6000000000 | bytes 20000000 | tf_op jit(solution)/shard_map/ffn_backward/pallas_call | solution.py:750
  486.1 10.5 %ffn_backward.3 = (bf16[1536,2304]{1,0:T(8,128)(2,1)}, bf16[768,1024]{1,0:T(8,128)(2,1)S(1)}) custom-call(bf16[384,1024]{1,0:T(8,128)(2,1)S(1)} %collective-permute-done.41.refs_0_, bf16[384,1024]{1,0:T(8,128)(2,1)S(1)} %collective-permute-done.43.refs_1_, bf16[1536,3456]{1,0:T(8,128)(2,1)} %get-tuple-element.187.refs_2_, ...), custom_call_target="tpu_custom_call", output_to_operand_aliasing={{0}: (6, {})} | custom-call | flops 6000000000 | bytes 20000000 | tf_op jit(solution)/shard_map/ffn_backward/pallas_call | solution.py:750
  501.1 10.7 %convolution_convert_fusion = bf16[1024,2304]{1,0:T(8,128)(2,1)S(1)} fusion(bf16[1536,2304]{1,0:T(8,128)(2,1)} %get-tuple-element.193, bf16[384,1024]{1,0:T(8,128)(2,1)S(1)} %copy-done.26, bf16[384,1024]{1,0:T(8,128)(2,1)S(1)} %copy-done.21, bf16[384,1024]{1,0:T(8,128)(2,1)S(1)} %copy-done.23, bf16[384,1024]{1,0:T(8,128)(2,1)S(1)} %multiply_convert_fusion.2.refs_0_), kind=kOutput, calls=%fused_computation.4 | convolution fusion | flops 7262699520 | bytes 14942208 | tf_op jit(solution)/shard_map/dot_general | solution.py:19
  555.1 10.3 %conv_backward.1 = (bf16[1536,768]{1,0:T(8,128)(2,1)}, bf16[768,1024]{1,0:T(8,128)(2,1)S(1)}, bf16[768,1024]{1,0:T(8,128)(2,1)}, f32[3,256]{1,0:T(4,128)S(1)}) custom-call(s32[1]{0:T(128)} %bitcast.2.refs_0_, s32[4]{0:T(128)S(1)} %bitcast.107, bf16[384,1024]{1,0:T(8,128)(2,1)S(1)} %get-tuple-element.385.refs_2_, ...), custom_call_target="tpu_custom_call" | custom-call | bytes 100000 | tf_op jit(solution)/shard_map/conv_backward/pallas_call | solution.py:906
  594.4 16.5 %collective-permute-done.58.refs_3_ = bf16[128,3456]{1,0:T(8,128)(2,1)S(1)} collective-permute-done((bf16[128,3456]{1,0:T(8,128)(2,1)S(1)}, bf16[128,3456]{1,0:T(8,128)(2,1)S(1)}, u32[]{:S(2)}, u32[]{:S(2)}) %collective-permute-start.58) | collective-permute-done | bytes 884768 | tf_op jit(solution)/shard_map/ppermute | solution.py:70
  610.8 16.8 %collective-permute-done.55 = bf16[384,1024]{1,0:T(8,128)(2,1)S(1)} collective-permute-done((bf16[384,1024]{1,0:T(8,128)(2,1)S(1)}, bf16[384,1024]{1,0:T(8,128)(2,1)S(1)}, u32[]{:S(2)}, u32[]{:S(2)}) %collective-permute-start.55) | collective-permute-done | bytes 786464 | tf_op jit(solution)/shard_map/ppermute | solution.py:70
  627.7 15.8 %collective-permute-done.52 = bf16[384,1024]{1,0:T(8,128)(2,1)S(1)} collective-permute-done((bf16[384,1024]{1,0:T(8,128)(2,1)S(1)}, bf16[384,1024]{1,0:T(8,128)(2,1)S(1)}, u32[]{:S(2)}, u32[]{:S(2)}) %collective-permute-start.52) | collective-permute-done | bytes 786464 | tf_op jit(solution)/shard_map/ppermute | solution.py:70
  708.3 10.6 %collective-permute-done.74.refs_3_ = bf16[128,1920]{1,0:T(8,128)(2,1)S(1)} collective-permute-done((bf16[128,1920]{1,0:T(8,128)(2,1)S(1)}, bf16[128,1920]{1,0:T(8,128)(2,1)S(1)}, u32[]{:S(2)}, u32[]{:S(2)}) %collective-permute-start.74) | collective-permute-done | bytes 491552 | tf_op jit(solution)/shard_map/ppermute | solution.py:70
  (510 shorter events, 336.6 us)
Async XLA Ops:
  7.2 177.0 %all-gather.3.cloned.1.call-start = ((), (), s32[]{:S(2)}) async-start(), calls=%async_computation.3 | async-start | bytes 9732096 | tf_op jit(solution)/shard_map/all_gather | solution.py:526
  11.5 23.5 %collective-permute-start.7 = (bf16[128,1152]{0,1:T(8,128)(2,1)}, bf16[128,1152]{0,1:T(8,128)(2,1)S(1)}, u32[]{:S(2)}, u32[]{:S(2)}) collective-permute-start(bf16[128,1152]{0,1:T(8,128)(2,1)} %fusion.87), channel_id=1, source_target_pairs={{0,4},{1,5},{2,6},{3,7},{4,0},{5,1},{6,2},{7,3},{8,12},{9,13},{10,... | collective-permute-start | bytes 884744 | tf_op jit(solution)/shard_map/ppermute | solution.py:535
  36.0 273.6 %all-gather.5.cloned.1.call-start = ((), (), s32[]{:S(2)}) async-start(), calls=%async_computation.4 | async-start | bytes 7962624 | tf_op jit(solution)/shard_map/all_gather | solution.py:526
  37.9 20.7 %collective-permute-start.4 = (bf16[128,1152]{0,1:T(8,128)(2,1)}, bf16[128,1152]{0,1:T(8,128)(2,1)}, u32[]{:S(2)}, u32[]{:S(2)}) collective-permute-start(bf16[128,1152]{0,1:T(8,128)(2,1)} %fusion.87), channel_id=1, source_target_pairs={{0,1},{1,0},{2,3},{3,2},{4,5},{5,4},{6,7},{7,6},{8,9},{9,8},{10,11... | collective-permute-start | bytes 884744 | tf_op jit(solution)/shard_map/ppermute | solution.py:535
  49.3 40.0 %collective-permute-start.2 = (bf16[384,1024]{1,0:T(8,128)(2,1)S(1)}, bf16[384,1024]{1,0:T(8,128)(2,1)S(1)}, u32[]{:S(2)}, u32[]{:S(2)}) collective-permute-start(bf16[384,1024]{1,0:T(8,128)(2,1)S(1)} %bitcast.92), channel_id=1, source_target_pairs={{0,16},{8,24},{16,0},{24,8},{1,17},{9,25},{17,1},{25,9},{2,18},{10... | collective-permute-start | bytes 2359304 | tf_op jit(solution)/shard_map/ppermute | solution.py:70
  55.2 53.2 %collective-permute-start.1 = (bf16[384,1024]{1,0:T(8,128)(2,1)S(1)}, bf16[384,1024]{1,0:T(8,128)(2,1)S(1)}, u32[]{:S(2)}, u32[]{:S(2)}) collective-permute-start(bf16[384,1024]{1,0:T(8,128)(2,1)S(1)} %bitcast.93), channel_id=1, source_target_pairs={{0,8},{8,0},{16,24},{24,16},{1,9},{9,1},{17,25},{25,17},{2,10},{10... | collective-permute-start | bytes 2359304 | tf_op jit(solution)/shard_map/ppermute | solution.py:70
  58.6 29.3 %collective-permute-start.8 = (bf16[128,1152]{0,1:T(8,128)(2,1)S(1)}, bf16[128,1152]{0,1:T(8,128)(2,1)S(1)}, u32[]{:S(2)}, u32[]{:S(2)}) collective-permute-start(bf16[128,1152]{0,1:T(8,128)(2,1)S(1)} %copy-done.77), channel_id=1, source_target_pairs={{0,1},{1,0},{2,3},{3,2},{4,5},{5,4},{6,7},{7,6},{8,9},{9,8},{10,11... | collective-permute-start | bytes 884744 | tf_op jit(solution)/shard_map/ppermute | solution.py:535
  58.6 25.8 %collective-permute-start.9 = (bf16[128,1152]{0,1:T(8,128)(2,1)S(1)}, bf16[128,1152]{0,1:T(8,128)(2,1)S(1)}, u32[]{:S(2)}, u32[]{:S(2)}) collective-permute-start(bf16[128,1152]{0,1:T(8,128)(2,1)S(1)} %copy-done.77), channel_id=1, source_target_pairs={{0,2},{1,3},{2,0},{3,1},{4,6},{5,7},{6,4},{7,5},{8,10},{9,11},{10,... | collective-permute-start | bytes 884744 | tf_op jit(solution)/shard_map/ppermute | solution.py:535
  59.9 26.5 %collective-permute-start.6 = (bf16[128,1152]{0,1:T(8,128)(2,1)}, bf16[128,1152]{0,1:T(8,128)(2,1)S(1)}, u32[]{:S(2)}, u32[]{:S(2)}) collective-permute-start(bf16[128,1152]{0,1:T(8,128)(2,1)} %collective-permute-done.5), channel_id=1, source_target_pairs={{0,1},{1,0},{2,3},{3,2},{4,5},{5,4},{6,7},{7,6},{8,9},{9,8},{10,11... | collective-permute-start | bytes 884744 | tf_op jit(solution)/shard_map/ppermute | solution.py:535
  89.4 35.8 %collective-permute-start.13 = (bf16[384,1024]{1,0:T(8,128)(2,1)S(1)}, bf16[384,1024]{1,0:T(8,128)(2,1)}, u32[]{:S(2)}, u32[]{:S(2)}) collective-permute-start(bf16[384,1024]{1,0:T(8,128)(2,1)S(1)} %bitcast.96), channel_id=1, source_target_pairs={{0,8},{8,0},{16,24},{24,16},{1,9},{9,1},{17,25},{25,17},{2,10},{10... | collective-permute-start | bytes 2359304 | tf_op jit(solution)/shard_map/ppermute | solution.py:70
  89.5 19.8 %collective-permute-start.3 = (bf16[384,1024]{1,0:T(8,128)(2,1)S(1)}, bf16[384,1024]{1,0:T(8,128)(2,1)}, u32[]{:S(2)}, u32[]{:S(2)}) collective-permute-start(bf16[384,1024]{1,0:T(8,128)(2,1)S(1)} %collective-permute-done.2.refs_4_), channel_id=1, source_target_pairs={{0,8},{8,0},{16,24},{24,16},{1,9},{9,1},{17,25},{25,17},{2,10},{10... | collective-permute-start | bytes 2359304 | tf_op jit(solution)/shard_map/ppermute | solution.py:70
  125.0 428.9 %reduce-scatter.4.cloned.1.call-start = ((), (), s32[]{:S(2)}) async-start(), calls=%async_computation.5 | async-start | bytes 7962624 | tf_op jit(solution)/shard_map/reduce_scatter | solution.py:530
  308.1 20.1 %collective-permute-start.29 = (bf16[384,1024]{1,0:T(8,128)(2,1)S(1)}, bf16[384,1024]{1,0:T(8,128)(2,1)}, u32[]{:S(2)}, u32[]{:S(2)}) collective-permute-start(bf16[384,1024]{1,0:T(8,128)(2,1)S(1)} %multiply_convert_fusion.refs_0_), channel_id=1, source_target_pairs={{0,16},{8,24},{16,0},{24,8},{1,17},{9,25},{17,1},{25,9},{2,18},{10... | collective-permute-start | bytes 2359304 | tf_op jit(solution)/shard_map/ppermute | solution.py:70
  389.0 267.8 %reduce-scatter.6.cloned.1.call-start = ((), (), s32[]{:S(2)}) async-start(), calls=%async_computation.6 | async-start | bytes 7077888 | tf_op jit(solution)/shard_map/reduce_scatter | solution.py:530
  463.8 20.0 %collective-permute-start.41 = (bf16[384,1024]{1,0:T(8,128)(2,1)S(1)}, bf16[384,1024]{1,0:T(8,128)(2,1)S(1)}, u32[]{:S(2)}, u32[]{:S(2)}) collective-permute-start(bf16[384,1024]{1,0:T(8,128)(2,1)S(1)} %get-tuple-element.387.refs_0_), channel_id=1, source_target_pairs={{0,16},{8,24},{16,0},{24,8},{1,17},{9,25},{17,1},{25,9},{2,18},{10... | collective-permute-start | bytes 2359304 | tf_op jit(solution)/shard_map/ppermute | solution.py:70
  524.0 180.6 %reduce-scatter.8.cloned.1.call-start = ((), (), s32[]{:S(2)}) async-start(), calls=%async_computation.7 | async-start | bytes 2785280 | tf_op jit(solution)/shard_map/reduce_scatter | solution.py:597
  587.4 67.3 %collective-permute-start.50 = (bf16[512,2176]{1,0:T(8,128)(2,1)S(1)}, bf16[512,2176]{1,0:T(8,128)(2,1)S(1)}, u32[]{:S(2)}, u32[]{:S(2)}) collective-permute-start(bf16[512,2176]{1,0:T(8,128)(2,1)S(1)} %bitcast.110), channel_id=1, source_target_pairs={{0,1},{1,0},{2,3},{3,2},{4,5},{5,4},{6,7},{7,6},{8,9},{9,8},{10,11... | collective-permute-start | bytes 6684680 | tf_op jit(solution)/shard_map/ppermute | solution.py:535
  588.3 22.5 %collective-permute-start.58 = (bf16[128,3456]{1,0:T(8,128)(2,1)S(1)}, bf16[128,3456]{1,0:T(8,128)(2,1)S(1)}, u32[]{:S(2)}, u32[]{:S(2)}) collective-permute-start(bf16[128,3456]{1,0:T(8,128)(2,1)S(1)} %copy-done.9), channel_id=1, source_target_pairs={{0,16},{8,24},{16,0},{24,8},{1,17},{9,25},{17,1},{25,9},{2,18},{10... | collective-permute-start | bytes 2654216 | tf_op jit(solution)/shard_map/ppermute | solution.py:70
  591.2 36.5 %collective-permute-start.55 = (bf16[384,1024]{1,0:T(8,128)(2,1)S(1)}, bf16[384,1024]{1,0:T(8,128)(2,1)S(1)}, u32[]{:S(2)}, u32[]{:S(2)}) collective-permute-start(bf16[384,1024]{1,0:T(8,128)(2,1)S(1)} %add_convert_fusion), channel_id=1, source_target_pairs={{0,16},{8,24},{16,0},{24,8},{1,17},{9,25},{17,1},{25,9},{2,18},{10... | collective-permute-start | bytes 2359304 | tf_op jit(solution)/shard_map/ppermute | solution.py:70
  592.4 51.0 %collective-permute-start.52 = (bf16[384,1024]{1,0:T(8,128)(2,1)S(1)}, bf16[384,1024]{1,0:T(8,128)(2,1)S(1)}, u32[]{:S(2)}, u32[]{:S(2)}) collective-permute-start(bf16[384,1024]{1,0:T(8,128)(2,1)S(1)} %get-tuple-element.398), channel_id=1, source_target_pairs={{0,16},{8,24},{16,0},{24,8},{1,17},{9,25},{17,1},{25,9},{2,18},{10... | collective-permute-start | bytes 2359304 | tf_op jit(solution)/shard_map/ppermute | solution.py:70
  594.0 53.9 %collective-permute-start.57 = (bf16[128,3456]{1,0:T(8,128)(2,1)S(1)}, bf16[128,3456]{1,0:T(8,128)(2,1)S(1)}, u32[]{:S(2)}, u32[]{:S(2)}) collective-permute-start(bf16[128,3456]{1,0:T(8,128)(2,1)S(1)} %copy-done.9), channel_id=1, source_target_pairs={{0,8},{8,0},{16,24},{24,16},{1,9},{9,1},{17,25},{25,17},{2,10},{10... | collective-permute-start | bytes 2654216 | tf_op jit(solution)/shard_map/ppermute | solution.py:70
  610.8 38.0 %collective-permute-start.59 = (bf16[128,3456]{1,0:T(8,128)(2,1)S(1)}, bf16[128,3456]{1,0:T(8,128)(2,1)S(1)}, u32[]{:S(2)}, u32[]{:S(2)}) collective-permute-start(bf16[128,3456]{1,0:T(8,128)(2,1)S(1)} %collective-permute-done.58.refs_3_), channel_id=1, source_target_pairs={{0,8},{8,0},{16,24},{24,16},{1,9},{9,1},{17,25},{25,17},{2,10},{10... | collective-permute-start | bytes 2654216 | tf_op jit(solution)/shard_map/ppermute | solution.py:70
  669.5 29.8 %collective-permute-start.60 = (bf16[128,2816]{1,0:T(8,128)(2,1)S(1)}, bf16[128,2816]{1,0:T(8,128)(2,1)}, u32[]{:S(2)}, u32[]{:S(2)}) collective-permute-start(bf16[128,2816]{1,0:T(8,128)(2,1)S(1)} %slice.340.refs_1_), channel_id=1, source_target_pairs={{0,8},{8,0},{16,24},{24,16},{1,9},{9,1},{17,25},{25,17},{2,10},{10... | collective-permute-start | bytes 2162696 | tf_op jit(solution)/shard_map/ppermute | solution.py:70
  677.3 21.9 %collective-permute-start.62 = (bf16[128,2816]{1,0:T(8,128)(2,1)}, bf16[128,2816]{1,0:T(8,128)(2,1)}, u32[]{:S(2)}, u32[]{:S(2)}) collective-permute-start(bf16[128,2816]{1,0:T(8,128)(2,1)} %collective-permute-done.61.refs_3_), channel_id=1, source_target_pairs={{0,8},{8,0},{16,24},{24,16},{1,9},{9,1},{17,25},{25,17},{2,10},{10... | collective-permute-start | bytes 2162696 | tf_op jit(solution)/shard_map/ppermute | solution.py:70
  (153 other events, 1433.2 us)
Sparse Core Ops, SparseCore 0:
  36.1 148.1 all-gather.2
  187.0 106.9 all-gather.4
  389.1 127.1 reduce-scatter.3
  524.1 129.7 reduce-scatter.5
  657.0 47.5 reduce-scatter.7

commit v6 on v5

--- a/solution.py
+++ b/solution.py
@@ -1038,7 +1038,7 @@
     small = jnp.pad(small, ((0, 0), (0, 128 - small.shape[1])))
     out_piece = pack_piece(dealt_out, channels)
     o_piece = pack_piece(dealt_o, channels)
-    mix_block = jnp.concatenate([column_block(w_in, 3), small, out_piece], 1)
+    mix_block = jnp.concatenate([column_block(w_in, 3), small], 1)
     mix_block, w_gate1, w_up1, w_down1, w_q, key_projection_weight, value_projection_weight = tie(
         mix_block, w_gate1, w_up1, w_down1, w_q, key_projection_weight, value_projection_weight
     )
@@ -1054,6 +1054,7 @@
         1,
     )
     mix_all, ffn_one = dp_gather_small(mix_block, ffn_one)
+    out_all, ffn_one = dp_gather_small(out_piece, ffn_one)
     ffn_one = dp_gather(ffn_one)
     attn_all = ffn_one[:, 3 * hidden :]
     ffn_two = dp_gather(
@@ -1064,7 +1065,7 @@
     o_block = unpack_rows(attn_all[:, qkv_width:], dp_count)
     bounds = cu_seqlens[0]
     place = seq_place.reshape(1).astype(jnp.int32)
-    out_block = unpack_rows(mix_all[:, 3 * channels + 128 :], dp_count)
+    out_block = unpack_rows(out_all, dp_count)
     small_all = mix_all[:, 3 * channels : 3 * channels + 128].astype(F32).T
     kernel = lax.dynamic_slice_in_dim(small_all[:taps], seq_place * channels, channels, 1)
     gain_mix, gain_ffn_one, gain_attn, gain_ffn_two = (small_all[taps + i] for i in range(4))

time: 743 us -> 730 us (0.983)
  local copies, waits for them, and re-layouts: 76.8 us -> 65 us
  starting transfers between devices: 80.3 us -> 71.1 us
    ppermute x11 -> x18, waiting for transfers between devices: 39.3 us -> 45.5 us  [swap_dp(): return lax.ppermute(array, 'dp', [(i, i ^ bit) for i in range(size)])]
    ppermute x11 -> x18, starting transfers between devices: 35.8 us -> 30.2 us  [swap_dp(): return lax.ppermute(array, 'dp', [(i, i ^ bit) for i in range(size)])]
    unnamed x198 -> x194, local copies, waits for them, and re-layouts: 32.2 us -> 28.3 us
  transfers between devices with their start and end apart: 85 -> 92, of which waited for: 45 -> 54; matrix products, arithmetic and copies ran while one was open for 22% -> 21% of each run, Pallas kernels for 20% -> 21%
where the time goes in v6:
time: 730 us; the launch traced here: 721 us
  waiting for transfers between devices  292 us (40%)
  Pallas kernels  166 us (23%)
  starting transfers between devices  71.1 us (10%)
  local copies, waits for them, and re-layouts  65 us (9%)
  matrix products  59.6 us (8%)
  other arithmetic  51.8 us (7%)
  between operations  15.7 us (2%)
    ppermute x66, waiting for transfers between devices, swap_seq(): return lax.ppermute(array, 'seq', [(i, i ^ bit) for i in range(size)])  237 us
    pallas_call x5, Pallas kernels, ffn_call(): pl.pallas_call(lambda *refs: kernel(*refs, count=count), grid=(count,), i...  69.1 us
    dot_general x8, matrix products, left_dot(): lax.dot_general(left, right, (((0,), (0,)), ((), ())), preferred_element_...  52.5 us
    ppermute x18, waiting for transfers between devices, swap_dp(): return lax.ppermute(array, 'dp', [(i, i ^ bit) for i in range(size)])  45.5 us
    ppermute x66, starting transfers between devices, swap_seq(): return lax.ppermute(array, 'seq', [(i, i ^ bit) for i in range(size)])  37.4 us
    pallas_call x1, Pallas kernels, attention_backward(): pl.pallas_call(lambda *refs: attention_backward_kernel(*refs, length=leng...  37.2 us
    ppermute x18, starting transfers between devices, swap_dp(): return lax.ppermute(array, 'dp', [(i, i ^ bit) for i in range(size)])  30.2 us
    unnamed x194, local copies, waits for them, and re-layouts  28.3 us
  transfers between devices with their start and end apart: 92, of which 54 were waited for; matrix products, arithmetic and copies ran while one was open for 21% of the time, Pallas kernels for 21%

profile of v6, /device:TPU:0, one launch (start us, length us, event | category | flops | bytes accessed | tf_op | source)
XLA Modules:
  0.0 721.3 jit_solution(5065320427973605381)
XLA Ops:
  89.5 11.0 %collective-permute-done.21.refs_2_ = bf16[384,1024]{1,0:T(8,128)(2,1)} collective-permute-done((bf16[384,1024]{1,0:T(8,128)(2,1)S(1)}, bf16[384,1024]{1,0:T(8,128)(2,1)}, u32[]{:S(2)}, u32[]{:S(2)}) %collective-permute-start.21) | collective-permute-done | bytes 786464 | tf_op jit(solution)/shard_map/ppermute | solution.py:70
  100.6 10.0 %conv_forward.1 = (bf16[1536,1024]{1,0:T(8,128)(2,1)}, f32[1536,768]{1,0:T(8,128)}, bf16[1536,256]{1,0:T(8,128)(2,1)S(1)}, bf16[768,1024]{1,0:T(8,128)(2,1)S(1)}, bf16[768,1024]{1,0:T(8,128)(2,1)}) custom-call(s32[1]{0:T(128)} %bitcast.2.refs_0_, s32[4]{0:T(128)S(1)} %bitcast.105, bf16[384,1024]{1,0:T(8,128)(2,1)S(1)} %bitcast.94, ...), custom_call_target="tpu_custom_call" | custom-call | flops 4000000000 | bytes 20000000 | tf_op jit(solution)/shard_map/conv_forward/pallas_call | solution.py:972
  126.4 12.6 %collective-permute-done.19 = bf16[384,1024]{1,0:T(8,128)(2,1)S(1)} collective-permute-done((bf16[384,1024]{1,0:T(8,128)(2,1)S(1)}, bf16[384,1024]{1,0:T(8,128)(2,1)S(1)}, u32[]{:S(2)}, u32[]{:S(2)}) %collective-permute-start.19) | collective-permute-done | bytes 786464 | tf_op jit(solution)/shard_map/ppermute | solution.py:70
  141.1 18.1 %collective-permute-done.25.refs_2_ = bf16[384,1024]{1,0:T(8,128)(2,1)S(1)} collective-permute-done((bf16[384,1024]{1,0:T(8,128)(2,1)S(1)}, bf16[384,1024]{1,0:T(8,128)(2,1)S(1)}, u32[]{:S(2)}, u32[]{:S(2)}) %collective-permute-start.25) | collective-permute-done | bytes 786464 | tf_op jit(solution)/shard_map/ppermute | solution.py:70
  171.0 18.3 %ffn_forward.1 = (bf16[1536,3456]{1,0:T(8,128)(2,1)}, bf16[1536,1024]{1,0:T(8,128)(2,1)}) custom-call(bf16[384,1024]{1,0:T(8,128)(2,1)S(1)} %multiply_convert_fusion.2.refs_0_, bf16[384,1024]{1,0:T(8,128)(2,1)S(1)} %collective-permute-done.24.refs_1_, bf16[384,1024]{1,0:T(8,128)(2,1)S(1)} %collective-permute-done.25.refs_2_, ...), custom_call_target="tpu_custom_call" | custom-call | flops 6000000000 | bytes 20000000 | tf_op jit(solution)/shard_map/ffn_forward/pallas_call | solution.py:750
  200.4 15.7 %collective-permute-done.28 = bf16[384,1024]{1,0:T(8,128)(2,1)S(1)} collective-permute-done((bf16[384,1024]{1,0:T(8,128)(2,1)S(1)}, bf16[384,1024]{1,0:T(8,128)(2,1)S(1)}, u32[]{:S(2)}, u32[]{:S(2)}) %collective-permute-start.28) | collective-permute-done | bytes 786464 | tf_op jit(solution)/shard_map/ppermute | solution.py:70
  220.2 17.6 %collective-permute-done.31.refs_3_ = bf16[384,1024]{1,0:T(8,128)(2,1)} collective-permute-done((bf16[384,1024]{1,0:T(8,128)(2,1)}, bf16[384,1024]{1,0:T(8,128)(2,1)}, u32[]{:S(2)}, u32[]{:S(2)}) %collective-permute-start.31) | collective-permute-done | bytes 786464 | tf_op jit(solution)/shard_map/ppermute | solution.py:70
  241.5 27.0 %attention_forward.1 = (f32[1536,512]{1,0:T(8,128)}, bf16[1536,256]{1,0:T(8,128)(2,1)S(1)}, f32[256,1536]{1,0:T(8,128)}, f32[8,1536]{1,0:T(8,128)S(1)}, bf16[768...) custom-call(s32[1]{0:T(128)} %bitcast.2.refs_0_, bf16[384,1024]{1,0:T(8,128)(2,1)} %multiply_convert_fusion.1.refs_1_, ...), custom_call_target="tpu_custom_call" | custom-call | flops 20000000000 | bytes 20000000 | tf_op jit(solution)/shard_map/attention_forward/pallas_call | solution.py:405
  274.5 17.8 %collective-permute-done.34 = bf16[384,1024]{1,0:T(8,128)(2,1)S(1)} collective-permute-done((bf16[384,1024]{1,0:T(8,128)(2,1)S(1)}, bf16[384,1024]{1,0:T(8,128)(2,1)S(1)}, u32[]{:S(2)}, u32[]{:S(2)}) %collective-permute-start.34) | collective-permute-done | bytes 786464 | tf_op jit(solution)/shard_map/ppermute | solution.py:70
  296.1 14.8 %ffn_turn.2 = (bf16[1536,3456]{1,0:T(8,128)(2,1)}, bf16[768,1024]{1,0:T(8,128)(2,1)S(1)}) custom-call(bf16[384,1024]{1,0:T(8,128)(2,1)S(1)} %multiply_convert_fusion.refs_0_, bf16[384,1024]{1,0:T(8,128)(2,1)S(1)} %collective-permute-done.37.refs_1_, bf16[384,1024]{1,0:T(8,128)(2,1)S(1)} %bitcast.97, bf16[384,1024]{1,0:T(8,128)(2,1)} %collective-permute-done.20.refs_3_, ...), custom_call_target="tpu_custom_call" | custom-call | flops 6000000000 | bytes 20000000 | tf_op jit(solution)/shard_map/ffn_turn/pallas_call | solution.py:750
  316.4 14.8 %ffn_turn.3 = (bf16[1536,3456]{1,0:T(8,128)(2,1)}, bf16[768,1024]{1,0:T(8,128)(2,1)S(1)}) custom-call(bf16[384,1024]{1,0:T(8,128)(2,1)} %collective-permute-done.36.refs_0_, bf16[384,1024]{1,0:T(8,128)(2,1)S(1)} %collective-permute-done.38.refs_1_, bf16[384,1024]{1,0:T(8,128)(2,1)} %collective-permute-done.21.refs_2_, ...), custom_call_target="tpu_custom_call", output_to_operand_aliasing={{0}: (7, {})} | custom-call | flops 6000000000 | bytes 20000000 | tf_op jit(solution)/shard_map/ffn_turn/pallas_call | solution.py:750
  335.5 12.6 %fusion.2 = bf16[1024,2304]{1,0:T(8,128)(2,1)} fusion(bf16[1536,3456]{1,0:T(8,128)(2,1)} %get-tuple-element.209, bf16[384,1024]{1,0:T(8,128)(2,1)S(1)} %collective-permute-done.38.refs_1_, bf16[384,1024]{1,0:T(8,128)(2,1)} %collective-permute-done.36.refs_0_, bf16[384,1024]{1,0:T(8,128)(2,1)S(1)} %collective-permute-done.37.refs_1_, ...), kind=kOutput, calls=%fused_computation.5 | convolution fusion | flops 7262699520 | bytes 14942208 | tf_op jit(solution)/shard_map/dot_general | solution.py:19
  379.7 37.2 %attention_backward.1 = (bf16[1536,512]{1,0:T(8,128)(2,1)}, bf16[768,1024]{1,0:T(8,128)(2,1)}, bf16[768,1024]{1,0:T(8,128)(2,1)}, f32[2,128]{1,0:T(2,128)S(1)}) custom-call(s32[1]{0:T(128)} %bitcast.2.refs_0_, bf16[384,1024]{1,0:T(8,128)(2,1)S(1)} %get-tuple-element.393.refs_1_, bf16[384,1024]{1,0:T(8,128)(2,1)S(1)} %collective-permute-done.42.refs_2_, ...), custom_call_target="tpu_custom_call" | custom-call | flops 20000000000 | bytes 20000000 | tf_op jit(solution)/shard_map/attention_backward/pallas_call | solution.py:437
  432.5 14.0 %collective-permute-done.46 = bf16[384,1024]{1,0:T(8,128)(2,1)S(1)} collective-permute-done((bf16[384,1024]{1,0:T(8,128)(2,1)S(1)}, bf16[384,1024]{1,0:T(8,128)(2,1)S(1)}, u32[]{:S(2)}, u32[]{:S(2)}) %collective-permute-start.46) | collective-permute-done | bytes 786464 | tf_op jit(solution)/shard_map/ppermute | solution.py:70
  451.8 10.7 %ffn_backward.2 = (bf16[1536,2304]{1,0:T(8,128)(2,1)}, bf16[768,1024]{1,0:T(8,128)(2,1)S(1)}) custom-call(bf16[384,1024]{1,0:T(8,128)(2,1)S(1)} %get-tuple-element.391.refs_0_, bf16[384,1024]{1,0:T(8,128)(2,1)S(1)} %collective-permute-done.49.refs_1_, bf16[1536,3456]{1,0:T(8,128)(2,1)} %get-tuple-element.191.refs_2_, ...), custom_call_target="tpu_custom_call" | custom-call | flops 6000000000 | bytes 20000000 | tf_op jit(solution)/shard_map/ffn_backward/pallas_call | solution.py:750
  471.8 10.5 %ffn_backward.3 = (bf16[1536,2304]{1,0:T(8,128)(2,1)}, bf16[768,1024]{1,0:T(8,128)(2,1)S(1)}) custom-call(bf16[384,1024]{1,0:T(8,128)(2,1)S(1)} %collective-permute-done.48.refs_0_, bf16[384,1024]{1,0:T(8,128)(2,1)S(1)} %collective-permute-done.50.refs_1_, bf16[1536,3456]{1,0:T(8,128)(2,1)} %get-tuple-element.191.refs_2_, ...), custom_call_target="tpu_custom_call", output_to_operand_aliasing={{0}: (6, {})} | custom-call | flops 6000000000 | bytes 20000000 | tf_op jit(solution)/shard_map/ffn_backward/pallas_call | solution.py:750
  486.8 10.7 %convolution_convert_fusion = bf16[1024,2304]{1,0:T(8,128)(2,1)S(1)} fusion(bf16[1536,2304]{1,0:T(8,128)(2,1)} %get-tuple-element.197, bf16[384,1024]{1,0:T(8,128)(2,1)S(1)} %copy-done.24, bf16[384,1024]{1,0:T(8,128)(2,1)S(1)} %copy-done.19, bf16[384,1024]{1,0:T(8,128)(2,1)S(1)} %copy-done.21, bf16[384,1024]{1,0:T(8,128)(2,1)S(1)} %multiply_convert_fusion.2.refs_0_), kind=kOutput, calls=%fused_computation.4 | convolution fusion | flops 7262699520 | bytes 14942208 | tf_op jit(solution)/shard_map/dot_general | solution.py:19
  518.1 7.7 %convolution_convert_fusion.1 = bf16[1024,1152]{1,0:T(8,128)(2,1)} fusion(bf16[1536,3456]{1,0:T(8,128)(2,1)} %get-tuple-element.191.refs_2_, bf16[384,1024]{1,0:T(8,128)(2,1)S(1)} %copy-done.30, bf16[384,1024]{1,0:T(8,128)(2,1)S(1)} %copy-done.28, bf16[384,1024]{1,0:T(8,128)(2,1)S(1)} %copy-done.26, bf16[384,1024]{1,0:T(8,128)(2,1)S(1)} %get-tuple-element.391.refs_0_), kind=kOutput, calls=%fused_computation.9 | convolution fusion | flops 3637641216 | bytes 9043968 | tf_op jit(solution)/shard_map/dot_general | solution.py:19
  525.8 9.3 %collective-permute-done.54.refs_4_ = bf16[384,1024]{1,0:T(8,128)(2,1)S(1)} collective-permute-done((bf16[384,1024]{1,0:T(8,128)(2,1)S(1)}, bf16[384,1024]{1,0:T(8,128)(2,1)S(1)}, u32[]{:S(2)}, u32[]{:S(2)}) %collective-permute-start.54) | collective-permute-done | bytes 786464 | tf_op jit(solution)/shard_map/ppermute | solution.py:70
  538.7 10.1 %conv_backward.1 = (bf16[1536,768]{1,0:T(8,128)(2,1)}, bf16[768,1024]{1,0:T(8,128)(2,1)S(1)}, bf16[768,1024]{1,0:T(8,128)(2,1)}, f32[3,256]{1,0:T(4,128)S(1)}) custom-call(s32[1]{0:T(128)} %bitcast.2.refs_0_, s32[4]{0:T(128)S(1)} %bitcast.107, bf16[384,1024]{1,0:T(8,128)(2,1)S(1)} %get-tuple-element.389.refs_2_, ...), custom_call_target="tpu_custom_call" | custom-call | bytes 100000 | tf_op jit(solution)/shard_map/conv_backward/pallas_call | solution.py:906
  577.9 16.5 %collective-permute-done.65.refs_3_ = bf16[128,3456]{1,0:T(8,128)(2,1)S(1)} collective-permute-done((bf16[128,3456]{1,0:T(8,128)(2,1)S(1)}, bf16[128,3456]{1,0:T(8,128)(2,1)S(1)}, u32[]{:S(2)}, u32[]{:S(2)}) %collective-permute-start.65) | collective-permute-done | bytes 884768 | tf_op jit(solution)/shard_map/ppermute | solution.py:70
  594.4 16.8 %collective-permute-done.62 = bf16[384,1024]{1,0:T(8,128)(2,1)S(1)} collective-permute-done((bf16[384,1024]{1,0:T(8,128)(2,1)S(1)}, bf16[384,1024]{1,0:T(8,128)(2,1)S(1)}, u32[]{:S(2)}, u32[]{:S(2)}) %collective-permute-start.62) | collective-permute-done | bytes 786464 | tf_op jit(solution)/shard_map/ppermute | solution.py:70
  611.2 15.7 %collective-permute-done.59 = bf16[384,1024]{1,0:T(8,128)(2,1)S(1)} collective-permute-done((bf16[384,1024]{1,0:T(8,128)(2,1)S(1)}, bf16[384,1024]{1,0:T(8,128)(2,1)S(1)}, u32[]{:S(2)}, u32[]{:S(2)}) %collective-permute-start.59) | collective-permute-done | bytes 786464 | tf_op jit(solution)/shard_map/ppermute | solution.py:70
  695.9 9.0 %collective-permute-done.81.refs_3_ = bf16[128,1920]{1,0:T(8,128)(2,1)S(1)} collective-permute-done((bf16[128,1920]{1,0:T(8,128)(2,1)S(1)}, bf16[128,1920]{1,0:T(8,128)(2,1)S(1)}, u32[]{:S(2)}, u32[]{:S(2)}) %collective-permute-start.81) | collective-permute-done | bytes 491552 | tf_op jit(solution)/shard_map/ppermute | solution.py:70
  (525 shorter events, 346.8 us)
Async XLA Ops:
  7.3 162.6 %all-gather.3.cloned.1.call-start = ((), (), s32[]{:S(2)}) async-start(), calls=%async_computation.3 | async-start | bytes 9732096 | tf_op jit(solution)/shard_map/all_gather | solution.py:526
  12.3 22.2 %collective-permute-start.7 = (bf16[128,896]{0,1:T(8,128)(2,1)S(1)}, bf16[128,896]{0,1:T(8,128)(2,1)S(1)}, u32[]{:S(2)}, u32[]{:S(2)}) collective-permute-start(bf16[128,896]{0,1:T(8,128)(2,1)S(1)} %fusion.86), channel_id=1, source_target_pairs={{0,4},{1,5},{2,6},{3,7},{4,0},{5,1},{6,2},{7,3},{8,12},{9,13},{10,... | collective-permute-start | bytes 688136 | tf_op jit(solution)/shard_map/ppermute | solution.py:535
  35.9 259.4 %all-gather.5.cloned.1.call-start = ((), (), s32[]{:S(2)}) async-start(), calls=%async_computation.4 | async-start | bytes 7962624 | tf_op jit(solution)/shard_map/all_gather | solution.py:526
  44.3 36.2 %collective-permute-start.2 = (bf16[384,1024]{1,0:T(8,128)(2,1)S(1)}, bf16[384,1024]{1,0:T(8,128)(2,1)S(1)}, u32[]{:S(2)}, u32[]{:S(2)}) collective-permute-start(bf16[384,1024]{1,0:T(8,128)(2,1)S(1)} %bitcast.92), channel_id=1, source_target_pairs={{0,16},{8,24},{16,0},{24,8},{1,17},{9,25},{17,1},{25,9},{2,18},{10... | collective-permute-start | bytes 2359304 | tf_op jit(solution)/shard_map/ppermute | solution.py:70
  45.1 55.5 %collective-permute-start.1 = (bf16[384,1024]{1,0:T(8,128)(2,1)S(1)}, bf16[384,1024]{1,0:T(8,128)(2,1)}, u32[]{:S(2)}, u32[]{:S(2)}) collective-permute-start(bf16[384,1024]{1,0:T(8,128)(2,1)S(1)} %bitcast.93), channel_id=1, source_target_pairs={{0,8},{8,0},{16,24},{24,16},{1,9},{9,1},{17,25},{25,17},{2,10},{10... | collective-permute-start | bytes 2359304 | tf_op jit(solution)/shard_map/ppermute | solution.py:70
  51.8 22.8 %collective-permute-start.9 = (bf16[128,896]{0,1:T(8,128)(2,1)S(1)}, bf16[128,896]{0,1:T(8,128)(2,1)S(1)}, u32[]{:S(2)}, u32[]{:S(2)}) collective-permute-start(bf16[128,896]{0,1:T(8,128)(2,1)S(1)} %copy-done.73), channel_id=1, source_target_pairs={{0,2},{1,3},{2,0},{3,1},{4,6},{5,7},{6,4},{7,5},{8,10},{9,11},{10,... | collective-permute-start | bytes 688136 | tf_op jit(solution)/shard_map/ppermute | solution.py:535
  54.1 24.3 %collective-permute-start.6 = (bf16[128,896]{0,1:T(8,128)(2,1)}, bf16[128,896]{0,1:T(8,128)(2,1)S(1)}, u32[]{:S(2)}, u32[]{:S(2)}) collective-permute-start(bf16[128,896]{0,1:T(8,128)(2,1)} %collective-permute-done.5), channel_id=1, source_target_pairs={{0,1},{1,0},{2,3},{3,2},{4,5},{5,4},{6,7},{7,6},{8,9},{9,8},{10,11... | collective-permute-start | bytes 688136 | tf_op jit(solution)/shard_map/ppermute | solution.py:535
  80.5 20.1 %collective-permute-start.3 = (bf16[384,1024]{1,0:T(8,128)(2,1)S(1)}, bf16[384,1024]{1,0:T(8,128)(2,1)}, u32[]{:S(2)}, u32[]{:S(2)}) collective-permute-start(bf16[384,1024]{1,0:T(8,128)(2,1)S(1)} %collective-permute-done.2.refs_4_), channel_id=1, source_target_pairs={{0,8},{8,0},{16,24},{24,16},{1,9},{9,1},{17,25},{25,17},{2,10},{10... | collective-permute-start | bytes 2359304 | tf_op jit(solution)/shard_map/ppermute | solution.py:70
  80.5 20.1 %collective-permute-start.21 = (bf16[384,1024]{1,0:T(8,128)(2,1)S(1)}, bf16[384,1024]{1,0:T(8,128)(2,1)}, u32[]{:S(2)}, u32[]{:S(2)}) collective-permute-start(bf16[384,1024]{1,0:T(8,128)(2,1)S(1)} %bitcast.95), channel_id=1, source_target_pairs={{0,16},{8,24},{16,0},{24,8},{1,17},{9,25},{17,1},{25,9},{2,18},{10... | collective-permute-start | bytes 2359304 | tf_op jit(solution)/shard_map/ppermute | solution.py:70
  89.5 27.1 %collective-permute-start.20 = (bf16[384,1024]{1,0:T(8,128)(2,1)S(1)}, bf16[384,1024]{1,0:T(8,128)(2,1)}, u32[]{:S(2)}, u32[]{:S(2)}) collective-permute-start(bf16[384,1024]{1,0:T(8,128)(2,1)S(1)} %bitcast.96), channel_id=1, source_target_pairs={{0,8},{8,0},{16,24},{24,16},{1,9},{9,1},{17,25},{25,17},{2,10},{10... | collective-permute-start | bytes 2359304 | tf_op jit(solution)/shard_map/ppermute | solution.py:70
  116.3 422.2 %reduce-scatter.4.cloned.1.call-start = ((), (), s32[]{:S(2)}) async-start(), calls=%async_computation.5 | async-start | bytes 7962624 | tf_op jit(solution)/shard_map/reduce_scatter | solution.py:530
  293.8 20.1 %collective-permute-start.36 = (bf16[384,1024]{1,0:T(8,128)(2,1)S(1)}, bf16[384,1024]{1,0:T(8,128)(2,1)}, u32[]{:S(2)}, u32[]{:S(2)}) collective-permute-start(bf16[384,1024]{1,0:T(8,128)(2,1)S(1)} %multiply_convert_fusion.refs_0_), channel_id=1, source_target_pairs={{0,16},{8,24},{16,0},{24,8},{1,17},{9,25},{17,1},{25,9},{2,18},{10... | collective-permute-start | bytes 2359304 | tf_op jit(solution)/shard_map/ppermute | solution.py:70
  374.7 266.1 %reduce-scatter.6.cloned.1.call-start = ((), (), s32[]{:S(2)}) async-start(), calls=%async_computation.6 | async-start | bytes 7077888 | tf_op jit(solution)/shard_map/reduce_scatter | solution.py:530
  426.7 19.7 %collective-permute-start.46 = (bf16[384,1024]{1,0:T(8,128)(2,1)S(1)}, bf16[384,1024]{1,0:T(8,128)(2,1)S(1)}, u32[]{:S(2)}, u32[]{:S(2)}) collective-permute-start(bf16[384,1024]{1,0:T(8,128)(2,1)S(1)} %add_convert_fusion.3), channel_id=1, source_target_pairs={{0,16},{8,24},{16,0},{24,8},{1,17},{9,25},{17,1},{25,9},{2,18},{10... | collective-permute-start | bytes 2359304 | tf_op jit(solution)/shard_map/ppermute | solution.py:70
  449.6 20.0 %collective-permute-start.48 = (bf16[384,1024]{1,0:T(8,128)(2,1)S(1)}, bf16[384,1024]{1,0:T(8,128)(2,1)S(1)}, u32[]{:S(2)}, u32[]{:S(2)}) collective-permute-start(bf16[384,1024]{1,0:T(8,128)(2,1)S(1)} %get-tuple-element.391.refs_0_), channel_id=1, source_target_pairs={{0,16},{8,24},{16,0},{24,8},{1,17},{9,25},{17,1},{25,9},{2,18},{10... | collective-permute-start | bytes 2359304 | tf_op jit(solution)/shard_map/ppermute | solution.py:70
  509.7 181.3 %reduce-scatter.8.cloned.1.call-start = ((), (), s32[]{:S(2)}) async-start(), calls=%async_computation.7 | async-start | bytes 2785280 | tf_op jit(solution)/shard_map/reduce_scatter | solution.py:597
  570.9 67.7 %collective-permute-start.57 = (bf16[512,2176]{1,0:T(8,128)(2,1)S(1)}, bf16[512,2176]{1,0:T(8,128)(2,1)S(1)}, u32[]{:S(2)}, u32[]{:S(2)}) collective-permute-start(bf16[512,2176]{1,0:T(8,128)(2,1)S(1)} %bitcast.110), channel_id=1, source_target_pairs={{0,1},{1,0},{2,3},{3,2},{4,5},{5,4},{6,7},{7,6},{8,9},{9,8},{10,11... | collective-permute-start | bytes 6684680 | tf_op jit(solution)/shard_map/ppermute | solution.py:535
  571.8 22.5 %collective-permute-start.65 = (bf16[128,3456]{1,0:T(8,128)(2,1)S(1)}, bf16[128,3456]{1,0:T(8,128)(2,1)S(1)}, u32[]{:S(2)}, u32[]{:S(2)}) collective-permute-start(bf16[128,3456]{1,0:T(8,128)(2,1)S(1)} %copy-done.11), channel_id=1, source_target_pairs={{0,16},{8,24},{16,0},{24,8},{1,17},{9,25},{17,1},{25,9},{2,18},{10... | collective-permute-start | bytes 2654216 | tf_op jit(solution)/shard_map/ppermute | solution.py:70
  574.7 36.5 %collective-permute-start.62 = (bf16[384,1024]{1,0:T(8,128)(2,1)S(1)}, bf16[384,1024]{1,0:T(8,128)(2,1)S(1)}, u32[]{:S(2)}, u32[]{:S(2)}) collective-permute-start(bf16[384,1024]{1,0:T(8,128)(2,1)S(1)} %add_convert_fusion), channel_id=1, source_target_pairs={{0,16},{8,24},{16,0},{24,8},{1,17},{9,25},{17,1},{25,9},{2,18},{10... | collective-permute-start | bytes 2359304 | tf_op jit(solution)/shard_map/ppermute | solution.py:70
  576.0 50.9 %collective-permute-start.59 = (bf16[384,1024]{1,0:T(8,128)(2,1)S(1)}, bf16[384,1024]{1,0:T(8,128)(2,1)S(1)}, u32[]{:S(2)}, u32[]{:S(2)}) collective-permute-start(bf16[384,1024]{1,0:T(8,128)(2,1)S(1)} %get-tuple-element.402), channel_id=1, source_target_pairs={{0,16},{8,24},{16,0},{24,8},{1,17},{9,25},{17,1},{25,9},{2,18},{10... | collective-permute-start | bytes 2359304 | tf_op jit(solution)/shard_map/ppermute | solution.py:70
  577.5 54.0 %collective-permute-start.64 = (bf16[128,3456]{1,0:T(8,128)(2,1)S(1)}, bf16[128,3456]{1,0:T(8,128)(2,1)S(1)}, u32[]{:S(2)}, u32[]{:S(2)}) collective-permute-start(bf16[128,3456]{1,0:T(8,128)(2,1)S(1)} %copy-done.11), channel_id=1, source_target_pairs={{0,8},{8,0},{16,24},{24,16},{1,9},{9,1},{17,25},{25,17},{2,10},{10... | collective-permute-start | bytes 2654216 | tf_op jit(solution)/shard_map/ppermute | solution.py:70
  594.4 37.1 %collective-permute-start.66 = (bf16[128,3456]{1,0:T(8,128)(2,1)S(1)}, bf16[128,3456]{1,0:T(8,128)(2,1)S(1)}, u32[]{:S(2)}, u32[]{:S(2)}) collective-permute-start(bf16[128,3456]{1,0:T(8,128)(2,1)S(1)} %collective-permute-done.65.refs_3_), channel_id=1, source_target_pairs={{0,8},{8,0},{16,24},{24,16},{1,9},{9,1},{17,25},{25,17},{2,10},{10... | collective-permute-start | bytes 2654216 | tf_op jit(solution)/shard_map/ppermute | solution.py:70
  655.8 27.5 %collective-permute-start.67 = (bf16[128,2816]{1,0:T(8,128)(2,1)S(1)}, bf16[128,2816]{1,0:T(8,128)(2,1)}, u32[]{:S(2)}, u32[]{:S(2)}) collective-permute-start(bf16[128,2816]{1,0:T(8,128)(2,1)S(1)} %slice.336.refs_1_), channel_id=1, source_target_pairs={{0,8},{8,0},{16,24},{24,16},{1,9},{9,1},{17,25},{25,17},{2,10},{10... | collective-permute-start | bytes 2162696 | tf_op jit(solution)/shard_map/ppermute | solution.py:70
  661.7 21.6 %collective-permute-start.69 = (bf16[128,2816]{1,0:T(8,128)(2,1)}, bf16[128,2816]{1,0:T(8,128)(2,1)}, u32[]{:S(2)}, u32[]{:S(2)}) collective-permute-start(bf16[128,2816]{1,0:T(8,128)(2,1)} %collective-permute-done.68.refs_3_), channel_id=1, source_target_pairs={{0,8},{8,0},{16,24},{24,16},{1,9},{9,1},{17,25},{25,17},{2,10},{10... | collective-permute-start | bytes 2162696 | tf_op jit(solution)/shard_map/ppermute | solution.py:70
  (159 other events, 1519.0 us)
Sparse Core Ops, SparseCore 0:
  36.1 133.7 all-gather.2
  172.7 106.9 all-gather.4
  374.8 127.1 reduce-scatter.3
  509.8 130.9 reduce-scatter.5
  643.6 47.3 reduce-scatter.7
